TPU v7x, 512 devices: a whole 4x4x16 slice. The times are simulated.
512 devices in a mesh: node: 64 (over y, z), local: 8 (over x, core).
Axes of the slice: x: 4, y: 4, z: 16, core: 2. Of those that a mesh axis runs over, the one named last changes fastest.
Arguments:
- grad_out: bfloat16 [65536, 3584], P(('node', 'local')), may hold values from -6 to 6
- expert_ids: int32 [65536, 8], P(('node', 'local')), may hold values from 0 to 255, as said below
- gate_weights: float32 [65536, 8], P(('node', 'local')), may hold values from 0.05 to 0.35
- saved_hidden: bfloat16 [64, 1024, 1024], P('node', None, 'local'), may hold values from -0.59765625 to 0.59765625
- down_weight: bfloat16 [64, 1024, 3584], P('node', 'local'), may hold values from -0.1875 to 0.1875
- second_moment: bfloat16 [64, 1024, 3584], P('node', 'local'), may hold values from 0.0019989014 to 0.25
Outputs:
- gate_weight_gradient: float32 [65536, 8], P(('node', 'local'))
- hidden_grad: bfloat16 [64, 1024, 1024], P('node', None, 'local')
- new_weight: bfloat16 [64, 1024, 3584], P('node', 'local')
- new_second: bfloat16 [64, 1024, 3584], P('node', 'local')
Inputs may be any that keep to these rules, and one draw needn't show every extreme that they name: `expert_ids`: each row names 8 different experts on at most 4 nodes (node = id // 4), two on each; at most one per row is in flight (id % 4 == 0). Among the rows of one device at most 2 name the in-flight expert of any one node, and in every draw some node receives exactly 2 from every device.
All inputs are finite; a program needn't handle non-finite values.
Results may differ from a plain program's by a relative error of at most 0.0051.
Values may be sent and summed in bfloat16 or wider, within the bound.
No kernel may reach another device: no remote copies, remote signals or barrier semaphores. Data moves between devices by JAX's collectives and lax.ppermute only.
A program may use at most 128 MiB of HBM per device.

v0:
```python
import jax
import jax.numpy as jnp
from jax import lax
from jax.sharding import PartitionSpec as P

EXPERTS_PER_HOST = 4
CAP = 2


beta_second = 0.95
learn_rate = 0.002
decay_rate = 0.1
epsilon = 1e-08
correct_second = 0.994079470779666


def gather_rows(picked_experts, gate_values, grads, node_count):
    transit_rows = picked_experts % EXPERTS_PER_HOST == 0
    row_present = jnp.any(transit_rows, 1)
    destination_node = jnp.sum(jnp.where(transit_rows, picked_experts // EXPERTS_PER_HOST, 0), 1)
    onehot = (
        (destination_node[:, None] == jnp.arange(node_count, dtype=jnp.int32)[None, :])
        & row_present[:, None]
    ).astype(jnp.int32)
    within_rank = jnp.sum(onehot * (jnp.cumsum(onehot, 0) - 1), 1)
    slot_index = destination_node * CAP + within_rank
    expert_location = (
        jnp.arange(node_count * CAP, dtype=jnp.int32)[:, None] == slot_index[None, :]
    ) & row_present[None, :]
    matched_gate = jnp.sum(jnp.where(transit_rows, gate_values, 0.0), 1).astype(jnp.bfloat16)
    departing_rows = jnp.dot(
        expert_location.astype(jnp.bfloat16), grads, preferred_element_type=jnp.float32
    ).astype(jnp.bfloat16)
    departing_gates = jnp.sum(
        jnp.where(expert_location, matched_gate.astype(jnp.float32)[None, :], 0.0), 1
    ).astype(jnp.bfloat16)
    feature_count = grads.shape[1]
    return (
        departing_rows.reshape(node_count, CAP, feature_count),
        departing_gates.reshape(node_count, CAP),
        expert_location,
        transit_rows,
    )


def on_device(grad_out, expert_ids, gate_weights, saved_hidden, down_weight, second_moment):
    node_count = lax.axis_size("node")
    members = lax.axis_size("local")
    feature_count = grad_out.shape[1]
    departing_rows, departing_gates, expert_location, transit_rows = gather_rows(
        expert_ids, gate_weights, grad_out, node_count
    )
    copies, copy_gates = (
        lax.all_gather(departing_rows[None], "local", axis=0, tiled=True),
        lax.all_gather(departing_gates[None], "local", axis=0, tiled=True),
    )
    arrived, arrived_gates = (
        lax.all_to_all(copies, "node", split_axis=1, concat_axis=1, tiled=True),
        lax.all_to_all(copy_gates, "node", split_axis=1, concat_axis=1, tiled=True),
    )
    arrived_rows = arrived.reshape(-1, feature_count)
    slot_gates = arrived_gates.reshape(-1).astype(jnp.float32)
    weight_now = down_weight[0]
    hidden_now = saved_hidden[0]
    unscaled = lax.dot_general(
        arrived_rows, weight_now, (((1,), (1,)), ((), ())), preferred_element_type=jnp.float32
    )
    hidden_out = (slot_gates[:, None] * unscaled).astype(jnp.bfloat16)
    slot_score = jnp.sum(unscaled * hidden_now.astype(jnp.float32), 1)
    scaled = (slot_gates[:, None] * arrived_rows.astype(jnp.float32)).astype(jnp.bfloat16)
    grad = lax.dot_general(
        hidden_now, scaled, (((0,), (0,)), ((), ())), preferred_element_type=jnp.float32
    )
    second_new = (
        beta_second * second_moment[0].astype(jnp.float32) + (1.0 - beta_second) * grad * grad
    )
    weight_f = weight_now.astype(jnp.float32)
    update = grad / (jnp.sqrt(second_new / correct_second) + epsilon) + decay_rate * weight_f
    weight_new = weight_f - learn_rate * update
    score_terms = slot_score.reshape(members, node_count * CAP)
    summed = lax.psum(score_terms, "local")
    own_terms = lax.dynamic_slice_in_dim(summed, lax.axis_index("local"), 1, 0)
    returned = lax.all_to_all(
        own_terms.reshape(node_count, CAP), "node", split_axis=0, concat_axis=0, tiled=True
    )
    returned_flat = returned.reshape(node_count * CAP)
    token_gradient = jnp.sum(jnp.where(expert_location, returned_flat[:, None], 0.0), 0)
    gate_weight_gradient = jnp.where(transit_rows, token_gradient[:, None], 0.0)
    return (
        gate_weight_gradient,
        hidden_out[None],
        weight_new.astype(jnp.bfloat16)[None],
        second_new.astype(jnp.bfloat16)[None],
    )


def solution(mesh):
    return jax.shard_map(
        on_device,
        mesh=mesh,
        in_specs=(
            P(("node", "local"), None),
            P(("node", "local"), None),
            P(("node", "local"), None),
            P("node", None, "local"),
            P("node", "local", None),
            P("node", "local", None),
        ),
        out_specs=(
            P(("node", "local"), None),
            P("node", None, "local"),
            P("node", "local", None),
            P("node", "local", None),
        ),
        check_vma=False,
    )
```

profile of v0, /device:TPU:1, one launch (start us, length us, event | category | flops | bytes accessed | tf_op | source)
XLA Modules:
  0.0 565.6 jit_solution(3273625820910826075)
XLA Ops:
  7.2 0.0 copy-start
  7.2 0.0 all-gather.2.cloned.1.call-start
  7.2 0.8 fusion.22
  8.0 0.7 fusion.19
  8.7 0.1 fusion.14
  8.8 0.2 reduce_window_sum.11
  9.0 0.2 select_reduce_fusion.2
  9.2 0.4 convolution_convert_fusion
  9.6 0.3 broadcast_in_dim_reshape.2
  9.9 1.0 copy.65
  11.0 0.0 all-gather.2.cloned.1.call-update
  11.0 58.8 %all-gather.2.cloned.1.call-done = bf16[8,64,2,3584]{3,1,2,0:T(8,128)(2,1)} async-done(((bf16[1,64,2,3584]{3,1,2,0:T(8,128)(2,1)}), bf16[8,64,2,3584]{3,1,2,0:T(8,128)(2,1)}) %all-gather.2.cloned.1.call-update) | async-done | bytes 7340048 | tf_op jit(solution)/shard_map/all_gather | solution.py:54
  69.8 14.7 %copy.66 = bf16[8,64,2,3584]{3,2,0,1:T(2,128)(2,1)} copy(bf16[8,64,2,3584]{3,1,2,0:T(8,128)(2,1)} %all-gather.2.cloned.1.call-done) | data formatting | bytes 14680064 | tf_op jit(solution)/shard_map/all_gather | solution.py:54
  84.5 15.7 %all-to-all-start = ((bf16[8,64,2,3584]{3,2,0,1:T(2,128)(2,1)}), bf16[8,64,2,3584]{3,2,0,1:T(2,128)(2,1)}, u32[]{:S(2)}, u32[]{:S(2)}) async-start(bf16[8,64,2,3584]{3,2,0,1:T(2,128)(2,1)} %copy.66), calls=%async_computation | async-start | bytes 14680064 | tf_op jit(solution)/shard_map/all_to_all | solution.py:58
  100.2 0.1 copy.69
  100.4 318.7 %all-to-all-done = bf16[8,64,2,3584]{3,2,0,1:T(2,128)(2,1)} async-done(((bf16[8,64,2,3584]{3,2,0,1:T(2,128)(2,1)}), bf16[8,64,2,3584]{3,2,0,1:T(2,128)(2,1)}, u32[]{:S(2)}, u32[]{:S(2)}) %all-to-all-start) | async-done | bytes 7340064 | tf_op jit(solution)/shard_map/all_to_all | solution.py:58
  419.1 7.4 %copy.67 = bf16[8,64,2,3584]{3,2,1,0:T(2,128)(2,1)} copy(bf16[8,64,2,3584]{3,2,0,1:T(2,128)(2,1)} %all-to-all-done) | data formatting | bytes 14680064 | tf_op jit(solution)/shard_map/all_to_all | solution.py:58
  426.5 15.5 %reshape.62 = bf16[1024,3584]{1,0:T(8,128)(2,1)} reshape(bf16[8,64,2,3584]{3,2,1,0:T(2,128)(2,1)} %copy.67) | data formatting | bytes 14680064 | tf_op jit(solution)/shard_map/reshape | solution.py:61
  442.1 5.5 multiply_reduce_fusion
  447.6 17.6 %psum.7 = f32[8,128]{1,0:T(8,128)S(1)} all-reduce(f32[8,128]{1,0:T(8,128)S(1)} %bitcast.41), channel_id=1, replica_groups=mesh['node'=64,'local'=8] {'local'}, use_global_device_ids=true, to_apply=%region_5.6 | all-reduce | flops 1024 | bytes 8192 | tf_op jit(solution)/shard_map/psum | solution.py:81
  465.3 0.8 all_to_all.13
  466.0 6.6 %all-to-all-start.1 = ((f32[64,1,2]{2,1,0:T(1,128)}), f32[64,1,2]{2,1,0:T(1,128)}, u32[]{:S(2)}, u32[]{:S(2)}) async-start(f32[64,1,2]{2,1,0:T(1,128)} %bitcast.3), calls=%async_computation.1 | async-start | bytes 65536 | tf_op jit(solution)/shard_map/all_to_all | solution.py:83
  472.7 0.5 select_reduce_fusion.3
  473.2 0.6 copy.68
  473.8 0.7 convert_element_type.132
  474.5 0.6 copy.78
  475.1 10.6 %all-to-all-done.1 = f32[64,1,2]{2,1,0:T(1,128)} async-done(((f32[64,1,2]{2,1,0:T(1,128)}), f32[64,1,2]{2,1,0:T(1,128)}, u32[]{:S(2)}, u32[]{:S(2)}) %all-to-all-start.1) | async-done | bytes 544 | tf_op jit(solution)/shard_map/all_to_all | solution.py:83
  485.7 0.5 broadcast.47
  486.2 1.5 reduce.7
  487.7 0.1 broadcast_in_dim.59
  487.8 0.1 select_reduce_fusion
  488.0 0.2 convert_element_type.82
  488.1 0.1 copy.71
  488.2 9.5 %all_gather.7 = bf16[8,64,2]{1,2,0:T(2,128)(2,1)S(1)} all-gather(bf16[1,64,2]{1,2,0:T(2,128)(2,1)S(1)} %copy.71), channel_id=1, replica_groups=mesh['node'=64,'local'=8] {'local'}, dimensions={0}, use_global_device_ids=true | all-gather | bytes 2304 | tf_op jit(solution)/shard_map/all_gather | solution.py:55
  497.7 0.7 copy.72
  498.4 4.8 all-to-all-start.2
  503.2 0.6 broadcast_select_fusion
  503.8 12.4 %all-to-all-done.2 = bf16[8,64,2]{0,2,1:T(2,128)(2,1)S(1)} async-done(((bf16[8,64,2]{0,2,1:T(2,128)(2,1)}), bf16[8,64,2]{0,2,1:T(2,128)(2,1)S(1)}, u32[]{:S(2)}, u32[]{:S(2)}) %all-to-all-start.2) | async-done | bytes 2080 | tf_op jit(solution)/shard_map/all_to_all | solution.py:59
  516.2 0.1 copy.73
  516.3 0.2 copy.74
  516.5 7.8 %multiply_convert_fusion = bf16[8,64,2,3584]{3,1,2,0:T(8,128)(2,1)S(1)} fusion(bf16[8,64,2,3584]{3,2,0,1:T(2,128)(2,1)} %all-to-all-done, f32[8,64,2]{1,2,0:T(2,128)S(1)} %copy.75), kind=kLoop, calls=%fused_computation | loop fusion | flops 11010048 | bytes 14684160 | tf_op jit(solution)/shard_map/convert_element_type | solution.py:70
  524.3 7.1 %copy.77 = bf16[8,64,2,3584]{3,2,1,0:T(2,128)(2,1)} copy(bf16[8,64,2,3584]{3,1,2,0:T(8,128)(2,1)S(1)} %multiply_convert_fusion) | data formatting | bytes 14680064 | tf_op jit(solution)/shard_map/convert_element_type | solution.py:70
  531.3 15.4 %convert_element_type.90 = bf16[1024,3584]{1,0:T(8,128)(2,1)} reshape(bf16[8,64,2,3584]{3,2,1,0:T(2,128)(2,1)} %copy.77) | data formatting | bytes 14680064 | tf_op jit(solution)/shard_map/convert_element_type | solution.py:70
  546.8 7.3 %fusion.5 = (bf16[1,128,3584]{1,2,0:T(8,128)(2,1)}, bf16[1,128,3584]{1,2,0:T(8,128)(2,1)}) fusion(bf16[1,128,3584]{1,2,0:T(8,128)(2,1)S(1)} %copy.78, bf16[1,128,3584]{1,2,0:T(8,128)(2,1)S(1)} %copy.68, bf16[1024,3584]{1,0:T(8,128)(2,1)} %convert_element_type.90, bf16[1,1024,128]{2,1,0:T(8,128)(2,1)S(1)} %copy-done.5), kind=kOutput, calls=%fused_computation.11 | convolution fusion | flops 946405376 | bytes 11272192 | tf_op jit(solution)/shard_map/dot_general | solution.py:71
  554.1 2.3 copy.80
  556.4 1.3 copy.81
  557.7 0.2 reshape.64
  557.9 0.8 copy.79
  (17 shorter events, 0.1 us)
Async XLA Ops:
  7.2 2.0 copy-start
  7.2 62.6 %all-gather.2.cloned.1.call-start = ((), (), s32[]{:S(2)}) async-start(), calls=%async_computation.3 | async-start | bytes 8257536 | tf_op jit(solution)/shard_map/all_gather | solution.py:54
  84.5 15.7 %copy-start.5 = (bf16[1,1024,128]{2,1,0:T(8,128)(2,1)S(1)}, bf16[1,1024,128]{2,1,0:T(8,128)(2,1)}, u32[]{:S(2)}) copy-start(bf16[1,1024,128]{2,1,0:T(8,128)(2,1)} %param.9) | copy-start | bytes 786436
  84.5 334.6 %all-to-all-start = ((bf16[8,64,2,3584]{3,2,0,1:T(2,128)(2,1)}), bf16[8,64,2,3584]{3,2,0,1:T(2,128)(2,1)}, u32[]{:S(2)}, u32[]{:S(2)}) async-start(bf16[8,64,2,3584]{3,2,0,1:T(2,128)(2,1)} %copy.66), calls=%async_computation | async-start | bytes 14680064 | tf_op jit(solution)/shard_map/all_to_all | solution.py:58
  426.5 15.5 %copy-start.2 = (bf16[1,128,3584]{2,1,0:T(8,128)(2,1)S(1)}, bf16[1,128,3584]{2,1,0:T(8,128)(2,1)}, u32[]{:S(2)}) copy-start(bf16[1,128,3584]{2,1,0:T(8,128)(2,1)} %param.10) | copy-start | bytes 2752516
  442.1 30.6 %copy-start.6 = (f32[128,8]{0,1:T(8,128)S(1)}, f32[128,8]{0,1:T(8,128)}, u32[]{:S(2)}) copy-start(f32[128,8]{0,1:T(8,128)} %param.8) | copy-start | bytes 12292
  447.6 26.8 %copy-start.3 = (bf16[1,128,3584]{2,1,0:T(8,128)(2,1)S(1)}, bf16[1,128,3584]{2,1,0:T(8,128)(2,1)}, u32[]{:S(2)}) copy-start(bf16[1,128,3584]{2,1,0:T(8,128)(2,1)} %param.11) | copy-start | bytes 2752516
  466.0 19.7 %all-to-all-start.1 = ((f32[64,1,2]{2,1,0:T(1,128)}), f32[64,1,2]{2,1,0:T(1,128)}, u32[]{:S(2)}, u32[]{:S(2)}) async-start(f32[64,1,2]{2,1,0:T(1,128)} %bitcast.3), calls=%async_computation.1 | async-start | bytes 65536 | tf_op jit(solution)/shard_map/all_to_all | solution.py:83
  498.4 17.8 %all-to-all-start.2 = ((bf16[8,64,2]{0,2,1:T(2,128)(2,1)}), bf16[8,64,2]{0,2,1:T(2,128)(2,1)S(1)}, u32[]{:S(2)}, u32[]{:S(2)}) async-start(bf16[8,64,2]{0,2,1:T(2,128)(2,1)} %copy.72), calls=%async_computation.2 | async-start | bytes 65536 | tf_op jit(solution)/shard_map/all_to_all | solution.py:59
  554.1 2.4 copy-start.4
  554.1 4.7 copy-start.1
Sparse Core Ops, SparseCore 0:
  11.1 58.6 all-gather.1
where the time goes:
time: 567 us; the launch traced here: 566 us
  waiting for transfers between devices  401 us (71%)
  local copies, waits for them, and re-layouts  70.1 us (12%)
  starting transfers between devices  27.2 us (5%)
  blocking collectives  27.1 us (5%)
  between operations  14.2 us (3%)
  other arithmetic  13.2 us (2%)
  matrix products  13.2 us (2%)
    all_to_all x1, waiting for transfers between devices, on_device(): lax.all_to_all(copies, 'node', split_axis=1, concat_axis=1, tiled=True)  319 us
    all_gather x1, waiting for transfers between devices, on_device(): lax.all_gather(departing_rows[None], 'local', axis=0, tiled=True)  58.8 us
    convert_element_type x2, local copies, waits for them, and re-layouts, on_device(): (slot_gates[:, None] * arrived_rows.astype(jnp.float32)).astype(jnp.bfloa...  22.5 us
    psum x1, blocking collectives, on_device(): summed = lax.psum(score_terms, 'local')  17.6 us
    all_to_all x1, starting transfers between devices, on_device(): lax.all_to_all(copies, 'node', split_axis=1, concat_axis=1, tiled=True)  15.7 us
    reshape x1, local copies, waits for them, and re-layouts, on_device(): arrived_rows = arrived.reshape(-1, feature_count)  15.5 us
    all_gather x1, local copies, waits for them, and re-layouts, on_device(): lax.all_gather(departing_rows[None], 'local', axis=0, tiled=True)  14.7 us
    all_to_all x1, waiting for transfers between devices, on_device(): lax.all_to_all(copy_gates, 'node', split_axis=1, concat_axis=1, tiled=True)  12.4 us
  transfers between devices with their start and end apart: 4, of which 4 were waited for; matrix products, arithmetic and copies ran while one was open for 1% of the time, Pallas kernels for 0%

commit v1 on v0

v1 whole, which is shorter than its diff:
```python
import jax
import jax.numpy as jnp
from jax import lax
from jax.sharding import PartitionSpec as P

EXPERTS_PER_HOST = 4
CAP = 2


beta_second = 0.95
learn_rate = 0.002
decay_rate = 0.1
epsilon = 1e-08
correct_second = 0.994079470779666


def route(picked_experts, gate_values, node_count):
    transit_rows = picked_experts % EXPERTS_PER_HOST == 0
    row_present = jnp.any(transit_rows, 1)
    destination_node = jnp.sum(jnp.where(transit_rows, picked_experts // EXPERTS_PER_HOST, 0), 1)
    tokens = picked_experts.shape[0]
    same = (
        (destination_node[:, None] == destination_node[None, :])
        & row_present[None, :]
        & (jnp.arange(tokens)[None, :] < jnp.arange(tokens)[:, None])
    )
    within_rank = jnp.sum(same.astype(jnp.int32), 1)
    slot_index = destination_node * CAP + within_rank
    expert_location = (
        jnp.arange(node_count * CAP, dtype=jnp.int32)[:, None] == slot_index[None, :]
    ) & row_present[None, :]
    matched_gate = jnp.sum(jnp.where(transit_rows, gate_values, 0.0), 1).astype(jnp.bfloat16)
    return expert_location, transit_rows, row_present, matched_gate.astype(jnp.float32)


def on_device(grad_out, expert_ids, gate_weights, saved_hidden, down_weight, second_moment):
    node_count = lax.axis_size("node")
    members = lax.axis_size("local")
    feature_count = grad_out.shape[1]
    expert_location, transit_rows, row_present, gate = route(expert_ids, gate_weights, node_count)
    slot_gate = jnp.sum(jnp.where(expert_location, gate[None, :], 0.0), 1)
    picked = jnp.dot(expert_location.astype(jnp.bfloat16), grad_out, preferred_element_type=jnp.float32)
    scaled_out = (slot_gate[:, None] * picked).astype(jnp.bfloat16)
    arrived = lax.all_to_all(
        scaled_out.reshape(node_count, CAP, feature_count), "node", split_axis=0, concat_axis=0, tiled=True
    )
    scaled = lax.all_gather(arrived.reshape(node_count * CAP, feature_count), "local", axis=0, tiled=True)
    weight_now = down_weight[0]
    hidden_now = saved_hidden[0]
    hidden_f = lax.dot_general(
        scaled, weight_now, (((1,), (1,)), ((), ())), preferred_element_type=jnp.float32
    )
    slot_score = jnp.sum(hidden_f * hidden_now.astype(jnp.float32), 1)
    grad = lax.dot_general(
        hidden_now, scaled, (((0,), (0,)), ((), ())), preferred_element_type=jnp.float32
    )
    second_new = (
        beta_second * second_moment[0].astype(jnp.float32) + (1.0 - beta_second) * grad * grad
    )
    weight_f = weight_now.astype(jnp.float32)
    update = grad / (jnp.sqrt(second_new / correct_second) + epsilon) + decay_rate * weight_f
    weight_new = weight_f - learn_rate * update
    score_terms = slot_score.reshape(members, node_count * CAP)
    summed = lax.psum(score_terms, "local")
    own_terms = lax.dynamic_slice_in_dim(summed, lax.axis_index("local"), 1, 0)
    returned = lax.all_to_all(
        own_terms.reshape(node_count, CAP), "node", split_axis=0, concat_axis=0, tiled=True
    )
    returned_flat = returned.reshape(node_count * CAP)
    token_score = jnp.sum(jnp.where(expert_location, returned_flat[:, None], 0.0), 0)
    token_gradient = jnp.where(row_present, token_score / jnp.where(row_present, gate, 1.0), 0.0)
    gate_weight_gradient = jnp.where(transit_rows, token_gradient[:, None], 0.0)
    return (
        gate_weight_gradient,
        hidden_f.astype(jnp.bfloat16)[None],
        weight_new.astype(jnp.bfloat16)[None],
        second_new.astype(jnp.bfloat16)[None],
    )


def solution(mesh):
    return jax.shard_map(
        on_device,
        mesh=mesh,
        in_specs=(
            P(("node", "local"), None),
            P(("node", "local"), None),
            P(("node", "local"), None),
            P("node", None, "local"),
            P("node", "local", None),
            P("node", "local", None),
        ),
        out_specs=(
            P(("node", "local"), None),
            P("node", None, "local"),
            P("node", "local", None),
            P("node", "local", None),
        ),
        check_vma=False,
    )
```

time: 567 us -> 182 us (0.32)
  waiting for transfers between devices: 401 us -> 48 us
  local copies, waits for them, and re-layouts: 70.1 us -> 10.3 us
  blocking collectives: 27.1 us -> 76.6 us
  starting transfers between devices: 27.2 us -> 15.4 us
  other arithmetic: 13.2 us -> 3.23 us
    all_to_all x2 -> x0, waiting for transfers between devices: 331 us -> none  [the longest x1 319 us: on_device(): lax.all_to_all(copies, 'node', split_axis=1, concat_axis=1, tiled=True)]
    all_to_all x0 -> x1, blocking collectives: none -> 64.6 us  [on_device(): lax.all_to_all(scaled_out.reshape(node_count, CAP, feature_count), 'node'...]
    convert_element_type x7 -> x0, local copies, waits for them, and re-layouts: 23.1 us -> none  [the longest x2 22.5 us: on_device(): (slot_gates[:, None] * arrived_rows.astype(jnp.float32)).astype(jnp.bfloa...]
    all_to_all x2 -> x0, starting transfers between devices: 20.5 us -> none  [the longest x1 15.7 us: on_device(): lax.all_to_all(copies, 'node', split_axis=1, concat_axis=1, tiled=True)]
    all_gather x2 -> x0, local copies, waits for them, and re-layouts: 15.4 us -> none  [the longest x1 14.7 us: on_device(): lax.all_gather(departing_rows[None], 'local', axis=0, tiled=True)]
    reshape x1 -> x2, local copies, waits for them, and re-layouts: 15.5 us -> 1.61 us  [the longest x1 1.27 us: on_device(): arrived.reshape(node_count * CAP, feature_count)]
    all_gather x1, waiting for transfers between devices: 58.8 us -> 46.4 us  [on_device(): lax.all_gather(arrived.reshape(node_count * CAP, feature_count), 'local',...]
    all_gather x1 -> x0, blocking collectives: 9.49 us -> none  [on_device(): lax.all_gather(departing_gates[None], 'local', axis=0, tiled=True)]
  transfers between devices with their start and end apart: 4 -> 2, of which waited for: 4 -> 2; matrix products, arithmetic and copies ran while one was open for 1% -> 8% of each run, Pallas kernels for 0% -> 0%
where the time goes in v1:
time: 182 us; the launch traced here: 181 us
  blocking collectives  76.6 us (42%)
  waiting for transfers between devices  48 us (26%)
  starting transfers between devices  15.4 us (8%)
  between operations  14.2 us (8%)
  matrix products  13.1 us (7%)
  local copies, waits for them, and re-layouts  10.3 us (6%)
  other arithmetic  3.23 us (2%)
    all_to_all x1, blocking collectives, on_device(): lax.all_to_all(scaled_out.reshape(node_count, CAP, feature_count), 'node'...  64.6 us
    all_gather x1, waiting for transfers between devices, on_device(): lax.all_gather(arrived.reshape(node_count * CAP, feature_count), 'local',...  46.4 us
    all_to_all x1, starting transfers between devices, on_device(): lax.all_to_all(own_terms.reshape(node_count, CAP), 'node', split_axis=0,...  15.4 us
    psum x1, blocking collectives, on_device(): summed = lax.psum(score_terms, 'local')  12 us
    unnamed x20, local copies, waits for them, and re-layouts  7.28 us
    dot_general x1, matrix products, on_device(): lax.dot_general(hidden_now, scaled, (((0,), (0,)), ((), ())), preferred_e...  7.21 us
    dot_general x1, matrix products, on_device(): lax.dot_general(scaled, weight_now, (((1,), (1,)), ((), ())), preferred_e...  5.52 us
  transfers between devices with their start and end apart: 2, of which 2 were waited for; matrix products, arithmetic and copies ran while one was open for 8% of the time, Pallas kernels for 0%

profile of v1, /device:TPU:1, one launch (start us, length us, event | category | flops | bytes accessed | tf_op | source)
XLA Modules:
  0.0 180.8 jit_solution(6624401985966689629)
XLA Ops:
  7.2 0.0 copy-start
  7.2 0.0 all-gather.2.cloned.1.call-start
  7.2 0.8 fusion.18
  8.0 0.7 select_reduce_fusion.2
  8.7 0.0 copy-start.5
  8.7 0.2 convert_reduce_fusion
  8.9 0.1 select_reduce_fusion.1
  9.0 0.3 copy-done.5
  9.3 0.0 copy-done
  9.3 0.4 fusion
  9.7 0.3 reshape.51
  10.1 64.6 %all_to_all.14 = bf16[64,2,3584]{2,1,0:T(2,128)(2,1)S(1)} all-to-all(bf16[64,2,3584]{2,1,0:T(2,128)(2,1)S(1)} %reshape.51), channel_id=1, replica_groups=mesh['node'=64,'local'=8] {'node'}, dimensions={0} | all-to-all | bytes 1835008 | tf_op jit(solution)/shard_map/all_to_all | solution.py:44
  74.6 0.0 copy-start.4
  74.6 0.0 copy-start.1
  74.6 1.3 reshape.52
  75.9 0.0 copy-start.2
  75.9 0.0 all-gather.2.cloned.1.call-update
  75.9 0.0 copy-done.4
  75.9 0.1 copy.30
  76.1 0.0 copy-done.1
  76.1 1.3 copy.32
  77.4 0.0 copy-done.2
  77.4 1.3 copy.29
  78.6 0.0 copy-start.3
  78.6 46.4 %all-gather.2.cloned.1.call-done = bf16[1024,3584]{1,0:T(8,128)(2,1)} async-done(((bf16[128,3584]{1,0:T(8,128)(2,1)}), bf16[1024,3584]{1,0:T(8,128)(2,1)}) %all-gather.2.cloned.1.call-update) | async-done | bytes 7340048 | tf_op jit(solution)/shard_map/all_gather | solution.py:47
  125.0 5.5 %convert_bitcast_fusion = (bf16[1,1024,128]{1,2,0:T(8,128)(2,1)S(1)}, f32[1024]{0:T(1024)S(1)}) fusion(bf16[1,1024,128]{1,2,0:T(8,128)(2,1)S(1)} %copy.30, bf16[1024,3584]{1,0:T(8,128)(2,1)} %all-gather.2.cloned.1.call-done, bf16[1,128,3584]{2,1,0:T(8,128)(2,1)S(1)} %copy-done.2), kind=kOutput, calls=%fused_computation.17 | convolution fusion | flops 940047360 | bytes 8785920 | tf_op jit(solution)/shard_map/dot_general | solution.py:50
  130.5 12.0 %psum.7 = f32[8,128]{1,0:T(8,128)S(1)} all-reduce(f32[8,128]{1,0:T(8,128)S(1)} %bitcast.41), channel_id=1, replica_groups=mesh['node'=64,'local'=8] {'local'}, use_global_device_ids=true, to_apply=%region_6.7 | all-reduce | flops 1024 | bytes 8192 | tf_op jit(solution)/shard_map/psum | solution.py:64
  142.6 0.7 all_to_all.10
  143.3 15.4 %all-to-all-start.1 = ((f32[64,1,2]{2,1,0:T(1,128)}), f32[64,1,2]{2,1,0:T(1,128)S(1)}, u32[]{:S(2)}, u32[]{:S(2)}) async-start(f32[64,1,2]{2,1,0:T(1,128)} %bitcast.3), calls=%async_computation.1 | async-start | bytes 65536 | tf_op jit(solution)/shard_map/all_to_all | solution.py:66
  158.7 0.0 copy-done.3
  158.7 7.2 %fusion.6 = (bf16[1,128,3584]{1,2,0:T(8,128)(2,1)}, bf16[1,128,3584]{1,2,0:T(8,128)(2,1)S(1)}) fusion(bf16[1,128,3584]{1,2,0:T(8,128)(2,1)S(1)} %copy-done.3, bf16[1,128,3584]{1,2,0:T(8,128)(2,1)} %copy.29, bf16[1024,3584]{1,0:T(8,128)(2,1)} %all-gather.2.cloned.1.call-done, bf16[1,1024,128]{2,1,0:T(8,128)(2,1)S(1)} %copy-done.4), kind=kOutput, calls=%fused_computation.11 | convolution fusion | flops 946405376 | bytes 11272192 | tf_op jit(solution)/shard_map/dot_general | solution.py:54
  165.9 0.8 copy.33
  166.8 0.0 copy-start.6
  166.8 2.2 %copy.35 = bf16[1,128,3584]{2,1,0:T(8,128)(2,1)} copy(bf16[1,128,3584]{1,2,0:T(8,128)(2,1)} %get-tuple-element.22) | data formatting | bytes 1835008
  169.0 1.3 copy.34
  170.2 1.6 all-to-all-done.1
  171.8 0.5 broadcast.39
  172.3 0.7 reduce.7
  173.1 0.1 broadcast_in_dim.70
  173.2 0.1 select_reduce_fusion
  173.3 0.0 copy-done.6
  173.3 0.6 broadcast_select_fusion
  (5 shorter events, 0.1 us)
Async XLA Ops:
  7.2 2.1 %copy-start = (bf16[128,3584]{1,0:T(8,128)(2,1)S(1)}, bf16[128,3584]{1,0:T(8,128)(2,1)}, u32[]{:S(2)}) copy-start(bf16[128,3584]{1,0:T(8,128)(2,1)} %param.6) | copy-start | bytes 2752516
  7.2 117.8 %all-gather.2.cloned.1.call-start = ((), (), s32[]{:S(2)}) async-start(), calls=%async_computation.2 | async-start | bytes 8257536 | tf_op jit(solution)/shard_map/all_gather | solution.py:47
  8.7 0.6 copy-start.5
  74.6 1.3 copy-start.4
  74.6 1.5 copy-start.1
  75.9 1.5 copy-start.2
  78.6 80.1 %copy-start.3 = (bf16[1,128,3584]{1,2,0:T(8,128)(2,1)S(1)}, bf16[1,128,3584]{1,2,0:T(8,128)(2,1)}, u32[]{:S(2)}) copy-start(bf16[1,128,3584]{1,2,0:T(8,128)(2,1)} %copy.32) | copy-start | bytes 2752516
  143.3 28.5 %all-to-all-start.1 = ((f32[64,1,2]{2,1,0:T(1,128)}), f32[64,1,2]{2,1,0:T(1,128)S(1)}, u32[]{:S(2)}, u32[]{:S(2)}) async-start(f32[64,1,2]{2,1,0:T(1,128)} %bitcast.3), calls=%async_computation.1 | async-start | bytes 65536 | tf_op jit(solution)/shard_map/all_to_all | solution.py:66
  166.8 6.6 %copy-start.6 = (bf16[128]{0:T(256)(128)(2,1)S(1)}, bf16[128]{0:T(256)(128)(2,1)}, u32[]{:S(2)}) copy-start(bf16[128]{0:T(256)(128)(2,1)} %copy-done.5) | copy-start | bytes 772
Sparse Core Ops, SparseCore 0:
  76.0 48.9 all-gather.1

commit v2 on v1

v2 whole, which is shorter than its diff:
```python
import functools
import jax
import jax.numpy as jnp
from jax import lax
from jax.experimental import pallas as pl
from jax.experimental.pallas import tpu as pltpu
from jax.sharding import PartitionSpec as P

EXPERTS_PER_HOST = 4
CAP = 2
TILE = 896
VMEM_BYTES = 12 << 20


beta_second = 0.95
learn_rate = 0.002
decay_rate = 0.1
epsilon = 1e-08
correct_second = 0.994079470779666


def route(picked_experts, gate_values, node_count):
    transit_rows = picked_experts % EXPERTS_PER_HOST == 0
    row_present = jnp.any(transit_rows, 1)
    destination_node = jnp.sum(jnp.where(transit_rows, picked_experts // EXPERTS_PER_HOST, 0), 1)
    tokens = picked_experts.shape[0]
    same = (
        (destination_node[:, None] == destination_node[None, :])
        & row_present[None, :]
        & (jnp.arange(tokens)[None, :] < jnp.arange(tokens)[:, None])
    )
    within_rank = jnp.sum(same.astype(jnp.int32), 1)
    slot_index = destination_node * CAP + within_rank
    expert_location = (
        jnp.arange(node_count * CAP, dtype=jnp.int32)[:, None] == slot_index[None, :]
    ) & row_present[None, :]
    matched_gate = jnp.sum(jnp.where(transit_rows, gate_values, 0.0), 1).astype(jnp.bfloat16)
    return expert_location, transit_rows, row_present, matched_gate.astype(jnp.float32)


def gather_near(block):
    members = lax.axis_size("local")
    up = [(i, (i + 2) % members) for i in range(members)]
    down = [(i, (i - 2) % members) for i in range(members)]
    swap = [(i, i ^ 1) for i in range(members)]
    low = lax.ppermute(block, "local", up)
    high = lax.ppermute(block, "local", down)
    other = lax.ppermute(block, "local", swap)
    return block, other, low, high


def gather_more(low, high, core):
    members = lax.axis_size("local")
    onward = [(i, (i + (2 if i % 2 == 0 else -2)) % members) for i in range(members)]
    swap = [(i, i ^ 1) for i in range(members)]
    far = lax.ppermute(jnp.where(core == 0, low, high), "local", onward)
    return lax.ppermute(low, "local", swap), lax.ppermute(high, "local", swap), far


def hand_over(piece):
    members = lax.axis_size("local")
    return lax.ppermute(piece, "local", [(i, i ^ 1) for i in range(members)])


def piece_blocks(me, members):
    mate = me + 1 - 2 * (me % 2)
    blocks = [me, mate, me - 2, me + 2, mate - 2, mate + 2, me + 4, mate + 4]
    return jnp.stack([b % members for b in blocks])


def block_at(block):
    return pl.ds(pl.multiple_of(block * 128, 128), 128)


def back_kernel(partners_ref, *refs):
    pieces, hidden_ref, out_ref = refs[:8], refs[8], refs[9]
    left = jnp.concatenate([hidden_ref[block_at(partners_ref[k]), :] for k in range(8)], 1)

    @pl.loop(0, out_ref.shape[1] // TILE, unroll=True)
    def _(j):
        at = pl.ds(pl.multiple_of(j * TILE, TILE), TILE)
        right = jnp.concatenate([r[:, at] for r in pieces], 0)
        out_ref[:, at] = jnp.dot(left, right, preferred_element_type=jnp.float32)


IN_VMEM = pl.BlockSpec(memory_space=pltpu.VMEM)
IN_SMEM = pl.BlockSpec(memory_space=pltpu.SMEM)


def back_projection(partners, pieces, hidden_own):
    width = pieces[0].shape[1]
    return pl.pallas_call(
        back_kernel,
        in_specs=[IN_SMEM] + [IN_VMEM] * 9,
        out_specs=IN_VMEM,
        out_shape=jax.ShapeDtypeStruct((pieces[0].shape[0], width), jnp.float32),
        compiler_params=pltpu.CompilerParams(vmem_limit_bytes=VMEM_BYTES),
        cost_estimate=pl.CostEstimate(
            flops=2 * 128 * 1024 * width, bytes_accessed=10 * 128 * width * 2, transcendentals=0
        ),
        name="back_projection",
    )(partners, *pieces, hidden_own)


def own_slots(hidden_now, me):
    members = lax.axis_size("local")
    rows, units = hidden_now.shape
    held = hidden_now.reshape(2, 2, 2, rows // members, units)
    for axis, bit in ((2, 1), (1, 2), (0, 4)):
        mine = (me // bit) % 2
        low = lax.index_in_dim(held, 0, axis, keepdims=False)
        high = lax.index_in_dim(held, 1, axis, keepdims=False)
        keep = jnp.where(mine == 0, low, high)
        give = jnp.where(mine == 0, high, low)
        got = lax.ppermute(give, "local", [(i, i ^ bit) for i in range(members)])
        held = jnp.stack([keep, got], axis)
    return held.reshape(rows, units)


def piece_partners(me):
    even = 1 - (me // 2) % 2
    below = 2 + 4 * even
    above = 6 - 4 * even
    return jnp.stack([0 * me, 0 * me + 1, below, above, below + 1, above + 1, 0 * me + 4, 0 * me + 5])


def grad_kernel(count, start, final, blocks_ref, *refs):
    rows, refs = refs[:count], refs[count:]
    (hidden_t, weight_ref), refs = refs[:2], refs[2:]
    if final:
        part_ref, done_ref, second_ref, hidden_out, weight_out, second_out, total_u = refs
    else:
        part_out, total_out, total_u = refs
    left = jnp.concatenate([hidden_t[:, block_at(blocks_ref[start + k])] for k in range(count)], 1)
    total_u[...] = jnp.zeros_like(total_u)

    @pl.loop(0, weight_ref.shape[1] // TILE, unroll=True)
    def _(j):
        at = pl.ds(pl.multiple_of(j * TILE, TILE), TILE)
        weight_now = weight_ref[:, at]
        right = jnp.concatenate([r[:, at] for r in rows], 0)
        grad = jnp.dot(left, right, preferred_element_type=jnp.float32)
        total_u[...] += lax.dot_general(
            right, weight_now, (((1,), (1,)), ((), ())), preferred_element_type=jnp.float32
        )
        if not final:
            part_out[:, at] = grad
            return
        grad = grad + part_ref[:, at]
        second_new = beta_second * second_ref[:, at].astype(jnp.float32) + (1.0 - beta_second) * grad * grad
        weight_f = weight_now.astype(jnp.float32)
        update = grad / (jnp.sqrt(second_new * (1.0 / correct_second)) + epsilon) + decay_rate * weight_f
        weight_out[:, at] = (weight_f - learn_rate * update).astype(jnp.bfloat16)
        second_out[:, at] = second_new.astype(jnp.bfloat16)

    if not final:
        total_out[...] = total_u[...].astype(jnp.bfloat16)
        return
    for k in range(start + count):
        at = block_at(blocks_ref[k])
        if k < start:
            hidden_out[at, :] = done_ref[k * 128 : k * 128 + 128, :]
        else:
            hidden_out[at, :] = total_u[(k - start) * 128 : (k - start) * 128 + 128, :].astype(jnp.bfloat16)


def grads(blocks, pieces, start, hidden_t, weight_now, before=None, second_now=None):
    width = weight_now.shape[1]
    units, slots = hidden_t.shape
    count = len(pieces)
    final = before is not None
    if final:
        out_shape = [
            jax.ShapeDtypeStruct((slots, units), jnp.bfloat16),
            jax.ShapeDtypeStruct((units, width), jnp.bfloat16),
            jax.ShapeDtypeStruct((units, width), jnp.bfloat16),
        ]
        extra = (*before, second_now)
    else:
        out_shape = [
            jax.ShapeDtypeStruct((units, width), jnp.float32),
            jax.ShapeDtypeStruct((count * 128, units), jnp.bfloat16),
        ]
        extra = ()
    operands = (*pieces, hidden_t, weight_now, *extra)
    return pl.pallas_call(
        functools.partial(grad_kernel, count, start, final),
        in_specs=[IN_SMEM] + [IN_VMEM] * len(operands),
        out_specs=[IN_VMEM] * len(out_shape),
        out_shape=out_shape,
        scratch_shapes=[pltpu.VMEM((count * 128, units), jnp.float32)],
        compiler_params=pltpu.CompilerParams(vmem_limit_bytes=VMEM_BYTES),
        cost_estimate=pl.CostEstimate(
            flops=4 * 128 * 128 * count * width, bytes_accessed=(count + 6) * 128 * width * 2, transcendentals=0
        ),
        name="grads_last" if final else "grads_first",
    )(blocks, *operands)


def on_device(grad_out, expert_ids, gate_weights, saved_hidden, down_weight, second_moment):
    node_count = lax.axis_size("node")
    members = lax.axis_size("local")
    feature_count = grad_out.shape[1]
    me = lax.axis_index("local").astype(jnp.int32)
    expert_location, transit_rows, row_present, gate = route(expert_ids, gate_weights, node_count)
    slot_gate = jnp.sum(jnp.where(expert_location, gate[None, :], 0.0), 1)
    picked = jnp.dot(expert_location.astype(jnp.bfloat16), grad_out, preferred_element_type=jnp.float32)
    scaled_out = (slot_gate[:, None] * picked).astype(jnp.bfloat16)
    blocks = piece_blocks(me, members)
    leaving = scaled_out.reshape(node_count, CAP, feature_count)
    scaled = lax.all_to_all(leaving, "node", split_axis=0, concat_axis=0, tiled=True).reshape(
        node_count * CAP, feature_count
    )
    core = me % 2
    weight_now = down_weight[0]
    hidden_now = saved_hidden[0]
    hidden_t = hidden_now.T
    near = gather_near(weight_now)
    low, high, hidden_later = lax.optimization_barrier((near[2], near[3], hidden_now))
    more = gather_more(low, high, core)
    hidden_own = own_slots(hidden_later, me)
    far, hidden_own = lax.optimization_barrier((more[2], hidden_own))
    y = back_projection(piece_partners(me), near + more[:2] + (far, hand_over(far)), hidden_own)
    own_score = jnp.sum(scaled.astype(jnp.float32) * y, 1)
    returned = lax.all_to_all(
        own_score.reshape(node_count, CAP), "node", split_axis=0, concat_axis=0, tiled=True
    )
    near = gather_near(scaled)
    low, high, returned = lax.optimization_barrier((near[2], near[3], returned))
    more = gather_more(low, high, core)
    early = len(near)
    returned_flat = returned.reshape(node_count * CAP)
    token_score = jnp.sum(jnp.where(expert_location, returned_flat[:, None], 0.0), 0)
    token_gradient = jnp.where(row_present, token_score / jnp.where(row_present, gate, 1.0), 0.0)
    gate_weight_gradient = jnp.where(transit_rows, token_gradient[:, None], 0.0)
    other, gate_weight_gradient = lax.optimization_barrier((near[1], gate_weight_gradient))
    before = grads(blocks, (near[0], other, near[2], near[3]), 0, hidden_t, weight_now)
    far, before = lax.optimization_barrier((more[2], before))
    hidden_out, weight_new, second_new = grads(
        blocks, (more[0], more[1], far, hand_over(far)), early, hidden_t, weight_now, before, second_moment[0]
    )
    return (gate_weight_gradient, hidden_out[None], weight_new[None], second_new[None])


def solution(mesh):
    return jax.shard_map(
        on_device,
        mesh=mesh,
        in_specs=(
            P(("node", "local"), None),
            P(("node", "local"), None),
            P(("node", "local"), None),
            P("node", None, "local"),
            P("node", "local", None),
            P("node", "local", None),
        ),
        out_specs=(
            P(("node", "local"), None),
            P("node", None, "local"),
            P("node", "local", None),
            P("node", "local", None),
        ),
        check_vma=False,
    )
```

time: 182 us -> 158 us (0.87)
  blocking collectives: 76.6 us -> 0 us
  starting transfers between devices: 15.4 us -> 89.5 us
  Pallas kernels: 0 us -> 13.1 us
  between operations: 14.2 us -> 1.22 us
  matrix products: 13.1 us -> 0.4 us
  waiting for transfers between devices: 48 us -> 38.4 us
  other arithmetic: 3.23 us -> 8.06 us
  local copies, waits for them, and re-layouts: 10.3 us -> 6.02 us
    all_to_all x1 -> x0, blocking collectives: 64.6 us -> none  [on_device(): lax.all_to_all(scaled_out.reshape(node_count, CAP, feature_count), 'node'...]
    ppermute x0 -> x17, starting transfers between devices: none -> 55.5 us  [the longest x3 9.84 us: own_slots(): got = lax.ppermute(give, 'local', [(i, i ^ bit) for i in range(members)])]
    all_gather x1 -> x0, waiting for transfers between devices: 46.4 us -> none  [on_device(): lax.all_gather(arrived.reshape(node_count * CAP, feature_count), 'local',...]
    ppermute x0 -> x17, waiting for transfers between devices: none -> 27.9 us  [the longest x2 17.4 us: gather_near(): low = lax.ppermute(block, 'local', up)]
    all_to_all x1 -> x2, starting transfers between devices: 15.4 us -> 34 us  [the longest x1 19.5 us: on_device(): lax.all_to_all(leaving, 'node', split_axis=0, concat_axis=0, tiled=True)]
    pallas_call x0 -> x3, Pallas kernels: none -> 13.1 us  [the longest x2 9.03 us: grads(): pl.pallas_call(functools.partial(grad_kernel, count, start, final), in_sp...]
    dot_general x2 -> x0, matrix products: 12.7 us -> none  [the longest x1 7.21 us: on_device(): lax.dot_general(hidden_now, scaled, (((0,), (0,)), ((), ())), preferred_e...]
    psum x1 -> x0, blocking collectives: 12 us -> none  [on_device(): summed = lax.psum(score_terms, 'local')]
  transfers between devices with their start and end apart: 2 -> 19, of which waited for: 2 -> 6; matrix products, arithmetic and copies ran while one was open for 8% -> 6% of each run, Pallas kernels for 0% -> 5%
where the time goes in v2:
time: 158 us; the launch traced here: 157 us
  starting transfers between devices  89.5 us (57%)
  waiting for transfers between devices  38.4 us (24%)
  Pallas kernels  13.1 us (8%)
  other arithmetic  8.06 us (5%)
  local copies, waits for them, and re-layouts  6.02 us (4%)
    all_to_all x1, starting transfers between devices, on_device(): lax.all_to_all(leaving, 'node', split_axis=0, concat_axis=0, tiled=True)  19.5 us
    ppermute x2, waiting for transfers between devices, gather_near(): low = lax.ppermute(block, 'local', up)  17.4 us
    all_to_all x1, starting transfers between devices, on_device(): lax.all_to_all(own_score.reshape(node_count, CAP), 'node', split_axis=0,...  14.5 us
    all_to_all x1, waiting for transfers between devices, on_device(): lax.all_to_all(own_score.reshape(node_count, CAP), 'node', split_axis=0,...  10.6 us
    ppermute x3, starting transfers between devices, own_slots(): got = lax.ppermute(give, 'local', [(i, i ^ bit) for i in range(members)])  9.84 us
    pallas_call x2, Pallas kernels, grads(): pl.pallas_call(functools.partial(grad_kernel, count, start, final), in_sp...  9.03 us
    ppermute x2, starting transfers between devices, hand_over(): return lax.ppermute(piece, 'local', [(i, i ^ 1) for i in range(members)])  8.21 us
    ppermute x2, starting transfers between devices, gather_more(): lax.ppermute(low, 'local', swap)  7.95 us
  transfers between devices with their start and end apart: 19, of which 6 were waited for; matrix products, arithmetic and copies ran while one was open for 6% of the time, Pallas kernels for 5%

profile of v2, /device:TPU:1, one launch (start us, length us, event | category | flops | bytes accessed | tf_op | source)
XLA Modules:
  0.0 156.8 jit_solution(8135769619614600083)
XLA Ops:
  0.6 0.8 fusion.13
  1.4 0.7 fusion.10
  2.1 0.2 convert_reduce_fusion
  2.3 0.7 select_reduce_fusion.2
  3.1 0.1 select_reduce_fusion.1
  3.2 0.4 fusion
  3.6 1.3 reshape.56
  4.9 19.5 %all-to-all-start = ((bf16[64,2,3584]{2,1,0:T(2,128)(2,1)}), bf16[64,2,3584]{2,1,0:T(2,128)(2,1)}, u32[]{:S(2)}, u32[]{:S(2)}) async-start(bf16[64,2,3584]{2,1,0:T(2,128)(2,1)} %reshape.56), calls=%async_computation | async-start | bytes 1835008 | tf_op jit(solution)/shard_map/all_to_all | solution.py:211
  24.4 3.1 %collective-permute-start.4 = (bf16[128,3584]{1,0:T(8,128)(2,1)S(1)}, bf16[128,3584]{1,0:T(8,128)(2,1)}, u32[]{:S(2)}, u32[]{:S(2)}) collective-permute-start(bf16[128,3584]{1,0:T(8,128)(2,1)S(1)} %bitcast.35), channel_id=1, source_target_pairs={{0,2},{1,3},{2,4},{3,5},{4,6},{5,7},{6,0},{7,1},{8,10},{9,11},{10,... | collective-permute-start | bytes 2752520 | tf_op jit(solution)/shard_map/ppermute | solution.py:46
  27.5 3.4 %collective-permute-start.5 = (bf16[128,3584]{1,0:T(8,128)(2,1)S(1)}, bf16[128,3584]{1,0:T(8,128)(2,1)}, u32[]{:S(2)}, u32[]{:S(2)}) collective-permute-start(bf16[128,3584]{1,0:T(8,128)(2,1)S(1)} %bitcast.36), channel_id=1, source_target_pairs={{0,6},{1,7},{2,0},{3,1},{4,2},{5,3},{6,4},{7,5},{8,14},{9,15},{10,... | collective-permute-start | bytes 2752520 | tf_op jit(solution)/shard_map/ppermute | solution.py:47
  30.9 0.1 copy.47
  31.1 17.4 %collective-permute-done.4.refs_2_ = bf16[128,3584]{1,0:T(8,128)(2,1)} collective-permute-done((bf16[128,3584]{1,0:T(8,128)(2,1)S(1)}, bf16[128,3584]{1,0:T(8,128)(2,1)}, u32[]{:S(2)}, u32[]{:S(2)}) %collective-permute-start.4) | collective-permute-done | bytes 917536 | tf_op jit(solution)/shard_map/ppermute | solution.py:46
  48.5 1.6 %collective-permute-done.5.refs_3_ = bf16[128,3584]{1,0:T(8,128)(2,1)} collective-permute-done((bf16[128,3584]{1,0:T(8,128)(2,1)S(1)}, bf16[128,3584]{1,0:T(8,128)(2,1)}, u32[]{:S(2)}, u32[]{:S(2)}) %collective-permute-start.5) | collective-permute-done | bytes 917536 | tf_op jit(solution)/shard_map/ppermute | solution.py:47
  50.1 0.2 reshape.58
  50.3 0.4 fusion.15
  50.7 0.2 copy.60
  50.8 0.2 copy.61
  51.0 2.2 %broadcast_select_fusion.1 = bf16[128,3584]{1,0:T(8,128)(2,1)} fusion(bf16[128,3584]{1,0:T(8,128)(2,1)} %collective-permute-done.4.refs_2_, bf16[128,3584]{1,0:T(8,128)(2,1)} %collective-permute-done.5.refs_3_, pred[]{:T(512)S(6)} %eq.71), kind=kLoop, calls=%fused_computation.4 | loop fusion | flops 458752 | bytes 2752513 | tf_op jit(solution)/shard_map/jit(_where)/select_n | solution.py:56
  53.2 4.6 %collective-permute-start.8 = (bf16[128,3584]{1,0:T(8,128)(2,1)}, bf16[128,3584]{1,0:T(8,128)(2,1)}, u32[]{:S(2)}, u32[]{:S(2)}) collective-permute-start(bf16[128,3584]{1,0:T(8,128)(2,1)} %broadcast_select_fusion.1), channel_id=1, source_target_pairs={{0,2},{1,7},{2,4},{3,1},{4,6},{5,3},{6,0},{7,5},{8,10},{9,15},{10,... | collective-permute-start | bytes 2752520 | tf_op jit(solution)/shard_map/ppermute | solution.py:56
  57.8 2.9 %collective-permute-start.9 = (bf16[2,2,128,128]{3,2,1,0:T(8,128)(2,1)S(1)}, bf16[2,2,128,128]{3,2,1,0:T(8,128)(2,1)S(1)}, u32[]{:S(2)}, u32[]{:S(2)}) collective-permute-start(bf16[2,2,128,128]{3,2,1,0:T(8,128)(2,1)S(1)} %get-tuple-element.47), channel_id=1, source_target_pairs={{0,1},{1,0},{2,3},{3,2},{4,5},{5,4},{6,7},{7,6},{8,9},{9,8},{10,11... | collective-permute-start | bytes 393224 | tf_op jit(solution)/shard_map/ppermute | solution.py:115
  60.7 1.9 %collective-permute-start.3 = (bf16[128,3584]{1,0:T(8,128)(2,1)S(1)}, bf16[128,3584]{1,0:T(8,128)(2,1)}, u32[]{:S(2)}, u32[]{:S(2)}) collective-permute-start(bf16[128,3584]{1,0:T(8,128)(2,1)S(1)} %bitcast.37), channel_id=1, source_target_pairs={{0,1},{1,0},{2,3},{3,2},{4,5},{5,4},{6,7},{7,6},{8,9},{9,8},{10,11... | collective-permute-start | bytes 2752520 | tf_op jit(solution)/shard_map/ppermute | solution.py:48
  62.7 2.8 %collective-permute-start.10 = (bf16[2,2,128,128]{3,2,0,1:T(8,128)(2,1)S(1)}, bf16[2,2,128,128]{3,2,0,1:T(8,128)(2,1)S(1)}, u32[]{:S(2)}, u32[]{:S(2)}) collective-permute-start(bf16[2,2,128,128]{3,2,0,1:T(8,128)(2,1)S(1)} %get-tuple-element.45), channel_id=1, source_target_pairs={{0,2},{1,3},{2,0},{3,1},{4,6},{5,7},{6,4},{7,5},{8,10},{9,11},{10,... | collective-permute-start | bytes 393224 | tf_op jit(solution)/shard_map/ppermute | solution.py:115
  65.6 4.7 %collective-permute-done.10 = bf16[2,2,128,128]{3,2,0,1:T(8,128)(2,1)S(1)} collective-permute-done((bf16[2,2,128,128]{3,2,0,1:T(8,128)(2,1)S(1)}, bf16[2,2,128,128]{3,2,0,1:T(8,128)(2,1)S(1)}, u32[]{:S(2)}, u32[]{:S(2)}) %collective-permute-start.10) | collective-permute-done | bytes 131104 | tf_op jit(solution)/shard_map/ppermute | solution.py:115
  70.3 4.1 %collective-permute-start.11 = (bf16[2,2,128,128]{3,2,0,1:T(8,128)(2,1)S(1)}, bf16[2,2,128,128]{3,2,0,1:T(8,128)(2,1)S(1)}, u32[]{:S(2)}, u32[]{:S(2)}) collective-permute-start(bf16[2,2,128,128]{3,2,0,1:T(8,128)(2,1)S(1)} %get-tuple-element.43), channel_id=1, source_target_pairs={{0,4},{1,5},{2,6},{3,7},{4,0},{5,1},{6,2},{7,3},{8,12},{9,13},{10,... | collective-permute-start | bytes 393224 | tf_op jit(solution)/shard_map/ppermute | solution.py:115
  74.4 5.0 %collective-permute-start.6 = (bf16[128,3584]{1,0:T(8,128)(2,1)}, bf16[128,3584]{1,0:T(8,128)(2,1)}, u32[]{:S(2)}, u32[]{:S(2)}) collective-permute-start(bf16[128,3584]{1,0:T(8,128)(2,1)} %collective-permute-done.4.refs_2_), channel_id=1, source_target_pairs={{0,1},{1,0},{2,3},{3,2},{4,5},{5,4},{6,7},{7,6},{8,9},{9,8},{10,11... | collective-permute-start | bytes 2752520 | tf_op jit(solution)/shard_map/ppermute | solution.py:57
  79.5 1.9 %collective-permute-start.7 = (bf16[128,3584]{1,0:T(8,128)(2,1)}, bf16[128,3584]{1,0:T(8,128)(2,1)}, u32[]{:S(2)}, u32[]{:S(2)}) collective-permute-start(bf16[128,3584]{1,0:T(8,128)(2,1)} %collective-permute-done.5.refs_3_), channel_id=1, source_target_pairs={{0,1},{1,0},{2,3},{3,2},{4,5},{5,4},{6,7},{7,6},{8,9},{9,8},{10,11... | collective-permute-start | bytes 2752520 | tf_op jit(solution)/shard_map/ppermute | solution.py:57
  81.5 2.4 %collective-permute-start.12 = (bf16[128,3584]{1,0:T(8,128)(2,1)}, bf16[128,3584]{1,0:T(8,128)(2,1)}, u32[]{:S(2)}, u32[]{:S(2)}) collective-permute-start(bf16[128,3584]{1,0:T(8,128)(2,1)} %collective-permute-done.8.refs_6_), channel_id=1, source_target_pairs={{0,1},{1,0},{2,3},{3,2},{4,5},{5,4},{6,7},{7,6},{8,9},{9,8},{10,11... | collective-permute-start | bytes 2752520 | tf_op jit(solution)/shard_map/ppermute | solution.py:62
  83.9 2.5 %reshape.57.refs_0_ = bf16[128,3584]{1,0:T(8,128)(2,1)S(1)} reshape(bf16[64,2,3584]{2,1,0:T(2,128)(2,1)} %all-to-all-done) | data formatting | bytes 1835008 | tf_op jit(solution)/shard_map/reshape | solution.py:211
  86.4 3.5 %collective-permute-start.1 = (bf16[128,3584]{1,0:T(8,128)(2,1)S(1)}, bf16[128,3584]{1,0:T(8,128)(2,1)}, u32[]{:S(2)}, u32[]{:S(2)}) collective-permute-start(bf16[128,3584]{1,0:T(8,128)(2,1)S(1)} %reshape.57.refs_0_), channel_id=1, source_target_pairs={{0,2},{1,3},{2,4},{3,5},{4,6},{5,7},{6,0},{7,1},{8,10},{9,11},{10,... | collective-permute-start | bytes 2752520 | tf_op jit(solution)/shard_map/ppermute | solution.py:46
  89.9 3.2 %collective-permute-start.2 = (bf16[128,3584]{1,0:T(8,128)(2,1)S(1)}, bf16[128,3584]{1,0:T(8,128)(2,1)}, u32[]{:S(2)}, u32[]{:S(2)}) collective-permute-start(bf16[128,3584]{1,0:T(8,128)(2,1)S(1)} %reshape.57.refs_0_), channel_id=1, source_target_pairs={{0,6},{1,7},{2,0},{3,1},{4,2},{5,3},{6,4},{7,5},{8,14},{9,15},{10,... | collective-permute-start | bytes 2752520 | tf_op jit(solution)/shard_map/ppermute | solution.py:47
  93.2 4.1 %back_projection.1 = f32[128,3584]{1,0:T(8,128)S(1)} custom-call(s32[8]{0:T(128)S(1)} %stack.67.partners_ref, bf16[128,3584]{1,0:T(8,128)(2,1)S(1)} %bitcast.38, bf16[128,3584]{1,0:T(8,128)(2,1)} %collective-permute-done.3.refs_1_, bf16[128,3584]{1,0:T(8,128)(2,1)} %collective-permute-done.4.refs_2_, bf16[128,3584]{1,0:T(8,128)(2,1)} %collective-permute-done.5.refs_3_, ...), custom_call_target="tpu_custom_call" | custom-call | flops 939524096 | bytes 9175040 | tf_op jit(solution)/shard_map/back_projection/pallas_call | solution.py:92
  97.3 0.3 multiply_reduce_fusion
  97.6 0.8 all_to_all.12
  98.4 14.5 %all-to-all-start.1 = ((f32[64,1,2]{2,1,0:T(1,128)}), f32[64,1,2]{2,1,0:T(1,128)S(1)}, u32[]{:S(2)}, u32[]{:S(2)}) async-start(f32[64,1,2]{2,1,0:T(1,128)} %bitcast.13), calls=%async_computation.1 | async-start | bytes 65536 | tf_op jit(solution)/shard_map/all_to_all | solution.py:225
  112.9 2.6 %collective-permute-start = (bf16[128,3584]{1,0:T(8,128)(2,1)S(1)}, bf16[128,3584]{1,0:T(8,128)(2,1)}, u32[]{:S(2)}, u32[]{:S(2)}) collective-permute-start(bf16[128,3584]{1,0:T(8,128)(2,1)S(1)} %reshape.57.refs_0_), channel_id=1, source_target_pairs={{0,1},{1,0},{2,3},{3,2},{4,5},{5,4},{6,7},{7,6},{8,9},{9,8},{10,11... | collective-permute-start | bytes 2752520 | tf_op jit(solution)/shard_map/ppermute | solution.py:48
  115.5 10.6 %all-to-all-done.1 = f32[64,1,2]{2,1,0:T(1,128)S(1)} async-done(((f32[64,1,2]{2,1,0:T(1,128)}), f32[64,1,2]{2,1,0:T(1,128)S(1)}, u32[]{:S(2)}, u32[]{:S(2)}) %all-to-all-start.1) | async-done | bytes 544 | tf_op jit(solution)/shard_map/all_to_all | solution.py:225
  126.2 2.2 %broadcast_select_fusion = bf16[128,3584]{1,0:T(8,128)(2,1)} fusion(bf16[128,3584]{1,0:T(8,128)(2,1)} %collective-permute-done.1.refs_2_, bf16[128,3584]{1,0:T(8,128)(2,1)} %collective-permute-done.2.refs_3_, pred[]{:T(512)S(6)} %eq.71), kind=kLoop, calls=%fused_computation.3 | loop fusion | flops 458752 | bytes 2752513 | tf_op jit(solution)/shard_map/jit(_where)/select_n | solution.py:56
  128.4 3.4 %collective-permute-start.15 = (bf16[128,3584]{1,0:T(8,128)(2,1)}, bf16[128,3584]{1,0:T(8,128)(2,1)}, u32[]{:S(2)}, u32[]{:S(2)}) collective-permute-start(bf16[128,3584]{1,0:T(8,128)(2,1)} %broadcast_select_fusion), channel_id=1, source_target_pairs={{0,2},{1,7},{2,4},{3,1},{4,6},{5,3},{6,0},{7,5},{8,10},{9,15},{10,... | collective-permute-start | bytes 2752520 | tf_op jit(solution)/shard_map/ppermute | solution.py:56
  132.0 2.9 %collective-permute-start.13 = (bf16[128,3584]{1,0:T(8,128)(2,1)}, bf16[128,3584]{1,0:T(8,128)(2,1)}, u32[]{:S(2)}, u32[]{:S(2)}) collective-permute-start(bf16[128,3584]{1,0:T(8,128)(2,1)} %collective-permute-done.1.refs_2_), channel_id=1, source_target_pairs={{0,1},{1,0},{2,3},{3,2},{4,5},{5,4},{6,7},{7,6},{8,9},{9,8},{10,11... | collective-permute-start | bytes 2752520 | tf_op jit(solution)/shard_map/ppermute | solution.py:57
  134.9 1.9 %collective-permute-start.14 = (bf16[128,3584]{1,0:T(8,128)(2,1)}, bf16[128,3584]{1,0:T(8,128)(2,1)}, u32[]{:S(2)}, u32[]{:S(2)}) collective-permute-start(bf16[128,3584]{1,0:T(8,128)(2,1)} %collective-permute-done.2.refs_3_), channel_id=1, source_target_pairs={{0,1},{1,0},{2,3},{3,2},{4,5},{5,4},{6,7},{7,6},{8,9},{9,8},{10,11... | collective-permute-start | bytes 2752520 | tf_op jit(solution)/shard_map/ppermute | solution.py:57
  136.9 0.1 broadcast_in_dim.70
  137.1 0.1 select_reduce_fusion
  137.2 0.6 broadcast_select_fusion.5
  137.8 3.5 %grads_first.1 = (f32[128,3584]{1,0:T(8,128)S(1)}, bf16[512,128]{1,0:T(8,128)(2,1)S(1)}) custom-call(s32[8]{0:T(128)S(1)} %stack.82.blocks_ref, bf16[128,3584]{1,0:T(8,128)(2,1)S(1)} %reshape.57.refs_0_, bf16[128,3584]{1,0:T(8,128)(2,1)} %collective-permute-done.refs_1_, bf16[128,3584]{1,0:T(8,128)(2,1)} %collective-permute-done.1.refs_2_, ...), custom_call_target="tpu_custom_call" | custom-call | flops 939524096 | bytes 9175040 | tf_op jit(solution)/shard_map/grads_first/pallas_call | solution.py:186
  141.3 1.8 %collective-permute-done.15.refs_2_ = bf16[128,3584]{1,0:T(8,128)(2,1)} collective-permute-done((bf16[128,3584]{1,0:T(8,128)(2,1)}, bf16[128,3584]{1,0:T(8,128)(2,1)}, u32[]{:S(2)}, u32[]{:S(2)}) %collective-permute-start.15) | collective-permute-done | bytes 917536 | tf_op jit(solution)/shard_map/ppermute | solution.py:56
  143.1 5.8 %collective-permute-start.16 = (bf16[128,3584]{1,0:T(8,128)(2,1)}, bf16[128,3584]{1,0:T(8,128)(2,1)S(1)}, u32[]{:S(2)}, u32[]{:S(2)}) collective-permute-start(bf16[128,3584]{1,0:T(8,128)(2,1)} %collective-permute-done.15.refs_2_), channel_id=1, source_target_pairs={{0,1},{1,0},{2,3},{3,2},{4,5},{5,4},{6,7},{7,6},{8,9},{9,8},{10,11... | collective-permute-start | bytes 2752520 | tf_op jit(solution)/shard_map/ppermute | solution.py:62
  149.0 2.3 %collective-permute-done.16.refs_3_ = bf16[128,3584]{1,0:T(8,128)(2,1)S(1)} collective-permute-done((bf16[128,3584]{1,0:T(8,128)(2,1)}, bf16[128,3584]{1,0:T(8,128)(2,1)S(1)}, u32[]{:S(2)}, u32[]{:S(2)}) %collective-permute-start.16) | collective-permute-done | bytes 917536 | tf_op jit(solution)/shard_map/ppermute | solution.py:62
  151.2 5.5 %grads_last.1 = (bf16[1024,128]{1,0:T(8,128)(2,1)}, bf16[128,3584]{1,0:T(8,128)(2,1)}, bf16[128,3584]{1,0:T(8,128)(2,1)}) custom-call(s32[8]{0:T(128)S(1)} %stack.82.blocks_ref, bf16[128,3584]{1,0:T(8,128)(2,1)} %collective-permute-done.13.refs_0_, bf16[128,3584]{1,0:T(8,128)(2,1)} %collective-permute-done.14.refs_1_, ...), custom_call_target="tpu_custom_call" | custom-call | flops 939524096 | bytes 9175040 | tf_op jit(solution)/shard_map/grads_last/pallas_call | solution.py:186
  (33 shorter events, 0.5 us)
Async XLA Ops:
  0.6 2.5 %copy-start = (bf16[128,3584]{1,0:T(8,128)(2,1)S(1)}, bf16[128,3584]{1,0:T(8,128)(2,1)}, u32[]{:S(2)}) copy-start(bf16[128,3584]{1,0:T(8,128)(2,1)} %param.6) | copy-start | bytes 2752516
  3.6 20.8 %copy-start.1 = (bf16[1,128,3584]{2,1,0:T(8,128)(2,1)S(1)}, bf16[1,128,3584]{2,1,0:T(8,128)(2,1)}, u32[]{:S(2)}) copy-start(bf16[1,128,3584]{2,1,0:T(8,128)(2,1)} %param.10) | copy-start | bytes 2752516
  3.6 27.3 %copy-start.3 = (bf16[1,1024,128]{2,1,0:T(8,128)(2,1)S(1)}, bf16[1,1024,128]{2,1,0:T(8,128)(2,1)}, u32[]{:S(2)}) copy-start(bf16[1,1024,128]{2,1,0:T(8,128)(2,1)} %param.9) | copy-start | bytes 786436
  4.9 79.0 %all-to-all-start = ((bf16[64,2,3584]{2,1,0:T(2,128)(2,1)}), bf16[64,2,3584]{2,1,0:T(2,128)(2,1)}, u32[]{:S(2)}, u32[]{:S(2)}) async-start(bf16[64,2,3584]{2,1,0:T(2,128)(2,1)} %reshape.56), calls=%async_computation | async-start | bytes 1835008 | tf_op jit(solution)/shard_map/all_to_all | solution.py:211
  24.4 24.1 %collective-permute-start.4 = (bf16[128,3584]{1,0:T(8,128)(2,1)S(1)}, bf16[128,3584]{1,0:T(8,128)(2,1)}, u32[]{:S(2)}, u32[]{:S(2)}) collective-permute-start(bf16[128,3584]{1,0:T(8,128)(2,1)S(1)} %bitcast.35), channel_id=1, source_target_pairs={{0,2},{1,3},{2,4},{3,5},{4,6},{5,7},{6,0},{7,1},{8,10},{9,11},{10,... | collective-permute-start | bytes 2752520 | tf_op jit(solution)/shard_map/ppermute | solution.py:46
  27.5 22.6 %collective-permute-start.5 = (bf16[128,3584]{1,0:T(8,128)(2,1)S(1)}, bf16[128,3584]{1,0:T(8,128)(2,1)}, u32[]{:S(2)}, u32[]{:S(2)}) collective-permute-start(bf16[128,3584]{1,0:T(8,128)(2,1)S(1)} %bitcast.36), channel_id=1, source_target_pairs={{0,6},{1,7},{2,0},{3,1},{4,2},{5,3},{6,4},{7,5},{8,14},{9,15},{10,... | collective-permute-start | bytes 2752520 | tf_op jit(solution)/shard_map/ppermute | solution.py:47
  53.2 28.3 %collective-permute-start.8 = (bf16[128,3584]{1,0:T(8,128)(2,1)}, bf16[128,3584]{1,0:T(8,128)(2,1)}, u32[]{:S(2)}, u32[]{:S(2)}) collective-permute-start(bf16[128,3584]{1,0:T(8,128)(2,1)} %broadcast_select_fusion.1), channel_id=1, source_target_pairs={{0,2},{1,7},{2,4},{3,1},{4,6},{5,3},{6,0},{7,5},{8,10},{9,15},{10,... | collective-permute-start | bytes 2752520 | tf_op jit(solution)/shard_map/ppermute | solution.py:56
  57.8 4.9 %collective-permute-start.9 = (bf16[2,2,128,128]{3,2,1,0:T(8,128)(2,1)S(1)}, bf16[2,2,128,128]{3,2,1,0:T(8,128)(2,1)S(1)}, u32[]{:S(2)}, u32[]{:S(2)}) collective-permute-start(bf16[2,2,128,128]{3,2,1,0:T(8,128)(2,1)S(1)} %get-tuple-element.47), channel_id=1, source_target_pairs={{0,1},{1,0},{2,3},{3,2},{4,5},{5,4},{6,7},{7,6},{8,9},{9,8},{10,11... | collective-permute-start | bytes 393224 | tf_op jit(solution)/shard_map/ppermute | solution.py:115
  60.7 29.2 %collective-permute-start.3 = (bf16[128,3584]{1,0:T(8,128)(2,1)S(1)}, bf16[128,3584]{1,0:T(8,128)(2,1)}, u32[]{:S(2)}, u32[]{:S(2)}) collective-permute-start(bf16[128,3584]{1,0:T(8,128)(2,1)S(1)} %bitcast.37), channel_id=1, source_target_pairs={{0,1},{1,0},{2,3},{3,2},{4,5},{5,4},{6,7},{7,6},{8,9},{9,8},{10,11... | collective-permute-start | bytes 2752520 | tf_op jit(solution)/shard_map/ppermute | solution.py:48
  62.7 7.5 %collective-permute-start.10 = (bf16[2,2,128,128]{3,2,0,1:T(8,128)(2,1)S(1)}, bf16[2,2,128,128]{3,2,0,1:T(8,128)(2,1)S(1)}, u32[]{:S(2)}, u32[]{:S(2)}) collective-permute-start(bf16[2,2,128,128]{3,2,0,1:T(8,128)(2,1)S(1)} %get-tuple-element.45), channel_id=1, source_target_pairs={{0,2},{1,3},{2,0},{3,1},{4,6},{5,7},{6,4},{7,5},{8,10},{9,11},{10,... | collective-permute-start | bytes 393224 | tf_op jit(solution)/shard_map/ppermute | solution.py:115
  70.3 11.1 %collective-permute-start.11 = (bf16[2,2,128,128]{3,2,0,1:T(8,128)(2,1)S(1)}, bf16[2,2,128,128]{3,2,0,1:T(8,128)(2,1)S(1)}, u32[]{:S(2)}, u32[]{:S(2)}) collective-permute-start(bf16[2,2,128,128]{3,2,0,1:T(8,128)(2,1)S(1)} %get-tuple-element.43), channel_id=1, source_target_pairs={{0,4},{1,5},{2,6},{3,7},{4,0},{5,1},{6,2},{7,3},{8,12},{9,13},{10,... | collective-permute-start | bytes 393224 | tf_op jit(solution)/shard_map/ppermute | solution.py:115
  74.4 18.7 %collective-permute-start.6 = (bf16[128,3584]{1,0:T(8,128)(2,1)}, bf16[128,3584]{1,0:T(8,128)(2,1)}, u32[]{:S(2)}, u32[]{:S(2)}) collective-permute-start(bf16[128,3584]{1,0:T(8,128)(2,1)} %collective-permute-done.4.refs_2_), channel_id=1, source_target_pairs={{0,1},{1,0},{2,3},{3,2},{4,5},{5,4},{6,7},{7,6},{8,9},{9,8},{10,11... | collective-permute-start | bytes 2752520 | tf_op jit(solution)/shard_map/ppermute | solution.py:57
  79.5 13.7 %collective-permute-start.7 = (bf16[128,3584]{1,0:T(8,128)(2,1)}, bf16[128,3584]{1,0:T(8,128)(2,1)}, u32[]{:S(2)}, u32[]{:S(2)}) collective-permute-start(bf16[128,3584]{1,0:T(8,128)(2,1)} %collective-permute-done.5.refs_3_), channel_id=1, source_target_pairs={{0,1},{1,0},{2,3},{3,2},{4,5},{5,4},{6,7},{7,6},{8,9},{9,8},{10,11... | collective-permute-start | bytes 2752520 | tf_op jit(solution)/shard_map/ppermute | solution.py:57
  81.5 11.7 %collective-permute-start.12 = (bf16[128,3584]{1,0:T(8,128)(2,1)}, bf16[128,3584]{1,0:T(8,128)(2,1)}, u32[]{:S(2)}, u32[]{:S(2)}) collective-permute-start(bf16[128,3584]{1,0:T(8,128)(2,1)} %collective-permute-done.8.refs_6_), channel_id=1, source_target_pairs={{0,1},{1,0},{2,3},{3,2},{4,5},{5,4},{6,7},{7,6},{8,9},{9,8},{10,11... | collective-permute-start | bytes 2752520 | tf_op jit(solution)/shard_map/ppermute | solution.py:62
  86.4 39.8 %collective-permute-start.1 = (bf16[128,3584]{1,0:T(8,128)(2,1)S(1)}, bf16[128,3584]{1,0:T(8,128)(2,1)}, u32[]{:S(2)}, u32[]{:S(2)}) collective-permute-start(bf16[128,3584]{1,0:T(8,128)(2,1)S(1)} %reshape.57.refs_0_), channel_id=1, source_target_pairs={{0,2},{1,3},{2,4},{3,5},{4,6},{5,7},{6,0},{7,1},{8,10},{9,11},{10,... | collective-permute-start | bytes 2752520 | tf_op jit(solution)/shard_map/ppermute | solution.py:46
  89.9 36.3 %collective-permute-start.2 = (bf16[128,3584]{1,0:T(8,128)(2,1)S(1)}, bf16[128,3584]{1,0:T(8,128)(2,1)}, u32[]{:S(2)}, u32[]{:S(2)}) collective-permute-start(bf16[128,3584]{1,0:T(8,128)(2,1)S(1)} %reshape.57.refs_0_), channel_id=1, source_target_pairs={{0,6},{1,7},{2,0},{3,1},{4,2},{5,3},{6,4},{7,5},{8,14},{9,15},{10,... | collective-permute-start | bytes 2752520 | tf_op jit(solution)/shard_map/ppermute | solution.py:47
  98.4 27.7 %all-to-all-start.1 = ((f32[64,1,2]{2,1,0:T(1,128)}), f32[64,1,2]{2,1,0:T(1,128)S(1)}, u32[]{:S(2)}, u32[]{:S(2)}) async-start(f32[64,1,2]{2,1,0:T(1,128)} %bitcast.13), calls=%async_computation.1 | async-start | bytes 65536 | tf_op jit(solution)/shard_map/all_to_all | solution.py:225
  112.9 24.9 %collective-permute-start = (bf16[128,3584]{1,0:T(8,128)(2,1)S(1)}, bf16[128,3584]{1,0:T(8,128)(2,1)}, u32[]{:S(2)}, u32[]{:S(2)}) collective-permute-start(bf16[128,3584]{1,0:T(8,128)(2,1)S(1)} %reshape.57.refs_0_), channel_id=1, source_target_pairs={{0,1},{1,0},{2,3},{3,2},{4,5},{5,4},{6,7},{7,6},{8,9},{9,8},{10,11... | collective-permute-start | bytes 2752520 | tf_op jit(solution)/shard_map/ppermute | solution.py:48
  128.4 14.7 %collective-permute-start.15 = (bf16[128,3584]{1,0:T(8,128)(2,1)}, bf16[128,3584]{1,0:T(8,128)(2,1)}, u32[]{:S(2)}, u32[]{:S(2)}) collective-permute-start(bf16[128,3584]{1,0:T(8,128)(2,1)} %broadcast_select_fusion), channel_id=1, source_target_pairs={{0,2},{1,7},{2,4},{3,1},{4,6},{5,3},{6,0},{7,5},{8,10},{9,15},{10,... | collective-permute-start | bytes 2752520 | tf_op jit(solution)/shard_map/ppermute | solution.py:56
  132.0 17.0 %collective-permute-start.13 = (bf16[128,3584]{1,0:T(8,128)(2,1)}, bf16[128,3584]{1,0:T(8,128)(2,1)}, u32[]{:S(2)}, u32[]{:S(2)}) collective-permute-start(bf16[128,3584]{1,0:T(8,128)(2,1)} %collective-permute-done.1.refs_2_), channel_id=1, source_target_pairs={{0,1},{1,0},{2,3},{3,2},{4,5},{5,4},{6,7},{7,6},{8,9},{9,8},{10,11... | collective-permute-start | bytes 2752520 | tf_op jit(solution)/shard_map/ppermute | solution.py:57
  134.9 14.1 %collective-permute-start.14 = (bf16[128,3584]{1,0:T(8,128)(2,1)}, bf16[128,3584]{1,0:T(8,128)(2,1)}, u32[]{:S(2)}, u32[]{:S(2)}) collective-permute-start(bf16[128,3584]{1,0:T(8,128)(2,1)} %collective-permute-done.2.refs_3_), channel_id=1, source_target_pairs={{0,1},{1,0},{2,3},{3,2},{4,5},{5,4},{6,7},{7,6},{8,9},{9,8},{10,11... | collective-permute-start | bytes 2752520 | tf_op jit(solution)/shard_map/ppermute | solution.py:57
  137.8 13.4 %copy-start.2 = (bf16[1,128,3584]{2,1,0:T(8,128)(2,1)S(1)}, bf16[1,128,3584]{2,1,0:T(8,128)(2,1)}, u32[]{:S(2)}) copy-start(bf16[1,128,3584]{2,1,0:T(8,128)(2,1)} %param.11) | copy-start | bytes 2752516
  143.1 8.1 %collective-permute-start.16 = (bf16[128,3584]{1,0:T(8,128)(2,1)}, bf16[128,3584]{1,0:T(8,128)(2,1)S(1)}, u32[]{:S(2)}, u32[]{:S(2)}) collective-permute-start(bf16[128,3584]{1,0:T(8,128)(2,1)} %collective-permute-done.15.refs_2_), channel_id=1, source_target_pairs={{0,1},{1,0},{2,3},{3,2},{4,5},{5,4},{6,7},{7,6},{8,9},{9,8},{10,11... | collective-permute-start | bytes 2752520 | tf_op jit(solution)/shard_map/ppermute | solution.py:62

commit v3 on v2

--- a/solution.py
+++ b/solution.py
@@ -221,6 +221,7 @@
     hidden_own = own_slots(hidden_later, me)
     far, hidden_own = lax.optimization_barrier((more[2], hidden_own))
     y = back_projection(piece_partners(me), near + more[:2] + (far, hand_over(far)), hidden_own)
+    scaled, y = lax.optimization_barrier((scaled, y))
     own_score = jnp.sum(scaled.astype(jnp.float32) * y, 1)
     returned = lax.all_to_all(
         own_score.reshape(node_count, CAP), "node", split_axis=0, concat_axis=0, tiled=True

time: 158 us -> 149 us (0.943)
  waiting for transfers between devices: 38.4 us -> 26.8 us
  local copies, waits for them, and re-layouts: 6.02 us -> 12.6 us
  starting transfers between devices: 89.5 us -> 84 us
    ppermute x2, waiting for transfers between devices: 17.4 us -> 0.01 us  [gather_near(): low = lax.ppermute(block, 'local', up)]
    ppermute x3, waiting for transfers between devices: 4.69 us -> 10.2 us  [own_slots(): got = lax.ppermute(give, 'local', [(i, i ^ bit) for i in range(members)])]
    unnamed x11 -> x19, local copies, waits for them, and re-layouts: 0.48 us -> 4.52 us
    ppermute x3, starting transfers between devices: 9.84 us -> 7.47 us  [own_slots(): got = lax.ppermute(give, 'local', [(i, i ^ bit) for i in range(members)])]
    ppermute x2, waiting for transfers between devices: 2.27 us -> 4.4 us  [hand_over(): return lax.ppermute(piece, 'local', [(i, i ^ 1) for i in range(members)])]
    ppermute x2, starting transfers between devices: 7.92 us -> 6 us  [gather_more(): far = lax.ppermute(jnp.where(core == 0, low, high), 'local', onward)]
    reshape x1, local copies, waits for them, and re-layouts: 1.27 us -> 3.1 us  [on_device(): leaving = scaled_out.reshape(node_count, CAP, feature_count)]
    ppermute x2, starting transfers between devices: 7.95 us -> 6.16 us  [gather_more(): lax.ppermute(low, 'local', swap)]
  transfers between devices with their start and end apart: 19 -> 19, of which waited for: 6 -> 8; matrix products, arithmetic and copies ran while one was open for 6% -> 12% of each run, Pallas kernels for 5% -> 5%
where the time goes in v3:
time: 149 us; the launch traced here: 148 us
  starting transfers between devices  84 us (56%)
  waiting for transfers between devices  26.8 us (18%)
  local copies, waits for them, and re-layouts  12.6 us (8%)
  Pallas kernels  12.5 us (8%)
  other arithmetic  9.5 us (6%)
    all_to_all x1, starting transfers between devices, on_device(): lax.all_to_all(leaving, 'node', split_axis=0, concat_axis=0, tiled=True)  18.9 us
    all_to_all x1, starting transfers between devices, on_device(): lax.all_to_all(own_score.reshape(node_count, CAP), 'node', split_axis=0,...  14.4 us
    all_to_all x1, waiting for transfers between devices, on_device(): lax.all_to_all(own_score.reshape(node_count, CAP), 'node', split_axis=0,...  10.2 us
    ppermute x3, waiting for transfers between devices, own_slots(): got = lax.ppermute(give, 'local', [(i, i ^ bit) for i in range(members)])  10.2 us
    pallas_call x2, Pallas kernels, grads(): pl.pallas_call(functools.partial(grad_kernel, count, start, final), in_sp...  8.95 us
    ppermute x2, starting transfers between devices, hand_over(): return lax.ppermute(piece, 'local', [(i, i ^ 1) for i in range(members)])  8.57 us
    ppermute x3, starting transfers between devices, own_slots(): got = lax.ppermute(give, 'local', [(i, i ^ bit) for i in range(members)])  7.47 us
    ppermute x2, starting transfers between devices, gather_near(): low = lax.ppermute(block, 'local', up)  7.23 us
  transfers between devices with their start and end apart: 19, of which 8 were waited for; matrix products, arithmetic and copies ran while one was open for 12% of the time, Pallas kernels for 5%

profile of v3, /device:TPU:1, one launch (start us, length us, event | category | flops | bytes accessed | tf_op | source)
XLA Modules:
  0.0 147.9 jit_solution(16435610586324002182)
XLA Ops:
  0.6 4.1 %collective-permute-start.1 = (bf16[128,3584]{1,0:T(8,128)(2,1)}, bf16[128,3584]{1,0:T(8,128)(2,1)S(1)}, u32[]{:S(2)}, u32[]{:S(2)}) collective-permute-start(bf16[128,3584]{1,0:T(8,128)(2,1)} %bitcast.35), channel_id=1, source_target_pairs={{0,2},{1,3},{2,4},{3,5},{4,6},{5,7},{6,0},{7,1},{8,10},{9,11},{10,... | collective-permute-start | bytes 2752520 | tf_op jit(solution)/shard_map/ppermute | solution.py:46
  4.7 3.2 %collective-permute-start.2 = (bf16[128,3584]{1,0:T(8,128)(2,1)}, bf16[128,3584]{1,0:T(8,128)(2,1)S(1)}, u32[]{:S(2)}, u32[]{:S(2)}) collective-permute-start(bf16[128,3584]{1,0:T(8,128)(2,1)} %bitcast.36), channel_id=1, source_target_pairs={{0,6},{1,7},{2,0},{3,1},{4,2},{5,3},{6,4},{7,5},{8,14},{9,15},{10,... | collective-permute-start | bytes 2752520 | tf_op jit(solution)/shard_map/ppermute | solution.py:47
  7.9 0.7 fusion.13
  8.6 0.7 fusion.10
  9.4 0.7 select_reduce_fusion.2
  10.1 0.2 convert_reduce_fusion
  10.4 1.3 fusion
  11.7 3.1 %reshape.56 = bf16[64,2,3584]{2,1,0:T(2,128)(2,1)} reshape(bf16[128,3584]{1,0:T(8,128)(2,1)} %fusion) | data formatting | bytes 1835008 | tf_op jit(solution)/shard_map/reshape | solution.py:210
  14.8 18.9 %all-to-all-start = ((bf16[64,2,3584]{2,1,0:T(2,128)(2,1)}), bf16[64,2,3584]{2,1,0:T(2,128)(2,1)}, u32[]{:S(2)}, u32[]{:S(2)}) async-start(bf16[64,2,3584]{2,1,0:T(2,128)(2,1)} %reshape.56), calls=%async_computation | async-start | bytes 1835008 | tf_op jit(solution)/shard_map/all_to_all | solution.py:211
  33.9 0.2 reshape.58
  34.1 1.1 fusion.15
  35.1 1.1 copy.60
  36.3 0.8 copy.61
  37.1 2.3 %broadcast_select_fusion.1 = bf16[128,3584]{1,0:T(8,128)(2,1)} fusion(bf16[128,3584]{1,0:T(8,128)(2,1)S(1)} %collective-permute-done.1.refs_2_, bf16[128,3584]{1,0:T(8,128)(2,1)} %copy-done.3, pred[]{:T(512)S(6)} %eq.71), kind=kLoop, calls=%fused_computation.4 | loop fusion | flops 458752 | bytes 2752513 | tf_op jit(solution)/shard_map/jit(_where)/select_n | solution.py:56
  39.3 3.2 %collective-permute-start.5 = (bf16[128,3584]{1,0:T(8,128)(2,1)}, bf16[128,3584]{1,0:T(8,128)(2,1)}, u32[]{:S(2)}, u32[]{:S(2)}) collective-permute-start(bf16[128,3584]{1,0:T(8,128)(2,1)} %broadcast_select_fusion.1), channel_id=1, source_target_pairs={{0,2},{1,7},{2,4},{3,1},{4,6},{5,3},{6,0},{7,5},{8,10},{9,15},{10,... | collective-permute-start | bytes 2752520 | tf_op jit(solution)/shard_map/ppermute | solution.py:56
  42.6 1.9 %collective-permute-start.6 = (bf16[2,2,128,128]{3,2,1,0:T(8,128)(2,1)S(1)}, bf16[2,2,128,128]{3,2,1,0:T(8,128)(2,1)S(1)}, u32[]{:S(2)}, u32[]{:S(2)}) collective-permute-start(bf16[2,2,128,128]{3,2,1,0:T(8,128)(2,1)S(1)} %get-tuple-element.51), channel_id=1, source_target_pairs={{0,1},{1,0},{2,3},{3,2},{4,5},{5,4},{6,7},{7,6},{8,9},{9,8},{10,11... | collective-permute-start | bytes 393224 | tf_op jit(solution)/shard_map/ppermute | solution.py:115
  44.5 1.3 collective-permute-done.6
  45.8 2.1 %collective-permute-start.7 = (bf16[2,2,128,128]{3,2,0,1:T(8,128)(2,1)S(1)}, bf16[2,2,128,128]{3,2,0,1:T(8,128)(2,1)S(1)}, u32[]{:S(2)}, u32[]{:S(2)}) collective-permute-start(bf16[2,2,128,128]{3,2,0,1:T(8,128)(2,1)S(1)} %get-tuple-element.49), channel_id=1, source_target_pairs={{0,2},{1,3},{2,0},{3,1},{4,6},{5,7},{6,4},{7,5},{8,10},{9,11},{10,... | collective-permute-start | bytes 393224 | tf_op jit(solution)/shard_map/ppermute | solution.py:115
  48.0 8.9 %collective-permute-done.7 = bf16[2,2,128,128]{3,2,0,1:T(8,128)(2,1)S(1)} collective-permute-done((bf16[2,2,128,128]{3,2,0,1:T(8,128)(2,1)S(1)}, bf16[2,2,128,128]{3,2,0,1:T(8,128)(2,1)S(1)}, u32[]{:S(2)}, u32[]{:S(2)}) %collective-permute-start.7) | collective-permute-done | bytes 131104 | tf_op jit(solution)/shard_map/ppermute | solution.py:115
  56.9 3.4 %collective-permute-start.8 = (bf16[2,2,128,128]{3,2,0,1:T(8,128)(2,1)S(1)}, bf16[2,2,128,128]{3,2,0,1:T(8,128)(2,1)S(1)}, u32[]{:S(2)}, u32[]{:S(2)}) collective-permute-start(bf16[2,2,128,128]{3,2,0,1:T(8,128)(2,1)S(1)} %get-tuple-element.47), channel_id=1, source_target_pairs={{0,4},{1,5},{2,6},{3,7},{4,0},{5,1},{6,2},{7,3},{8,12},{9,13},{10,... | collective-permute-start | bytes 393224 | tf_op jit(solution)/shard_map/ppermute | solution.py:115
  60.4 1.9 %collective-permute-start = (bf16[128,3584]{1,0:T(8,128)(2,1)S(1)}, bf16[128,3584]{1,0:T(8,128)(2,1)}, u32[]{:S(2)}, u32[]{:S(2)}) collective-permute-start(bf16[128,3584]{1,0:T(8,128)(2,1)S(1)} %bitcast.37), channel_id=1, source_target_pairs={{0,1},{1,0},{2,3},{3,2},{4,5},{5,4},{6,7},{7,6},{8,9},{9,8},{10,11... | collective-permute-start | bytes 2752520 | tf_op jit(solution)/shard_map/ppermute | solution.py:48
  62.3 2.4 %collective-permute-start.3 = (bf16[128,3584]{1,0:T(8,128)(2,1)S(1)}, bf16[128,3584]{1,0:T(8,128)(2,1)}, u32[]{:S(2)}, u32[]{:S(2)}) collective-permute-start(bf16[128,3584]{1,0:T(8,128)(2,1)S(1)} %collective-permute-done.1.refs_2_), channel_id=1, source_target_pairs={{0,1},{1,0},{2,3},{3,2},{4,5},{5,4},{6,7},{7,6},{8,9},{9,8},{10,11... | collective-permute-start | bytes 2752520 | tf_op jit(solution)/shard_map/ppermute | solution.py:57
  64.7 1.9 %collective-permute-start.4 = (bf16[128,3584]{1,0:T(8,128)(2,1)}, bf16[128,3584]{1,0:T(8,128)(2,1)}, u32[]{:S(2)}, u32[]{:S(2)}) collective-permute-start(bf16[128,3584]{1,0:T(8,128)(2,1)} %copy-done.3), channel_id=1, source_target_pairs={{0,1},{1,0},{2,3},{3,2},{4,5},{5,4},{6,7},{7,6},{8,9},{9,8},{10,11... | collective-permute-start | bytes 2752520 | tf_op jit(solution)/shard_map/ppermute | solution.py:57
  66.7 2.4 %collective-permute-start.9 = (bf16[128,3584]{1,0:T(8,128)(2,1)}, bf16[128,3584]{1,0:T(8,128)(2,1)}, u32[]{:S(2)}, u32[]{:S(2)}) collective-permute-start(bf16[128,3584]{1,0:T(8,128)(2,1)} %collective-permute-done.5.refs_6_), channel_id=1, source_target_pairs={{0,1},{1,0},{2,3},{3,2},{4,5},{5,4},{6,7},{7,6},{8,9},{9,8},{10,11... | collective-permute-start | bytes 2752520 | tf_op jit(solution)/shard_map/ppermute | solution.py:62
  69.3 0.2 collective-permute-done.4.refs_5_
  69.4 2.1 %collective-permute-done.9.refs_7_ = bf16[128,3584]{1,0:T(8,128)(2,1)} collective-permute-done((bf16[128,3584]{1,0:T(8,128)(2,1)}, bf16[128,3584]{1,0:T(8,128)(2,1)}, u32[]{:S(2)}, u32[]{:S(2)}) %collective-permute-start.9) | collective-permute-done | bytes 917536 | tf_op jit(solution)/shard_map/ppermute | solution.py:62
  71.6 1.2 copy-done.4
  72.7 3.5 %back_projection.1 = f32[128,3584]{1,0:T(8,128)S(1)} custom-call(s32[8]{0:T(128)S(1)} %stack.67.partners_ref, bf16[128,3584]{1,0:T(8,128)(2,1)S(1)} %bitcast.38, bf16[128,3584]{1,0:T(8,128)(2,1)} %collective-permute-done.refs_1_, bf16[128,3584]{1,0:T(8,128)(2,1)S(1)} %collective-permute-done.1.refs_2_, bf16[128,3584]{1,0:T(8,128)(2,1)S(1)} %copy-done.4, ...), custom_call_target="tpu_custom_call" | custom-call | flops 939524096 | bytes 9175040 | tf_op jit(solution)/shard_map/back_projection/pallas_call | solution.py:92
  76.3 1.3 copy-done.2
  77.6 0.2 all-to-all-done
  77.8 2.5 %reshape.57.refs_0_ = bf16[128,3584]{1,0:T(8,128)(2,1)S(1)} reshape(bf16[64,2,3584]{2,1,0:T(2,128)(2,1)} %all-to-all-done) | data formatting | bytes 1835008 | tf_op jit(solution)/shard_map/reshape | solution.py:211
  80.3 3.1 %collective-permute-start.11 = (bf16[128,3584]{1,0:T(8,128)(2,1)S(1)}, bf16[128,3584]{1,0:T(8,128)(2,1)}, u32[]{:S(2)}, u32[]{:S(2)}) collective-permute-start(bf16[128,3584]{1,0:T(8,128)(2,1)S(1)} %reshape.57.refs_0_), channel_id=1, source_target_pairs={{0,2},{1,3},{2,4},{3,5},{4,6},{5,7},{6,0},{7,1},{8,10},{9,11},{10,... | collective-permute-start | bytes 2752520 | tf_op jit(solution)/shard_map/ppermute | solution.py:46
  83.4 3.3 %collective-permute-start.12 = (bf16[128,3584]{1,0:T(8,128)(2,1)S(1)}, bf16[128,3584]{1,0:T(8,128)(2,1)}, u32[]{:S(2)}, u32[]{:S(2)}) collective-permute-start(bf16[128,3584]{1,0:T(8,128)(2,1)S(1)} %reshape.57.refs_0_), channel_id=1, source_target_pairs={{0,6},{1,7},{2,0},{3,1},{4,2},{5,3},{6,4},{7,5},{8,14},{9,15},{10,... | collective-permute-start | bytes 2752520 | tf_op jit(solution)/shard_map/ppermute | solution.py:47
  86.8 1.8 %multiply_reduce_fusion = f32[128]{0:T(128)S(1)} fusion(f32[128,3584]{1,0:T(8,128)} %copy-done.2, bf16[128,3584]{1,0:T(8,128)(2,1)S(1)} %reshape.57.refs_0_), kind=kLoop, calls=%fused_computation.2 | loop fusion | flops 1376128 | bytes 2753024 | tf_op jit(solution)/shard_map/reduce_sum | solution.py:225
  88.6 0.8 all_to_all.12
  89.3 14.4 %all-to-all-start.1 = ((f32[64,1,2]{2,1,0:T(1,128)}), f32[64,1,2]{2,1,0:T(1,128)S(1)}, u32[]{:S(2)}, u32[]{:S(2)}) async-start(f32[64,1,2]{2,1,0:T(1,128)} %bitcast.13), calls=%async_computation.1 | async-start | bytes 65536 | tf_op jit(solution)/shard_map/all_to_all | solution.py:226
  103.7 3.0 %collective-permute-start.10 = (bf16[128,3584]{1,0:T(8,128)(2,1)S(1)}, bf16[128,3584]{1,0:T(8,128)(2,1)}, u32[]{:S(2)}, u32[]{:S(2)}) collective-permute-start(bf16[128,3584]{1,0:T(8,128)(2,1)S(1)} %reshape.57.refs_0_), channel_id=1, source_target_pairs={{0,1},{1,0},{2,3},{3,2},{4,5},{5,4},{6,7},{7,6},{8,9},{9,8},{10,11... | collective-permute-start | bytes 2752520 | tf_op jit(solution)/shard_map/ppermute | solution.py:48
  106.7 10.2 %all-to-all-done.1 = f32[64,1,2]{2,1,0:T(1,128)S(1)} async-done(((f32[64,1,2]{2,1,0:T(1,128)}), f32[64,1,2]{2,1,0:T(1,128)S(1)}, u32[]{:S(2)}, u32[]{:S(2)}) %all-to-all-start.1) | async-done | bytes 544 | tf_op jit(solution)/shard_map/all_to_all | solution.py:226
  117.0 2.2 %broadcast_select_fusion = bf16[128,3584]{1,0:T(8,128)(2,1)} fusion(bf16[128,3584]{1,0:T(8,128)(2,1)} %collective-permute-done.11.refs_2_, bf16[128,3584]{1,0:T(8,128)(2,1)} %collective-permute-done.12.refs_3_, pred[]{:T(512)S(6)} %eq.71), kind=kLoop, calls=%fused_computation.3 | loop fusion | flops 458752 | bytes 2752513 | tf_op jit(solution)/shard_map/jit(_where)/select_n | solution.py:56
  119.3 2.8 %collective-permute-start.15 = (bf16[128,3584]{1,0:T(8,128)(2,1)}, bf16[128,3584]{1,0:T(8,128)(2,1)}, u32[]{:S(2)}, u32[]{:S(2)}) collective-permute-start(bf16[128,3584]{1,0:T(8,128)(2,1)} %broadcast_select_fusion), channel_id=1, source_target_pairs={{0,2},{1,7},{2,4},{3,1},{4,6},{5,3},{6,0},{7,5},{8,10},{9,15},{10,... | collective-permute-start | bytes 2752520 | tf_op jit(solution)/shard_map/ppermute | solution.py:56
  122.3 3.8 %collective-permute-start.13 = (bf16[128,3584]{1,0:T(8,128)(2,1)}, bf16[128,3584]{1,0:T(8,128)(2,1)}, u32[]{:S(2)}, u32[]{:S(2)}) collective-permute-start(bf16[128,3584]{1,0:T(8,128)(2,1)} %collective-permute-done.11.refs_2_), channel_id=1, source_target_pairs={{0,1},{1,0},{2,3},{3,2},{4,5},{5,4},{6,7},{7,6},{8,9},{9,8},{10,11... | collective-permute-start | bytes 2752520 | tf_op jit(solution)/shard_map/ppermute | solution.py:57
  126.1 1.9 %collective-permute-start.14 = (bf16[128,3584]{1,0:T(8,128)(2,1)}, bf16[128,3584]{1,0:T(8,128)(2,1)}, u32[]{:S(2)}, u32[]{:S(2)}) collective-permute-start(bf16[128,3584]{1,0:T(8,128)(2,1)} %collective-permute-done.12.refs_3_), channel_id=1, source_target_pairs={{0,1},{1,0},{2,3},{3,2},{4,5},{5,4},{6,7},{7,6},{8,9},{9,8},{10,11... | collective-permute-start | bytes 2752520 | tf_op jit(solution)/shard_map/ppermute | solution.py:57
  128.3 0.6 broadcast_select_fusion.5
  129.0 3.5 %grads_first.1 = (f32[128,3584]{1,0:T(8,128)S(1)}, bf16[512,128]{1,0:T(8,128)(2,1)S(1)}) custom-call(s32[8]{0:T(128)S(1)} %stack.82.blocks_ref, bf16[128,3584]{1,0:T(8,128)(2,1)S(1)} %reshape.57.refs_0_, bf16[128,3584]{1,0:T(8,128)(2,1)} %collective-permute-done.10.refs_1_, bf16[128,3584]{1,0:T(8,128)(2,1)} %collective-permute-done.11.refs_2_, ...), custom_call_target="tpu_custom_call" | custom-call | flops 939524096 | bytes 9175040 | tf_op jit(solution)/shard_map/grads_first/pallas_call | solution.py:186
  132.5 1.5 %collective-permute-done.15.refs_2_ = bf16[128,3584]{1,0:T(8,128)(2,1)} collective-permute-done((bf16[128,3584]{1,0:T(8,128)(2,1)}, bf16[128,3584]{1,0:T(8,128)(2,1)}, u32[]{:S(2)}, u32[]{:S(2)}) %collective-permute-start.15) | collective-permute-done | bytes 917536 | tf_op jit(solution)/shard_map/ppermute | solution.py:56
  134.0 6.2 %collective-permute-start.16 = (bf16[128,3584]{1,0:T(8,128)(2,1)}, bf16[128,3584]{1,0:T(8,128)(2,1)S(1)}, u32[]{:S(2)}, u32[]{:S(2)}) collective-permute-start(bf16[128,3584]{1,0:T(8,128)(2,1)} %collective-permute-done.15.refs_2_), channel_id=1, source_target_pairs={{0,1},{1,0},{2,3},{3,2},{4,5},{5,4},{6,7},{7,6},{8,9},{9,8},{10,11... | collective-permute-start | bytes 2752520 | tf_op jit(solution)/shard_map/ppermute | solution.py:62
  140.2 2.3 %collective-permute-done.16.refs_3_ = bf16[128,3584]{1,0:T(8,128)(2,1)S(1)} collective-permute-done((bf16[128,3584]{1,0:T(8,128)(2,1)}, bf16[128,3584]{1,0:T(8,128)(2,1)S(1)}, u32[]{:S(2)}, u32[]{:S(2)}) %collective-permute-start.16) | collective-permute-done | bytes 917536 | tf_op jit(solution)/shard_map/ppermute | solution.py:62
  142.5 5.4 %grads_last.1 = (bf16[1024,128]{1,0:T(8,128)(2,1)}, bf16[128,3584]{1,0:T(8,128)(2,1)}, bf16[128,3584]{1,0:T(8,128)(2,1)}) custom-call(s32[8]{0:T(128)S(1)} %stack.82.blocks_ref, bf16[128,3584]{1,0:T(8,128)(2,1)} %collective-permute-done.13.refs_0_, bf16[128,3584]{1,0:T(8,128)(2,1)} %collective-permute-done.14.refs_1_, ...), custom_call_target="tpu_custom_call" | custom-call | flops 939524096 | bytes 9175040 | tf_op jit(solution)/shard_map/grads_last/pallas_call | solution.py:186
  (41 shorter events, 1.0 us)
Async XLA Ops:
  0.6 9.7 %copy-start = (bf16[128,3584]{1,0:T(8,128)(2,1)S(1)}, bf16[128,3584]{1,0:T(8,128)(2,1)}, u32[]{:S(2)}) copy-start(bf16[128,3584]{1,0:T(8,128)(2,1)} %param.6) | copy-start | bytes 2752516
  0.6 33.2 %collective-permute-start.1 = (bf16[128,3584]{1,0:T(8,128)(2,1)}, bf16[128,3584]{1,0:T(8,128)(2,1)S(1)}, u32[]{:S(2)}, u32[]{:S(2)}) collective-permute-start(bf16[128,3584]{1,0:T(8,128)(2,1)} %bitcast.35), channel_id=1, source_target_pairs={{0,2},{1,3},{2,4},{3,5},{4,6},{5,7},{6,0},{7,1},{8,10},{9,11},{10,... | collective-permute-start | bytes 2752520 | tf_op jit(solution)/shard_map/ppermute | solution.py:46
  4.7 29.1 %collective-permute-start.2 = (bf16[128,3584]{1,0:T(8,128)(2,1)}, bf16[128,3584]{1,0:T(8,128)(2,1)S(1)}, u32[]{:S(2)}, u32[]{:S(2)}) collective-permute-start(bf16[128,3584]{1,0:T(8,128)(2,1)} %bitcast.36), channel_id=1, source_target_pairs={{0,6},{1,7},{2,0},{3,1},{4,2},{5,3},{6,4},{7,5},{8,14},{9,15},{10,... | collective-permute-start | bytes 2752520 | tf_op jit(solution)/shard_map/ppermute | solution.py:47
  11.7 22.0 %copy-start.7 = (bf16[1,1024,128]{2,1,0:T(8,128)(2,1)S(1)}, bf16[1,1024,128]{2,1,0:T(8,128)(2,1)}, u32[]{:S(2)}) copy-start(bf16[1,1024,128]{2,1,0:T(8,128)(2,1)} %param.9) | copy-start | bytes 786436
  14.8 63.0 %all-to-all-start = ((bf16[64,2,3584]{2,1,0:T(2,128)(2,1)}), bf16[64,2,3584]{2,1,0:T(2,128)(2,1)}, u32[]{:S(2)}, u32[]{:S(2)}) async-start(bf16[64,2,3584]{2,1,0:T(2,128)(2,1)} %reshape.56), calls=%async_computation | async-start | bytes 1835008 | tf_op jit(solution)/shard_map/all_to_all | solution.py:211
  33.9 2.4 %copy-start.3 = (bf16[128,3584]{1,0:T(8,128)(2,1)}, bf16[128,3584]{1,0:T(8,128)(2,1)S(1)}, u32[]{:S(2)}) copy-start(bf16[128,3584]{1,0:T(8,128)(2,1)S(1)} %collective-permute-done.2.refs_3_) | copy-start | bytes 2752516
  37.0 5.5 %copy-start.6 = (bf16[2,2,1,128,128]{4,3,1,0,2:T(8,128)(2,1)S(1)}, bf16[2,2,1,128,128]{4,3,1,0,2:T(8,128)(2,1)}, u32[]{:S(2)}) copy-start(bf16[2,2,1,128,128]{4,3,1,0,2:T(8,128)(2,1)} %copy.61) | copy-start | bytes 393220
  37.0 23.3 %copy-start.1 = (bf16[1,128,3584]{2,1,0:T(8,128)(2,1)S(1)}, bf16[1,128,3584]{2,1,0:T(8,128)(2,1)}, u32[]{:S(2)}) copy-start(bf16[1,128,3584]{2,1,0:T(8,128)(2,1)} %param.10) | copy-start | bytes 2752516
  39.3 27.4 %collective-permute-start.5 = (bf16[128,3584]{1,0:T(8,128)(2,1)}, bf16[128,3584]{1,0:T(8,128)(2,1)}, u32[]{:S(2)}, u32[]{:S(2)}) collective-permute-start(bf16[128,3584]{1,0:T(8,128)(2,1)} %broadcast_select_fusion.1), channel_id=1, source_target_pairs={{0,2},{1,7},{2,4},{3,1},{4,6},{5,3},{6,0},{7,5},{8,10},{9,15},{10,... | collective-permute-start | bytes 2752520 | tf_op jit(solution)/shard_map/ppermute | solution.py:56
  42.6 3.2 %collective-permute-start.6 = (bf16[2,2,128,128]{3,2,1,0:T(8,128)(2,1)S(1)}, bf16[2,2,128,128]{3,2,1,0:T(8,128)(2,1)S(1)}, u32[]{:S(2)}, u32[]{:S(2)}) collective-permute-start(bf16[2,2,128,128]{3,2,1,0:T(8,128)(2,1)S(1)} %get-tuple-element.51), channel_id=1, source_target_pairs={{0,1},{1,0},{2,3},{3,2},{4,5},{5,4},{6,7},{7,6},{8,9},{9,8},{10,11... | collective-permute-start | bytes 393224 | tf_op jit(solution)/shard_map/ppermute | solution.py:115
  45.8 11.1 %collective-permute-start.7 = (bf16[2,2,128,128]{3,2,0,1:T(8,128)(2,1)S(1)}, bf16[2,2,128,128]{3,2,0,1:T(8,128)(2,1)S(1)}, u32[]{:S(2)}, u32[]{:S(2)}) collective-permute-start(bf16[2,2,128,128]{3,2,0,1:T(8,128)(2,1)S(1)} %get-tuple-element.49), channel_id=1, source_target_pairs={{0,2},{1,3},{2,0},{3,1},{4,6},{5,7},{6,4},{7,5},{8,10},{9,11},{10,... | collective-permute-start | bytes 393224 | tf_op jit(solution)/shard_map/ppermute | solution.py:115
  56.9 9.7 %collective-permute-start.8 = (bf16[2,2,128,128]{3,2,0,1:T(8,128)(2,1)S(1)}, bf16[2,2,128,128]{3,2,0,1:T(8,128)(2,1)S(1)}, u32[]{:S(2)}, u32[]{:S(2)}) collective-permute-start(bf16[2,2,128,128]{3,2,0,1:T(8,128)(2,1)S(1)} %get-tuple-element.47), channel_id=1, source_target_pairs={{0,4},{1,5},{2,6},{3,7},{4,0},{5,1},{6,2},{7,3},{8,12},{9,13},{10,... | collective-permute-start | bytes 393224 | tf_op jit(solution)/shard_map/ppermute | solution.py:115
  60.4 8.9 %collective-permute-start = (bf16[128,3584]{1,0:T(8,128)(2,1)S(1)}, bf16[128,3584]{1,0:T(8,128)(2,1)}, u32[]{:S(2)}, u32[]{:S(2)}) collective-permute-start(bf16[128,3584]{1,0:T(8,128)(2,1)S(1)} %bitcast.37), channel_id=1, source_target_pairs={{0,1},{1,0},{2,3},{3,2},{4,5},{5,4},{6,7},{7,6},{8,9},{9,8},{10,11... | collective-permute-start | bytes 2752520 | tf_op jit(solution)/shard_map/ppermute | solution.py:48
  62.3 6.9 %collective-permute-start.3 = (bf16[128,3584]{1,0:T(8,128)(2,1)S(1)}, bf16[128,3584]{1,0:T(8,128)(2,1)}, u32[]{:S(2)}, u32[]{:S(2)}) collective-permute-start(bf16[128,3584]{1,0:T(8,128)(2,1)S(1)} %collective-permute-done.1.refs_2_), channel_id=1, source_target_pairs={{0,1},{1,0},{2,3},{3,2},{4,5},{5,4},{6,7},{7,6},{8,9},{9,8},{10,11... | collective-permute-start | bytes 2752520 | tf_op jit(solution)/shard_map/ppermute | solution.py:57
  64.7 4.7 %collective-permute-start.4 = (bf16[128,3584]{1,0:T(8,128)(2,1)}, bf16[128,3584]{1,0:T(8,128)(2,1)}, u32[]{:S(2)}, u32[]{:S(2)}) collective-permute-start(bf16[128,3584]{1,0:T(8,128)(2,1)} %copy-done.3), channel_id=1, source_target_pairs={{0,1},{1,0},{2,3},{3,2},{4,5},{5,4},{6,7},{7,6},{8,9},{9,8},{10,11... | collective-permute-start | bytes 2752520 | tf_op jit(solution)/shard_map/ppermute | solution.py:57
  66.7 4.8 %collective-permute-start.9 = (bf16[128,3584]{1,0:T(8,128)(2,1)}, bf16[128,3584]{1,0:T(8,128)(2,1)}, u32[]{:S(2)}, u32[]{:S(2)}) collective-permute-start(bf16[128,3584]{1,0:T(8,128)(2,1)} %collective-permute-done.5.refs_6_), channel_id=1, source_target_pairs={{0,1},{1,0},{2,3},{3,2},{4,5},{5,4},{6,7},{7,6},{8,9},{9,8},{10,11... | collective-permute-start | bytes 2752520 | tf_op jit(solution)/shard_map/ppermute | solution.py:62
  71.6 1.2 copy-start.4
  76.3 1.3 copy-start.2
  80.3 36.7 %collective-permute-start.11 = (bf16[128,3584]{1,0:T(8,128)(2,1)S(1)}, bf16[128,3584]{1,0:T(8,128)(2,1)}, u32[]{:S(2)}, u32[]{:S(2)}) collective-permute-start(bf16[128,3584]{1,0:T(8,128)(2,1)S(1)} %reshape.57.refs_0_), channel_id=1, source_target_pairs={{0,2},{1,3},{2,4},{3,5},{4,6},{5,7},{6,0},{7,1},{8,10},{9,11},{10,... | collective-permute-start | bytes 2752520 | tf_op jit(solution)/shard_map/ppermute | solution.py:46
  83.4 33.6 %collective-permute-start.12 = (bf16[128,3584]{1,0:T(8,128)(2,1)S(1)}, bf16[128,3584]{1,0:T(8,128)(2,1)}, u32[]{:S(2)}, u32[]{:S(2)}) collective-permute-start(bf16[128,3584]{1,0:T(8,128)(2,1)S(1)} %reshape.57.refs_0_), channel_id=1, source_target_pairs={{0,6},{1,7},{2,0},{3,1},{4,2},{5,3},{6,4},{7,5},{8,14},{9,15},{10,... | collective-permute-start | bytes 2752520 | tf_op jit(solution)/shard_map/ppermute | solution.py:47
  89.3 27.6 %all-to-all-start.1 = ((f32[64,1,2]{2,1,0:T(1,128)}), f32[64,1,2]{2,1,0:T(1,128)S(1)}, u32[]{:S(2)}, u32[]{:S(2)}) async-start(f32[64,1,2]{2,1,0:T(1,128)} %bitcast.13), calls=%async_computation.1 | async-start | bytes 65536 | tf_op jit(solution)/shard_map/all_to_all | solution.py:226
  103.7 25.2 %collective-permute-start.10 = (bf16[128,3584]{1,0:T(8,128)(2,1)S(1)}, bf16[128,3584]{1,0:T(8,128)(2,1)}, u32[]{:S(2)}, u32[]{:S(2)}) collective-permute-start(bf16[128,3584]{1,0:T(8,128)(2,1)S(1)} %reshape.57.refs_0_), channel_id=1, source_target_pairs={{0,1},{1,0},{2,3},{3,2},{4,5},{5,4},{6,7},{7,6},{8,9},{9,8},{10,11... | collective-permute-start | bytes 2752520 | tf_op jit(solution)/shard_map/ppermute | solution.py:48
  119.3 14.7 %collective-permute-start.15 = (bf16[128,3584]{1,0:T(8,128)(2,1)}, bf16[128,3584]{1,0:T(8,128)(2,1)}, u32[]{:S(2)}, u32[]{:S(2)}) collective-permute-start(bf16[128,3584]{1,0:T(8,128)(2,1)} %broadcast_select_fusion), channel_id=1, source_target_pairs={{0,2},{1,7},{2,4},{3,1},{4,6},{5,3},{6,0},{7,5},{8,10},{9,15},{10,... | collective-permute-start | bytes 2752520 | tf_op jit(solution)/shard_map/ppermute | solution.py:56
  122.3 17.9 %collective-permute-start.13 = (bf16[128,3584]{1,0:T(8,128)(2,1)}, bf16[128,3584]{1,0:T(8,128)(2,1)}, u32[]{:S(2)}, u32[]{:S(2)}) collective-permute-start(bf16[128,3584]{1,0:T(8,128)(2,1)} %collective-permute-done.11.refs_2_), channel_id=1, source_target_pairs={{0,1},{1,0},{2,3},{3,2},{4,5},{5,4},{6,7},{7,6},{8,9},{9,8},{10,11... | collective-permute-start | bytes 2752520 | tf_op jit(solution)/shard_map/ppermute | solution.py:57
  126.1 14.1 %collective-permute-start.14 = (bf16[128,3584]{1,0:T(8,128)(2,1)}, bf16[128,3584]{1,0:T(8,128)(2,1)}, u32[]{:S(2)}, u32[]{:S(2)}) collective-permute-start(bf16[128,3584]{1,0:T(8,128)(2,1)} %collective-permute-done.12.refs_3_), channel_id=1, source_target_pairs={{0,1},{1,0},{2,3},{3,2},{4,5},{5,4},{6,7},{7,6},{8,9},{9,8},{10,11... | collective-permute-start | bytes 2752520 | tf_op jit(solution)/shard_map/ppermute | solution.py:57
  129.0 13.5 %copy-start.5 = (bf16[1,128,3584]{2,1,0:T(8,128)(2,1)S(1)}, bf16[1,128,3584]{2,1,0:T(8,128)(2,1)}, u32[]{:S(2)}) copy-start(bf16[1,128,3584]{2,1,0:T(8,128)(2,1)} %param.11) | copy-start | bytes 2752516
  134.0 8.5 %collective-permute-start.16 = (bf16[128,3584]{1,0:T(8,128)(2,1)}, bf16[128,3584]{1,0:T(8,128)(2,1)S(1)}, u32[]{:S(2)}, u32[]{:S(2)}) collective-permute-start(bf16[128,3584]{1,0:T(8,128)(2,1)} %collective-permute-done.15.refs_2_), channel_id=1, source_target_pairs={{0,1},{1,0},{2,3},{3,2},{4,5},{5,4},{6,7},{7,6},{8,9},{9,8},{10,11... | collective-permute-start | bytes 2752520 | tf_op jit(solution)/shard_map/ppermute | solution.py:62

commit v4 on v3

--- a/solution.py
+++ b/solution.py
@@ -38,23 +38,17 @@
     return expert_location, transit_rows, row_present, matched_gate.astype(jnp.float32)
 
 
-def gather_near(block):
+def gather_ways(block):
     members = lax.axis_size("local")
     up = [(i, (i + 2) % members) for i in range(members)]
     down = [(i, (i - 2) % members) for i in range(members)]
-    swap = [(i, i ^ 1) for i in range(members)]
-    low = lax.ppermute(block, "local", up)
-    high = lax.ppermute(block, "local", down)
-    other = lax.ppermute(block, "local", swap)
-    return block, other, low, high
-
-
-def gather_more(low, high, core):
+    return lax.ppermute(block, "local", up), lax.ppermute(block, "local", down)
+
+
+def go_on(low, high, core):
     members = lax.axis_size("local")
     onward = [(i, (i + (2 if i % 2 == 0 else -2)) % members) for i in range(members)]
-    swap = [(i, i ^ 1) for i in range(members)]
-    far = lax.ppermute(jnp.where(core == 0, low, high), "local", onward)
-    return lax.ppermute(low, "local", swap), lax.ppermute(high, "local", swap), far
+    return lax.ppermute(jnp.where(core == 0, low, high), "local", onward)
 
 
 def hand_over(piece):
@@ -73,7 +67,7 @@
 
 
 def back_kernel(partners_ref, *refs):
-    pieces, hidden_ref, out_ref = refs[:8], refs[8], refs[9]
+    pieces, (hidden_ref, out_ref) = refs[:-2], refs[-2:]
     left = jnp.concatenate([hidden_ref[block_at(partners_ref[k]), :] for k in range(8)], 1)
 
     @pl.loop(0, out_ref.shape[1] // TILE, unroll=True)
@@ -91,7 +85,7 @@
     width = pieces[0].shape[1]
     return pl.pallas_call(
         back_kernel,
-        in_specs=[IN_SMEM] + [IN_VMEM] * 9,
+        in_specs=[IN_SMEM] + [IN_VMEM] * (len(pieces) + 1),
         out_specs=IN_VMEM,
         out_shape=jax.ShapeDtypeStruct((pieces[0].shape[0], width), jnp.float32),
         compiler_params=pltpu.CompilerParams(vmem_limit_bytes=VMEM_BYTES),
@@ -121,7 +115,7 @@
     even = 1 - (me // 2) % 2
     below = 2 + 4 * even
     above = 6 - 4 * even
-    return jnp.stack([0 * me, 0 * me + 1, below, above, below + 1, above + 1, 0 * me + 4, 0 * me + 5])
+    return jnp.stack([0 * me, below, above, 0 * me + 1, below + 1, above + 1, 0 * me + 4, 0 * me + 5])
 
 
 def grad_kernel(count, start, final, blocks_ref, *refs):
@@ -208,27 +202,29 @@
     scaled_out = (slot_gate[:, None] * picked).astype(jnp.bfloat16)
     blocks = piece_blocks(me, members)
     leaving = scaled_out.reshape(node_count, CAP, feature_count)
+    weight_now, leaving = lax.optimization_barrier((down_weight[0], leaving))
     scaled = lax.all_to_all(leaving, "node", split_axis=0, concat_axis=0, tiled=True).reshape(
         node_count * CAP, feature_count
     )
     core = me % 2
-    weight_now = down_weight[0]
     hidden_now = saved_hidden[0]
     hidden_t = hidden_now.T
-    near = gather_near(weight_now)
-    low, high, hidden_later = lax.optimization_barrier((near[2], near[3], hidden_now))
-    more = gather_more(low, high, core)
+    low, high = gather_ways(weight_now)
+    low, high, hidden_later = lax.optimization_barrier((low, high, hidden_now))
+    far = go_on(low, high, core)
+    mates = hand_over(jnp.concatenate([weight_now, low, high], 0))
     hidden_own = own_slots(hidden_later, me)
-    far, hidden_own = lax.optimization_barrier((more[2], hidden_own))
-    y = back_projection(piece_partners(me), near + more[:2] + (far, hand_over(far)), hidden_own)
+    far, hidden_own = lax.optimization_barrier((far, hidden_own))
+    y = back_projection(piece_partners(me), (weight_now, low, high, mates, far, hand_over(far)), hidden_own)
     scaled, y = lax.optimization_barrier((scaled, y))
     own_score = jnp.sum(scaled.astype(jnp.float32) * y, 1)
     returned = lax.all_to_all(
         own_score.reshape(node_count, CAP), "node", split_axis=0, concat_axis=0, tiled=True
     )
-    near = gather_near(scaled)
-    low, high, returned = lax.optimization_barrier((near[2], near[3], returned))
-    more = gather_more(low, high, core)
+    low, high = gather_ways(scaled)
+    near = (scaled, hand_over(scaled), low, high)
+    low, high, returned = lax.optimization_barrier((low, high, returned))
+    more = (hand_over(low), hand_over(high), go_on(low, high, core))
     early = len(near)
     returned_flat = returned.reshape(node_count * CAP)
     token_score = jnp.sum(jnp.where(expert_location, returned_flat[:, None], 0.0), 0)

time: 149 us -> 147 us (0.987)
  waiting for transfers between devices: 26.8 us -> 31.3 us
  local copies, waits for them, and re-layouts: 12.6 us -> 8.39 us
  starting transfers between devices: 84 us -> 80.3 us
  other arithmetic: 9.5 us -> 12.2 us
    ppermute x12 -> x6, starting transfers between devices: 34.7 us -> 20.2 us  [the longest x2 7.76 us: gather_ways(): lax.ppermute(block, 'local', down)]
    ppermute x2 -> x6, starting transfers between devices: 8.57 us -> 19.7 us  [hand_over(): return lax.ppermute(piece, 'local', [(i, i ^ 1) for i in range(members)])]
    all_to_all x1, waiting for transfers between devices: 0.23 us -> 5.8 us  [on_device(): lax.all_to_all(leaving, 'node', split_axis=0, concat_axis=0, tiled=True)]
    unnamed x19 -> x11, local copies, waits for them, and re-layouts: 4.52 us -> 1.43 us
    concatenate x0 -> x1, other arithmetic: none -> 2.96 us  [on_device(): mates = hand_over(jnp.concatenate([weight_now, low, high], 0))]
    ppermute x2 -> x6, waiting for transfers between devices: 4.4 us -> 2.28 us  [hand_over(): return lax.ppermute(piece, 'local', [(i, i ^ 1) for i in range(members)])]
    ppermute x12 -> x6, waiting for transfers between devices: 1.73 us -> 3.59 us  [the longest x2 3.58 us: go_on(): return lax.ppermute(jnp.where(core == 0, low, high), 'local', onward)]
    reshape x1, local copies, waits for them, and re-layouts: 3.1 us -> 1.27 us  [on_device(): leaving = scaled_out.reshape(node_count, CAP, feature_count)]
  transfers between devices with their start and end apart: 19 -> 17, of which waited for: 8 -> 7; matrix products, arithmetic and copies ran while one was open for 12% -> 11% of each run, Pallas kernels for 5% -> 2%
where the time goes in v4:
time: 147 us; the launch traced here: 146 us
  starting transfers between devices  80.3 us (55%)
  waiting for transfers between devices  31.3 us (21%)
  Pallas kernels  12.7 us (9%)
  other arithmetic  12.2 us (8%)
  local copies, waits for them, and re-layouts  8.39 us (6%)
    ppermute x6, starting transfers between devices, hand_over(): return lax.ppermute(piece, 'local', [(i, i ^ 1) for i in range(members)])  19.7 us
    all_to_all x1, starting transfers between devices, on_device(): lax.all_to_all(leaving, 'node', split_axis=0, concat_axis=0, tiled=True)  18.9 us
    all_to_all x1, starting transfers between devices, on_device(): lax.all_to_all(own_score.reshape(node_count, CAP), 'node', split_axis=0,...  12.9 us
    all_to_all x1, waiting for transfers between devices, on_device(): lax.all_to_all(own_score.reshape(node_count, CAP), 'node', split_axis=0,...  10.4 us
    ppermute x3, waiting for transfers between devices, own_slots(): got = lax.ppermute(give, 'local', [(i, i ^ bit) for i in range(members)])  9.23 us
    pallas_call x2, Pallas kernels, grads(): pl.pallas_call(functools.partial(grad_kernel, count, start, final), in_sp...  8.86 us
    ppermute x3, starting transfers between devices, own_slots(): got = lax.ppermute(give, 'local', [(i, i ^ bit) for i in range(members)])  8.6 us
    ppermute x2, starting transfers between devices, gather_ways(): lax.ppermute(block, 'local', down)  7.76 us
  transfers between devices with their start and end apart: 17, of which 7 were waited for; matrix products, arithmetic and copies ran while one was open for 11% of the time, Pallas kernels for 2%

profile of v4, /device:TPU:1, one launch (start us, length us, event | category | flops | bytes accessed | tf_op | source)
XLA Modules:
  0.0 146.5 jit_solution(15617374786232160475)
XLA Ops:
  0.7 0.8 fusion.13
  1.5 0.7 fusion.10
  2.2 0.7 select_reduce_fusion.2
  2.9 0.2 convert_reduce_fusion
  3.1 0.1 select_reduce_fusion.1
  3.2 0.4 fusion
  3.6 1.3 reshape.56
  4.9 3.9 %collective-permute-start = (bf16[128,3584]{1,0:T(8,128)(2,1)S(1)}, bf16[128,3584]{1,0:T(8,128)(2,1)S(1)}, u32[]{:S(2)}, u32[]{:S(2)}) collective-permute-start(bf16[128,3584]{1,0:T(8,128)(2,1)S(1)} %bitcast.35), channel_id=1, source_target_pairs={{0,2},{1,3},{2,4},{3,5},{4,6},{5,7},{6,0},{7,1},{8,10},{9,11},{10,... | collective-permute-start | bytes 2752520 | tf_op jit(solution)/shard_map/ppermute | solution.py:45
  8.9 3.2 %collective-permute-start.1 = (bf16[128,3584]{1,0:T(8,128)(2,1)S(1)}, bf16[128,3584]{1,0:T(8,128)(2,1)}, u32[]{:S(2)}, u32[]{:S(2)}) collective-permute-start(bf16[128,3584]{1,0:T(8,128)(2,1)S(1)} %bitcast.36), channel_id=1, source_target_pairs={{0,6},{1,7},{2,0},{3,1},{4,2},{5,3},{6,4},{7,5},{8,14},{9,15},{10,... | collective-permute-start | bytes 2752520 | tf_op jit(solution)/shard_map/ppermute | solution.py:45
  12.1 18.9 %all-to-all-start = ((bf16[64,2,3584]{2,1,0:T(2,128)(2,1)}), bf16[64,2,3584]{2,1,0:T(2,128)(2,1)}, u32[]{:S(2)}, u32[]{:S(2)}) async-start(bf16[64,2,3584]{2,1,0:T(2,128)(2,1)} %reshape.56), calls=%async_computation | async-start | bytes 1835008 | tf_op jit(solution)/shard_map/all_to_all | solution.py:206
  31.0 0.1 copy.47
  31.2 3.0 %pad_maximum_fusion = bf16[384,3584]{1,0:T(8,128)(2,1)} fusion(bf16[128,3584]{1,0:T(8,128)(2,1)} %collective-permute-done.1.refs_2_, bf16[128,3584]{1,0:T(8,128)(2,1)S(1)} %collective-permute-done.refs_1_, bf16[128,3584]{1,0:T(8,128)(2,1)S(1)} %bitcast.37), kind=kLoop, calls=%fused_computation.2 | loop fusion | flops 8257536 | bytes 5505024 | tf_op jit(solution)/shard_map/concatenate | solution.py:215
  34.1 4.4 %collective-permute-start.2 = (bf16[384,3584]{1,0:T(8,128)(2,1)}, bf16[384,3584]{1,0:T(8,128)(2,1)}, u32[]{:S(2)}, u32[]{:S(2)}) collective-permute-start(bf16[384,3584]{1,0:T(8,128)(2,1)} %pad_maximum_fusion), channel_id=1, source_target_pairs={{0,1},{1,0},{2,3},{3,2},{4,5},{5,4},{6,7},{7,6},{8,9},{9,8},{10,11... | collective-permute-start | bytes 8257544 | tf_op jit(solution)/shard_map/ppermute | solution.py:56
  38.5 2.2 %broadcast_select_fusion.1 = bf16[128,3584]{1,0:T(8,128)(2,1)} fusion(bf16[128,3584]{1,0:T(8,128)(2,1)S(1)} %collective-permute-done.refs_1_, bf16[128,3584]{1,0:T(8,128)(2,1)} %collective-permute-done.1.refs_2_, pred[]{:T(512)S(6)} %eq.71), kind=kLoop, calls=%fused_computation.5 | loop fusion | flops 458752 | bytes 2752513 | tf_op jit(solution)/shard_map/jit(_where)/select_n | solution.py:51
  40.7 4.4 %collective-permute-start.3 = (bf16[128,3584]{1,0:T(8,128)(2,1)}, bf16[128,3584]{1,0:T(8,128)(2,1)}, u32[]{:S(2)}, u32[]{:S(2)}) collective-permute-start(bf16[128,3584]{1,0:T(8,128)(2,1)} %broadcast_select_fusion.1), channel_id=1, source_target_pairs={{0,2},{1,7},{2,4},{3,1},{4,6},{5,3},{6,0},{7,5},{8,10},{9,15},{10,... | collective-permute-start | bytes 2752520 | tf_op jit(solution)/shard_map/ppermute | solution.py:51
  45.1 0.2 reshape.58
  45.3 1.1 fusion.15
  46.3 1.1 copy.60
  47.4 0.2 copy.61
  47.6 1.9 %collective-permute-start.4 = (bf16[2,2,128,128]{3,2,1,0:T(8,128)(2,1)S(1)}, bf16[2,2,128,128]{3,2,1,0:T(8,128)(2,1)S(1)}, u32[]{:S(2)}, u32[]{:S(2)}) collective-permute-start(bf16[2,2,128,128]{3,2,1,0:T(8,128)(2,1)S(1)} %get-tuple-element.55), channel_id=1, source_target_pairs={{0,1},{1,0},{2,3},{3,2},{4,5},{5,4},{6,7},{7,6},{8,9},{9,8},{10,11... | collective-permute-start | bytes 393224 | tf_op jit(solution)/shard_map/ppermute | solution.py:109
  49.6 1.3 collective-permute-done.4
  50.9 1.9 %collective-permute-start.5 = (bf16[2,2,128,128]{3,2,0,1:T(8,128)(2,1)S(1)}, bf16[2,2,128,128]{3,2,0,1:T(8,128)(2,1)S(1)}, u32[]{:S(2)}, u32[]{:S(2)}) collective-permute-start(bf16[2,2,128,128]{3,2,0,1:T(8,128)(2,1)S(1)} %get-tuple-element.53), channel_id=1, source_target_pairs={{0,2},{1,3},{2,0},{3,1},{4,6},{5,7},{6,4},{7,5},{8,10},{9,11},{10,... | collective-permute-start | bytes 393224 | tf_op jit(solution)/shard_map/ppermute | solution.py:109
  52.9 5.0 %collective-permute-done.5 = bf16[2,2,128,128]{3,2,0,1:T(8,128)(2,1)S(1)} collective-permute-done((bf16[2,2,128,128]{3,2,0,1:T(8,128)(2,1)S(1)}, bf16[2,2,128,128]{3,2,0,1:T(8,128)(2,1)S(1)}, u32[]{:S(2)}, u32[]{:S(2)}) %collective-permute-start.5) | collective-permute-done | bytes 131104 | tf_op jit(solution)/shard_map/ppermute | solution.py:109
  57.9 4.8 %collective-permute-start.6 = (bf16[2,2,128,128]{3,2,0,1:T(8,128)(2,1)S(1)}, bf16[2,2,128,128]{3,2,0,1:T(8,128)(2,1)S(1)}, u32[]{:S(2)}, u32[]{:S(2)}) collective-permute-start(bf16[2,2,128,128]{3,2,0,1:T(8,128)(2,1)S(1)} %get-tuple-element.51), channel_id=1, source_target_pairs={{0,4},{1,5},{2,6},{3,7},{4,0},{5,1},{6,2},{7,3},{8,12},{9,13},{10,... | collective-permute-start | bytes 393224 | tf_op jit(solution)/shard_map/ppermute | solution.py:109
  62.6 3.0 %collective-permute-done.6 = bf16[2,2,128,128]{3,2,0,1:T(8,128)(2,1)S(1)} collective-permute-done((bf16[2,2,128,128]{3,2,0,1:T(8,128)(2,1)S(1)}, bf16[2,2,128,128]{3,2,0,1:T(8,128)(2,1)S(1)}, u32[]{:S(2)}, u32[]{:S(2)}) %collective-permute-start.6) | collective-permute-done | bytes 131104 | tf_op jit(solution)/shard_map/ppermute | solution.py:109
  65.7 3.5 %collective-permute-start.7 = (bf16[128,3584]{1,0:T(8,128)(2,1)}, bf16[128,3584]{1,0:T(8,128)(2,1)}, u32[]{:S(2)}, u32[]{:S(2)}) collective-permute-start(bf16[128,3584]{1,0:T(8,128)(2,1)} %collective-permute-done.3.refs_4_), channel_id=1, source_target_pairs={{0,1},{1,0},{2,3},{3,2},{4,5},{5,4},{6,7},{7,6},{8,9},{9,8},{10,11... | collective-permute-start | bytes 2752520 | tf_op jit(solution)/shard_map/ppermute | solution.py:56
  69.3 5.8 %all-to-all-done = bf16[64,2,3584]{2,1,0:T(2,128)(2,1)} async-done(((bf16[64,2,3584]{2,1,0:T(2,128)(2,1)}), bf16[64,2,3584]{2,1,0:T(2,128)(2,1)}, u32[]{:S(2)}, u32[]{:S(2)}) %all-to-all-start) | async-done | bytes 917536 | tf_op jit(solution)/shard_map/all_to_all | solution.py:206
  75.1 3.2 %reshape.57.refs_0_ = bf16[128,3584]{1,0:T(8,128)(2,1)} reshape(bf16[64,2,3584]{2,1,0:T(2,128)(2,1)} %all-to-all-done) | data formatting | bytes 1835008 | tf_op jit(solution)/shard_map/reshape | solution.py:206
  78.3 3.8 %back_projection.1 = f32[128,3584]{1,0:T(8,128)S(1)} custom-call(s32[8]{0:T(128)S(1)} %stack.67.partners_ref, bf16[128,3584]{1,0:T(8,128)(2,1)S(1)} %bitcast.38, bf16[128,3584]{1,0:T(8,128)(2,1)S(1)} %collective-permute-done.refs_1_, bf16[128,3584]{1,0:T(8,128)(2,1)} %collective-permute-done.1.refs_2_, bf16[384,3584]{1,0:T(8,128)(2,1)} %collective-permute-done.2.refs_3_, ...), custom_call_target="tpu_custom_call" | custom-call | flops 939524096 | bytes 9175040 | tf_op jit(solution)/shard_map/back_projection/pallas_call | solution.py:86
  82.1 1.9 %collective-permute-start.9 = (bf16[128,3584]{1,0:T(8,128)(2,1)}, bf16[128,3584]{1,0:T(8,128)(2,1)S(1)}, u32[]{:S(2)}, u32[]{:S(2)}) collective-permute-start(bf16[128,3584]{1,0:T(8,128)(2,1)} %reshape.57.refs_0_), channel_id=1, source_target_pairs={{0,2},{1,3},{2,4},{3,5},{4,6},{5,7},{6,0},{7,1},{8,10},{9,11},{10,... | collective-permute-start | bytes 2752520 | tf_op jit(solution)/shard_map/ppermute | solution.py:45
  84.0 4.6 %collective-permute-start.10 = (bf16[128,3584]{1,0:T(8,128)(2,1)}, bf16[128,3584]{1,0:T(8,128)(2,1)}, u32[]{:S(2)}, u32[]{:S(2)}) collective-permute-start(bf16[128,3584]{1,0:T(8,128)(2,1)} %reshape.57.refs_0_), channel_id=1, source_target_pairs={{0,6},{1,7},{2,0},{3,1},{4,2},{5,3},{6,4},{7,5},{8,14},{9,15},{10,... | collective-permute-start | bytes 2752520 | tf_op jit(solution)/shard_map/ppermute | solution.py:45
  88.6 1.5 %multiply_reduce_fusion = f32[128]{0:T(128)S(1)} fusion(f32[128,3584]{1,0:T(8,128)S(1)} %back_projection.1, bf16[128,3584]{1,0:T(8,128)(2,1)} %reshape.57.refs_0_), kind=kLoop, calls=%fused_computation.3 | loop fusion | flops 1376128 | bytes 2753024 | tf_op jit(solution)/shard_map/reduce_sum | solution.py:220
  90.1 0.8 all_to_all.12
  90.9 12.9 %all-to-all-start.1 = ((f32[64,1,2]{2,1,0:T(1,128)}), f32[64,1,2]{2,1,0:T(1,128)S(1)}, u32[]{:S(2)}, u32[]{:S(2)}) async-start(f32[64,1,2]{2,1,0:T(1,128)} %bitcast.13), calls=%async_computation.1 | async-start | bytes 65536 | tf_op jit(solution)/shard_map/all_to_all | solution.py:221
  103.7 2.8 %collective-permute-start.8 = (bf16[128,3584]{1,0:T(8,128)(2,1)}, bf16[128,3584]{1,0:T(8,128)(2,1)}, u32[]{:S(2)}, u32[]{:S(2)}) collective-permute-start(bf16[128,3584]{1,0:T(8,128)(2,1)} %reshape.57.refs_0_), channel_id=1, source_target_pairs={{0,1},{1,0},{2,3},{3,2},{4,5},{5,4},{6,7},{7,6},{8,9},{9,8},{10,11... | collective-permute-start | bytes 2752520 | tf_op jit(solution)/shard_map/ppermute | solution.py:56
  106.5 10.4 %all-to-all-done.1 = f32[64,1,2]{2,1,0:T(1,128)S(1)} async-done(((f32[64,1,2]{2,1,0:T(1,128)}), f32[64,1,2]{2,1,0:T(1,128)S(1)}, u32[]{:S(2)}, u32[]{:S(2)}) %all-to-all-start.1) | async-done | bytes 544 | tf_op jit(solution)/shard_map/all_to_all | solution.py:221
  117.0 2.2 %broadcast_select_fusion = bf16[128,3584]{1,0:T(8,128)(2,1)} fusion(bf16[128,3584]{1,0:T(8,128)(2,1)S(1)} %collective-permute-done.9.refs_2_, bf16[128,3584]{1,0:T(8,128)(2,1)} %collective-permute-done.10.refs_3_, pred[]{:T(512)S(6)} %eq.71), kind=kLoop, calls=%fused_computation.4 | loop fusion | flops 458752 | bytes 2752513 | tf_op jit(solution)/shard_map/jit(_where)/select_n | solution.py:51
  119.2 2.2 %collective-permute-start.13 = (bf16[128,3584]{1,0:T(8,128)(2,1)}, bf16[128,3584]{1,0:T(8,128)(2,1)}, u32[]{:S(2)}, u32[]{:S(2)}) collective-permute-start(bf16[128,3584]{1,0:T(8,128)(2,1)} %broadcast_select_fusion), channel_id=1, source_target_pairs={{0,2},{1,7},{2,4},{3,1},{4,6},{5,3},{6,0},{7,5},{8,10},{9,15},{10,... | collective-permute-start | bytes 2752520 | tf_op jit(solution)/shard_map/ppermute | solution.py:51
  121.7 2.4 %collective-permute-start.11 = (bf16[128,3584]{1,0:T(8,128)(2,1)S(1)}, bf16[128,3584]{1,0:T(8,128)(2,1)}, u32[]{:S(2)}, u32[]{:S(2)}) collective-permute-start(bf16[128,3584]{1,0:T(8,128)(2,1)S(1)} %collective-permute-done.9.refs_2_), channel_id=1, source_target_pairs={{0,1},{1,0},{2,3},{3,2},{4,5},{5,4},{6,7},{7,6},{8,9},{9,8},{10,11... | collective-permute-start | bytes 2752520 | tf_op jit(solution)/shard_map/ppermute | solution.py:56
  124.1 1.9 %collective-permute-start.12 = (bf16[128,3584]{1,0:T(8,128)(2,1)}, bf16[128,3584]{1,0:T(8,128)(2,1)}, u32[]{:S(2)}, u32[]{:S(2)}) collective-permute-start(bf16[128,3584]{1,0:T(8,128)(2,1)} %collective-permute-done.10.refs_3_), channel_id=1, source_target_pairs={{0,1},{1,0},{2,3},{3,2},{4,5},{5,4},{6,7},{7,6},{8,9},{9,8},{10,11... | collective-permute-start | bytes 2752520 | tf_op jit(solution)/shard_map/ppermute | solution.py:56
  126.1 0.1 broadcast_in_dim.70
  126.3 0.1 select_reduce_fusion
  126.4 0.6 broadcast_select_fusion.5
  127.0 3.4 %grads_first.1 = (f32[128,3584]{1,0:T(8,128)S(1)}, bf16[512,128]{1,0:T(8,128)(2,1)S(1)}) custom-call(s32[8]{0:T(128)S(1)} %stack.82.blocks_ref, bf16[128,3584]{1,0:T(8,128)(2,1)} %reshape.57.refs_0_, bf16[128,3584]{1,0:T(8,128)(2,1)} %collective-permute-done.8.refs_1_, bf16[128,3584]{1,0:T(8,128)(2,1)S(1)} %collective-permute-done.9.refs_2_, ...), custom_call_target="tpu_custom_call" | custom-call | flops 939524096 | bytes 9175040 | tf_op jit(solution)/shard_map/grads_first/pallas_call | solution.py:180
  130.4 3.6 %collective-permute-done.13.refs_2_ = bf16[128,3584]{1,0:T(8,128)(2,1)} collective-permute-done((bf16[128,3584]{1,0:T(8,128)(2,1)}, bf16[128,3584]{1,0:T(8,128)(2,1)}, u32[]{:S(2)}, u32[]{:S(2)}) %collective-permute-start.13) | collective-permute-done | bytes 917536 | tf_op jit(solution)/shard_map/ppermute | solution.py:51
  134.0 4.8 %collective-permute-start.14 = (bf16[128,3584]{1,0:T(8,128)(2,1)}, bf16[128,3584]{1,0:T(8,128)(2,1)S(1)}, u32[]{:S(2)}, u32[]{:S(2)}) collective-permute-start(bf16[128,3584]{1,0:T(8,128)(2,1)} %collective-permute-done.13.refs_2_), channel_id=1, source_target_pairs={{0,1},{1,0},{2,3},{3,2},{4,5},{5,4},{6,7},{7,6},{8,9},{9,8},{10,11... | collective-permute-start | bytes 2752520 | tf_op jit(solution)/shard_map/ppermute | solution.py:56
  138.8 2.3 %collective-permute-done.14.refs_3_ = bf16[128,3584]{1,0:T(8,128)(2,1)S(1)} collective-permute-done((bf16[128,3584]{1,0:T(8,128)(2,1)}, bf16[128,3584]{1,0:T(8,128)(2,1)S(1)}, u32[]{:S(2)}, u32[]{:S(2)}) %collective-permute-start.14) | collective-permute-done | bytes 917536 | tf_op jit(solution)/shard_map/ppermute | solution.py:56
  141.0 5.4 %grads_last.1 = (bf16[1024,128]{1,0:T(8,128)(2,1)}, bf16[128,3584]{1,0:T(8,128)(2,1)}, bf16[128,3584]{1,0:T(8,128)(2,1)}) custom-call(s32[8]{0:T(128)S(1)} %stack.82.blocks_ref, bf16[128,3584]{1,0:T(8,128)(2,1)} %collective-permute-done.11.refs_0_, bf16[128,3584]{1,0:T(8,128)(2,1)} %collective-permute-done.12.refs_1_, ...), custom_call_target="tpu_custom_call" | custom-call | flops 939524096 | bytes 9175040 | tf_op jit(solution)/shard_map/grads_last/pallas_call | solution.py:180
  (30 shorter events, 0.5 us)
Async XLA Ops:
  0.6 2.6 %copy-start = (bf16[128,3584]{1,0:T(8,128)(2,1)S(1)}, bf16[128,3584]{1,0:T(8,128)(2,1)}, u32[]{:S(2)}) copy-start(bf16[128,3584]{1,0:T(8,128)(2,1)} %param.6) | copy-start | bytes 2752516
  0.6 4.3 %copy-start.1 = (bf16[1,128,3584]{2,1,0:T(8,128)(2,1)S(1)}, bf16[1,128,3584]{2,1,0:T(8,128)(2,1)}, u32[]{:S(2)}) copy-start(bf16[1,128,3584]{2,1,0:T(8,128)(2,1)} %param.10) | copy-start | bytes 2752516
  3.2 27.7 %copy-start.3 = (bf16[1,1024,128]{2,1,0:T(8,128)(2,1)S(1)}, bf16[1,1024,128]{2,1,0:T(8,128)(2,1)}, u32[]{:S(2)}) copy-start(bf16[1,1024,128]{2,1,0:T(8,128)(2,1)} %param.9) | copy-start | bytes 786436
  4.9 26.2 %collective-permute-start = (bf16[128,3584]{1,0:T(8,128)(2,1)S(1)}, bf16[128,3584]{1,0:T(8,128)(2,1)S(1)}, u32[]{:S(2)}, u32[]{:S(2)}) collective-permute-start(bf16[128,3584]{1,0:T(8,128)(2,1)S(1)} %bitcast.35), channel_id=1, source_target_pairs={{0,2},{1,3},{2,4},{3,5},{4,6},{5,7},{6,0},{7,1},{8,10},{9,11},{10,... | collective-permute-start | bytes 2752520 | tf_op jit(solution)/shard_map/ppermute | solution.py:45
  8.9 22.3 %collective-permute-start.1 = (bf16[128,3584]{1,0:T(8,128)(2,1)S(1)}, bf16[128,3584]{1,0:T(8,128)(2,1)}, u32[]{:S(2)}, u32[]{:S(2)}) collective-permute-start(bf16[128,3584]{1,0:T(8,128)(2,1)S(1)} %bitcast.36), channel_id=1, source_target_pairs={{0,6},{1,7},{2,0},{3,1},{4,2},{5,3},{6,4},{7,5},{8,14},{9,15},{10,... | collective-permute-start | bytes 2752520 | tf_op jit(solution)/shard_map/ppermute | solution.py:45
  12.1 63.0 %all-to-all-start = ((bf16[64,2,3584]{2,1,0:T(2,128)(2,1)}), bf16[64,2,3584]{2,1,0:T(2,128)(2,1)}, u32[]{:S(2)}, u32[]{:S(2)}) async-start(bf16[64,2,3584]{2,1,0:T(2,128)(2,1)} %reshape.56), calls=%async_computation | async-start | bytes 1835008 | tf_op jit(solution)/shard_map/all_to_all | solution.py:206
  34.1 44.2 %collective-permute-start.2 = (bf16[384,3584]{1,0:T(8,128)(2,1)}, bf16[384,3584]{1,0:T(8,128)(2,1)}, u32[]{:S(2)}, u32[]{:S(2)}) collective-permute-start(bf16[384,3584]{1,0:T(8,128)(2,1)} %pad_maximum_fusion), channel_id=1, source_target_pairs={{0,1},{1,0},{2,3},{3,2},{4,5},{5,4},{6,7},{7,6},{8,9},{9,8},{10,11... | collective-permute-start | bytes 8257544 | tf_op jit(solution)/shard_map/ppermute | solution.py:56
  40.7 25.0 %collective-permute-start.3 = (bf16[128,3584]{1,0:T(8,128)(2,1)}, bf16[128,3584]{1,0:T(8,128)(2,1)}, u32[]{:S(2)}, u32[]{:S(2)}) collective-permute-start(bf16[128,3584]{1,0:T(8,128)(2,1)} %broadcast_select_fusion.1), channel_id=1, source_target_pairs={{0,2},{1,7},{2,4},{3,1},{4,6},{5,3},{6,0},{7,5},{8,10},{9,15},{10,... | collective-permute-start | bytes 2752520 | tf_op jit(solution)/shard_map/ppermute | solution.py:51
  47.6 3.2 %collective-permute-start.4 = (bf16[2,2,128,128]{3,2,1,0:T(8,128)(2,1)S(1)}, bf16[2,2,128,128]{3,2,1,0:T(8,128)(2,1)S(1)}, u32[]{:S(2)}, u32[]{:S(2)}) collective-permute-start(bf16[2,2,128,128]{3,2,1,0:T(8,128)(2,1)S(1)} %get-tuple-element.55), channel_id=1, source_target_pairs={{0,1},{1,0},{2,3},{3,2},{4,5},{5,4},{6,7},{7,6},{8,9},{9,8},{10,11... | collective-permute-start | bytes 393224 | tf_op jit(solution)/shard_map/ppermute | solution.py:109
  50.9 6.9 %collective-permute-start.5 = (bf16[2,2,128,128]{3,2,0,1:T(8,128)(2,1)S(1)}, bf16[2,2,128,128]{3,2,0,1:T(8,128)(2,1)S(1)}, u32[]{:S(2)}, u32[]{:S(2)}) collective-permute-start(bf16[2,2,128,128]{3,2,0,1:T(8,128)(2,1)S(1)} %get-tuple-element.53), channel_id=1, source_target_pairs={{0,2},{1,3},{2,0},{3,1},{4,6},{5,7},{6,4},{7,5},{8,10},{9,11},{10,... | collective-permute-start | bytes 393224 | tf_op jit(solution)/shard_map/ppermute | solution.py:109
  57.9 7.7 %collective-permute-start.6 = (bf16[2,2,128,128]{3,2,0,1:T(8,128)(2,1)S(1)}, bf16[2,2,128,128]{3,2,0,1:T(8,128)(2,1)S(1)}, u32[]{:S(2)}, u32[]{:S(2)}) collective-permute-start(bf16[2,2,128,128]{3,2,0,1:T(8,128)(2,1)S(1)} %get-tuple-element.51), channel_id=1, source_target_pairs={{0,4},{1,5},{2,6},{3,7},{4,0},{5,1},{6,2},{7,3},{8,12},{9,13},{10,... | collective-permute-start | bytes 393224 | tf_op jit(solution)/shard_map/ppermute | solution.py:109
  65.7 12.6 %collective-permute-start.7 = (bf16[128,3584]{1,0:T(8,128)(2,1)}, bf16[128,3584]{1,0:T(8,128)(2,1)}, u32[]{:S(2)}, u32[]{:S(2)}) collective-permute-start(bf16[128,3584]{1,0:T(8,128)(2,1)} %collective-permute-done.3.refs_4_), channel_id=1, source_target_pairs={{0,1},{1,0},{2,3},{3,2},{4,5},{5,4},{6,7},{7,6},{8,9},{9,8},{10,11... | collective-permute-start | bytes 2752520 | tf_op jit(solution)/shard_map/ppermute | solution.py:56
  82.1 34.9 %collective-permute-start.9 = (bf16[128,3584]{1,0:T(8,128)(2,1)}, bf16[128,3584]{1,0:T(8,128)(2,1)S(1)}, u32[]{:S(2)}, u32[]{:S(2)}) collective-permute-start(bf16[128,3584]{1,0:T(8,128)(2,1)} %reshape.57.refs_0_), channel_id=1, source_target_pairs={{0,2},{1,3},{2,4},{3,5},{4,6},{5,7},{6,0},{7,1},{8,10},{9,11},{10,... | collective-permute-start | bytes 2752520 | tf_op jit(solution)/shard_map/ppermute | solution.py:45
  84.0 33.0 %collective-permute-start.10 = (bf16[128,3584]{1,0:T(8,128)(2,1)}, bf16[128,3584]{1,0:T(8,128)(2,1)}, u32[]{:S(2)}, u32[]{:S(2)}) collective-permute-start(bf16[128,3584]{1,0:T(8,128)(2,1)} %reshape.57.refs_0_), channel_id=1, source_target_pairs={{0,6},{1,7},{2,0},{3,1},{4,2},{5,3},{6,4},{7,5},{8,14},{9,15},{10,... | collective-permute-start | bytes 2752520 | tf_op jit(solution)/shard_map/ppermute | solution.py:45
  90.9 26.1 %all-to-all-start.1 = ((f32[64,1,2]{2,1,0:T(1,128)}), f32[64,1,2]{2,1,0:T(1,128)S(1)}, u32[]{:S(2)}, u32[]{:S(2)}) async-start(f32[64,1,2]{2,1,0:T(1,128)} %bitcast.13), calls=%async_computation.1 | async-start | bytes 65536 | tf_op jit(solution)/shard_map/all_to_all | solution.py:221
  103.7 23.2 %collective-permute-start.8 = (bf16[128,3584]{1,0:T(8,128)(2,1)}, bf16[128,3584]{1,0:T(8,128)(2,1)}, u32[]{:S(2)}, u32[]{:S(2)}) collective-permute-start(bf16[128,3584]{1,0:T(8,128)(2,1)} %reshape.57.refs_0_), channel_id=1, source_target_pairs={{0,1},{1,0},{2,3},{3,2},{4,5},{5,4},{6,7},{7,6},{8,9},{9,8},{10,11... | collective-permute-start | bytes 2752520 | tf_op jit(solution)/shard_map/ppermute | solution.py:56
  119.2 14.7 %collective-permute-start.13 = (bf16[128,3584]{1,0:T(8,128)(2,1)}, bf16[128,3584]{1,0:T(8,128)(2,1)}, u32[]{:S(2)}, u32[]{:S(2)}) collective-permute-start(bf16[128,3584]{1,0:T(8,128)(2,1)} %broadcast_select_fusion), channel_id=1, source_target_pairs={{0,2},{1,7},{2,4},{3,1},{4,6},{5,3},{6,0},{7,5},{8,10},{9,15},{10,... | collective-permute-start | bytes 2752520 | tf_op jit(solution)/shard_map/ppermute | solution.py:51
  121.7 17.1 %collective-permute-start.11 = (bf16[128,3584]{1,0:T(8,128)(2,1)S(1)}, bf16[128,3584]{1,0:T(8,128)(2,1)}, u32[]{:S(2)}, u32[]{:S(2)}) collective-permute-start(bf16[128,3584]{1,0:T(8,128)(2,1)S(1)} %collective-permute-done.9.refs_2_), channel_id=1, source_target_pairs={{0,1},{1,0},{2,3},{3,2},{4,5},{5,4},{6,7},{7,6},{8,9},{9,8},{10,11... | collective-permute-start | bytes 2752520 | tf_op jit(solution)/shard_map/ppermute | solution.py:56
  124.1 14.7 %collective-permute-start.12 = (bf16[128,3584]{1,0:T(8,128)(2,1)}, bf16[128,3584]{1,0:T(8,128)(2,1)}, u32[]{:S(2)}, u32[]{:S(2)}) collective-permute-start(bf16[128,3584]{1,0:T(8,128)(2,1)} %collective-permute-done.10.refs_3_), channel_id=1, source_target_pairs={{0,1},{1,0},{2,3},{3,2},{4,5},{5,4},{6,7},{7,6},{8,9},{9,8},{10,11... | collective-permute-start | bytes 2752520 | tf_op jit(solution)/shard_map/ppermute | solution.py:56
  126.2 14.8 %copy-start.2 = (bf16[1,128,3584]{2,1,0:T(8,128)(2,1)S(1)}, bf16[1,128,3584]{2,1,0:T(8,128)(2,1)}, u32[]{:S(2)}) copy-start(bf16[1,128,3584]{2,1,0:T(8,128)(2,1)} %param.11) | copy-start | bytes 2752516
  134.0 7.1 %collective-permute-start.14 = (bf16[128,3584]{1,0:T(8,128)(2,1)}, bf16[128,3584]{1,0:T(8,128)(2,1)S(1)}, u32[]{:S(2)}, u32[]{:S(2)}) collective-permute-start(bf16[128,3584]{1,0:T(8,128)(2,1)} %collective-permute-done.13.refs_2_), channel_id=1, source_target_pairs={{0,1},{1,0},{2,3},{3,2},{4,5},{5,4},{6,7},{7,6},{8,9},{9,8},{10,11... | collective-permute-start | bytes 2752520 | tf_op jit(solution)/shard_map/ppermute | solution.py:56

commit v5 on v4

--- a/solution.py
+++ b/solution.py
@@ -96,7 +96,7 @@
     )(partners, *pieces, hidden_own)
 
 
-def own_slots(hidden_now, me):
+def own_slots(hidden_now, me, stack, far):
     members = lax.axis_size("local")
     rows, units = hidden_now.shape
     held = hidden_now.reshape(2, 2, 2, rows // members, units)
@@ -107,8 +107,14 @@
         keep = jnp.where(mine == 0, low, high)
         give = jnp.where(mine == 0, high, low)
         got = lax.ppermute(give, "local", [(i, i ^ bit) for i in range(members)])
+        if bit == 1:
+            got, *stack = lax.optimization_barrier((got, *stack))
+            mates = hand_over(jnp.concatenate(stack, 0))
+        if bit == 2:
+            got, far = lax.optimization_barrier((got, far))
+            far_mate = hand_over(far)
         held = jnp.stack([keep, got], axis)
-    return held.reshape(rows, units)
+    return held.reshape(rows, units), mates, far, far_mate
 
 
 def piece_partners(me):
@@ -212,10 +218,8 @@
     low, high = gather_ways(weight_now)
     low, high, hidden_later = lax.optimization_barrier((low, high, hidden_now))
     far = go_on(low, high, core)
-    mates = hand_over(jnp.concatenate([weight_now, low, high], 0))
-    hidden_own = own_slots(hidden_later, me)
-    far, hidden_own = lax.optimization_barrier((far, hidden_own))
-    y = back_projection(piece_partners(me), (weight_now, low, high, mates, far, hand_over(far)), hidden_own)
+    hidden_own, mates, far, far_mate = own_slots(hidden_later, me, (weight_now, low, high), far)
+    y = back_projection(piece_partners(me), (weight_now, low, high, mates, far, far_mate), hidden_own)
     scaled, y = lax.optimization_barrier((scaled, y))
     own_score = jnp.sum(scaled.astype(jnp.float32) * y, 1)
     returned = lax.all_to_all(

time: 147 us -> 155 us (1.054)
  starting transfers between devices: 80.3 us -> 87.8 us
  other arithmetic: 12.2 us -> 13.8 us
    ppermute x3, waiting for transfers between devices: 9.23 us -> 15.9 us  [own_slots(): got = lax.ppermute(give, 'local', [(i, i ^ bit) for i in range(members)])]
    all_to_all x1, waiting for transfers between devices: 5.8 us -> 0.01 us  [on_device(): lax.all_to_all(leaving, 'node', split_axis=0, concat_axis=0, tiled=True)]
    all_to_all x1, starting transfers between devices: 12.9 us -> 18.6 us  [on_device(): lax.all_to_all(own_score.reshape(node_count, CAP), 'node', split_axis=0,...]
    ppermute x3, starting transfers between devices: 8.6 us -> 10.6 us  [own_slots(): got = lax.ppermute(give, 'local', [(i, i ^ bit) for i in range(members)])]
    ppermute x6, starting transfers between devices: 19.7 us -> 18.2 us  [hand_over(): return lax.ppermute(piece, 'local', [(i, i ^ 1) for i in range(members)])]
  transfers between devices with their start and end apart: 17 -> 17, of which waited for: 7 -> 6; matrix products, arithmetic and copies ran while one was open for 11% -> 11% of each run, Pallas kernels for 2% -> 2%
where the time goes in v5:
time: 155 us; the launch traced here: 154 us
  starting transfers between devices  87.8 us (57%)
  waiting for transfers between devices  30 us (19%)
  other arithmetic  13.8 us (9%)
  Pallas kernels  12.8 us (8%)
  local copies, waits for them, and re-layouts  8.4 us (5%)
    all_to_all x1, starting transfers between devices, on_device(): lax.all_to_all(leaving, 'node', split_axis=0, concat_axis=0, tiled=True)  18.9 us
    all_to_all x1, starting transfers between devices, on_device(): lax.all_to_all(own_score.reshape(node_count, CAP), 'node', split_axis=0,...  18.6 us
    ppermute x6, starting transfers between devices, hand_over(): return lax.ppermute(piece, 'local', [(i, i ^ 1) for i in range(members)])  18.2 us
    ppermute x3, waiting for transfers between devices, own_slots(): got = lax.ppermute(give, 'local', [(i, i ^ bit) for i in range(members)])  15.9 us
    ppermute x3, starting transfers between devices, own_slots(): got = lax.ppermute(give, 'local', [(i, i ^ bit) for i in range(members)])  10.6 us
    all_to_all x1, waiting for transfers between devices, on_device(): lax.all_to_all(own_score.reshape(node_count, CAP), 'node', split_axis=0,...  9.38 us
    pallas_call x2, Pallas kernels, grads(): pl.pallas_call(functools.partial(grad_kernel, count, start, final), in_sp...  8.87 us
    ppermute x2, starting transfers between devices, go_on(): return lax.ppermute(jnp.where(core == 0, low, high), 'local', onward)  7.74 us
  transfers between devices with their start and end apart: 17, of which 6 were waited for; matrix products, arithmetic and copies ran while one was open for 11% of the time, Pallas kernels for 2%

profile of v5, /device:TPU:1, one launch (start us, length us, event | category | flops | bytes accessed | tf_op | source)
XLA Modules:
  0.0 154.4 jit_solution(12568505246482246510)
XLA Ops:
  0.7 0.8 fusion.15
  1.5 0.7 fusion.12
  2.2 0.7 select_reduce_fusion.2
  2.9 0.2 convert_reduce_fusion
  3.1 0.1 select_reduce_fusion.1
  3.2 0.4 fusion
  3.6 1.3 reshape.56
  4.9 3.9 %collective-permute-start = (bf16[128,3584]{1,0:T(8,128)(2,1)S(1)}, bf16[128,3584]{1,0:T(8,128)(2,1)S(1)}, u32[]{:S(2)}, u32[]{:S(2)}) collective-permute-start(bf16[128,3584]{1,0:T(8,128)(2,1)S(1)} %bitcast.55), channel_id=1, source_target_pairs={{0,2},{1,3},{2,4},{3,5},{4,6},{5,7},{6,0},{7,1},{8,10},{9,11},{10,... | collective-permute-start | bytes 2752520 | tf_op jit(solution)/shard_map/ppermute | solution.py:45
  8.9 3.2 %collective-permute-start.1 = (bf16[128,3584]{1,0:T(8,128)(2,1)S(1)}, bf16[128,3584]{1,0:T(8,128)(2,1)}, u32[]{:S(2)}, u32[]{:S(2)}) collective-permute-start(bf16[128,3584]{1,0:T(8,128)(2,1)S(1)} %bitcast.56), channel_id=1, source_target_pairs={{0,6},{1,7},{2,0},{3,1},{4,2},{5,3},{6,4},{7,5},{8,14},{9,15},{10,... | collective-permute-start | bytes 2752520 | tf_op jit(solution)/shard_map/ppermute | solution.py:45
  12.1 18.9 %all-to-all-start = ((bf16[64,2,3584]{2,1,0:T(2,128)(2,1)}), bf16[64,2,3584]{2,1,0:T(2,128)(2,1)}, u32[]{:S(2)}, u32[]{:S(2)}) async-start(bf16[64,2,3584]{2,1,0:T(2,128)(2,1)} %reshape.56), calls=%async_computation | async-start | bytes 1835008 | tf_op jit(solution)/shard_map/all_to_all | solution.py:212
  31.0 0.1 copy.55
  31.2 0.2 reshape.58
  31.3 1.1 fusion.17
  32.4 1.1 copy.71
  33.5 0.2 copy.70
  33.7 4.4 %collective-permute-start.2 = (bf16[2,2,128,128]{3,2,1,0:T(8,128)(2,1)S(1)}, bf16[2,2,128,128]{3,2,1,0:T(8,128)(2,1)S(1)}, u32[]{:S(2)}, u32[]{:S(2)}) collective-permute-start(bf16[2,2,128,128]{3,2,1,0:T(8,128)(2,1)S(1)} %get-tuple-element.59), channel_id=1, source_target_pairs={{0,1},{1,0},{2,3},{3,2},{4,5},{5,4},{6,7},{7,6},{8,9},{9,8},{10,11... | collective-permute-start | bytes 393224 | tf_op jit(solution)/shard_map/ppermute | solution.py:109
  38.1 1.0 collective-permute-done.2
  39.0 2.9 %pad_maximum_fusion = bf16[384,3584]{1,0:T(8,128)(2,1)} fusion(bf16[128,3584]{1,0:T(8,128)(2,1)} %collective-permute-done.1.refs_2_, bf16[128,3584]{1,0:T(8,128)(2,1)S(1)} %collective-permute-done.refs_1_, bf16[128,3584]{1,0:T(8,128)(2,1)S(1)} %bitcast.57), kind=kLoop, calls=%fused_computation.2 | loop fusion | flops 8257536 | bytes 5505024 | tf_op jit(solution)/shard_map/concatenate | solution.py:112
  42.0 2.3 %collective-permute-start.3 = (bf16[384,3584]{1,0:T(8,128)(2,1)}, bf16[384,3584]{1,0:T(8,128)(2,1)}, u32[]{:S(2)}, u32[]{:S(2)}) collective-permute-start(bf16[384,3584]{1,0:T(8,128)(2,1)} %pad_maximum_fusion), channel_id=1, source_target_pairs={{0,1},{1,0},{2,3},{3,2},{4,5},{5,4},{6,7},{7,6},{8,9},{9,8},{10,11... | collective-permute-start | bytes 8257544 | tf_op jit(solution)/shard_map/ppermute | solution.py:56
  44.3 2.2 %broadcast_select_fusion.1 = bf16[128,3584]{1,0:T(8,128)(2,1)} fusion(bf16[128,3584]{1,0:T(8,128)(2,1)S(1)} %collective-permute-done.refs_1_, bf16[128,3584]{1,0:T(8,128)(2,1)} %collective-permute-done.1.refs_2_, pred[]{:T(512)S(6)} %eq.71), kind=kLoop, calls=%fused_computation.5 | loop fusion | flops 458752 | bytes 2752513 | tf_op jit(solution)/shard_map/jit(_where)/select_n | solution.py:51
  46.5 4.4 %collective-permute-start.5 = (bf16[128,3584]{1,0:T(8,128)(2,1)}, bf16[128,3584]{1,0:T(8,128)(2,1)}, u32[]{:S(2)}, u32[]{:S(2)}) collective-permute-start(bf16[128,3584]{1,0:T(8,128)(2,1)} %broadcast_select_fusion.1), channel_id=1, source_target_pairs={{0,2},{1,7},{2,4},{3,1},{4,6},{5,3},{6,0},{7,5},{8,10},{9,15},{10,... | collective-permute-start | bytes 2752520 | tf_op jit(solution)/shard_map/ppermute | solution.py:51
  50.9 1.9 %collective-permute-start.4 = (bf16[2,2,128,128]{3,2,0,1:T(8,128)(2,1)S(1)}, bf16[2,2,128,128]{3,2,0,1:T(8,128)(2,1)S(1)}, u32[]{:S(2)}, u32[]{:S(2)}) collective-permute-start(bf16[2,2,128,128]{3,2,0,1:T(8,128)(2,1)S(1)} %fusion.4), channel_id=1, source_target_pairs={{0,2},{1,3},{2,0},{3,1},{4,6},{5,7},{6,4},{7,5},{8,10},{9,11},{10,... | collective-permute-start | bytes 393224 | tf_op jit(solution)/shard_map/ppermute | solution.py:109
  52.8 11.2 %collective-permute-done.4 = bf16[2,2,128,128]{3,2,0,1:T(8,128)(2,1)S(1)} collective-permute-done((bf16[2,2,128,128]{3,2,0,1:T(8,128)(2,1)S(1)}, bf16[2,2,128,128]{3,2,0,1:T(8,128)(2,1)S(1)}, u32[]{:S(2)}, u32[]{:S(2)}) %collective-permute-start.4) | collective-permute-done | bytes 131104 | tf_op jit(solution)/shard_map/ppermute | solution.py:109
  64.0 1.9 %collective-permute-start.6 = (bf16[128,3584]{1,0:T(8,128)(2,1)}, bf16[128,3584]{1,0:T(8,128)(2,1)}, u32[]{:S(2)}, u32[]{:S(2)}) collective-permute-start(bf16[128,3584]{1,0:T(8,128)(2,1)} %collective-permute-done.5.refs_4_), channel_id=1, source_target_pairs={{0,1},{1,0},{2,3},{3,2},{4,5},{5,4},{6,7},{7,6},{8,9},{9,8},{10,11... | collective-permute-start | bytes 2752520 | tf_op jit(solution)/shard_map/ppermute | solution.py:56
  66.0 0.7 fusion.1
  66.7 4.3 %collective-permute-start.7 = (bf16[2,2,128,128]{3,2,0,1:T(8,128)(2,1)}, bf16[2,2,128,128]{3,2,0,1:T(8,128)(2,1)}, u32[]{:S(2)}, u32[]{:S(2)}) collective-permute-start(bf16[2,2,128,128]{3,2,0,1:T(8,128)(2,1)} %fusion.1), channel_id=1, source_target_pairs={{0,4},{1,5},{2,6},{3,7},{4,0},{5,1},{6,2},{7,3},{8,12},{9,13},{10,... | collective-permute-start | bytes 393224 | tf_op jit(solution)/shard_map/ppermute | solution.py:109
  71.2 3.8 %collective-permute-done.7 = bf16[2,2,128,128]{3,2,0,1:T(8,128)(2,1)} collective-permute-done((bf16[2,2,128,128]{3,2,0,1:T(8,128)(2,1)}, bf16[2,2,128,128]{3,2,0,1:T(8,128)(2,1)}, u32[]{:S(2)}, u32[]{:S(2)}) %collective-permute-start.7) | collective-permute-done | bytes 131104 | tf_op jit(solution)/shard_map/ppermute | solution.py:109
  74.9 0.9 pad_maximum_fusion.1
  75.9 3.2 %reshape.57.refs_0_ = bf16[128,3584]{1,0:T(8,128)(2,1)} reshape(bf16[64,2,3584]{2,1,0:T(2,128)(2,1)} %all-to-all-done) | data formatting | bytes 1835008 | tf_op jit(solution)/shard_map/reshape | solution.py:212
  79.1 3.9 %back_projection.1 = f32[128,3584]{1,0:T(8,128)S(1)} custom-call(s32[8]{0:T(128)S(1)} %stack.67.partners_ref, bf16[128,3584]{1,0:T(8,128)(2,1)S(1)} %bitcast.58, bf16[128,3584]{1,0:T(8,128)(2,1)S(1)} %collective-permute-done.refs_1_, bf16[128,3584]{1,0:T(8,128)(2,1)} %collective-permute-done.1.refs_2_, bf16[384,3584]{1,0:T(8,128)(2,1)} %collective-permute-done.3.refs_3_, ...), custom_call_target="tpu_custom_call" | custom-call | flops 939524096 | bytes 9175040 | tf_op jit(solution)/shard_map/back_projection/pallas_call | solution.py:86
  83.0 3.4 %collective-permute-start.9 = (bf16[128,3584]{1,0:T(8,128)(2,1)}, bf16[128,3584]{1,0:T(8,128)(2,1)S(1)}, u32[]{:S(2)}, u32[]{:S(2)}) collective-permute-start(bf16[128,3584]{1,0:T(8,128)(2,1)} %reshape.57.refs_0_), channel_id=1, source_target_pairs={{0,2},{1,3},{2,4},{3,5},{4,6},{5,7},{6,0},{7,1},{8,10},{9,11},{10,... | collective-permute-start | bytes 2752520 | tf_op jit(solution)/shard_map/ppermute | solution.py:45
  86.4 3.2 %collective-permute-start.10 = (bf16[128,3584]{1,0:T(8,128)(2,1)}, bf16[128,3584]{1,0:T(8,128)(2,1)}, u32[]{:S(2)}, u32[]{:S(2)}) collective-permute-start(bf16[128,3584]{1,0:T(8,128)(2,1)} %reshape.57.refs_0_), channel_id=1, source_target_pairs={{0,6},{1,7},{2,0},{3,1},{4,2},{5,3},{6,4},{7,5},{8,14},{9,15},{10,... | collective-permute-start | bytes 2752520 | tf_op jit(solution)/shard_map/ppermute | solution.py:45
  89.6 1.5 multiply_reduce_fusion
  91.1 0.8 all_to_all.12
  91.9 18.6 %all-to-all-start.1 = ((f32[64,1,2]{2,1,0:T(1,128)}), f32[64,1,2]{2,1,0:T(1,128)S(1)}, u32[]{:S(2)}, u32[]{:S(2)}) async-start(f32[64,1,2]{2,1,0:T(1,128)} %bitcast.19), calls=%async_computation.1 | async-start | bytes 65536 | tf_op jit(solution)/shard_map/all_to_all | solution.py:225
  110.6 3.8 %collective-permute-start.8 = (bf16[128,3584]{1,0:T(8,128)(2,1)}, bf16[128,3584]{1,0:T(8,128)(2,1)}, u32[]{:S(2)}, u32[]{:S(2)}) collective-permute-start(bf16[128,3584]{1,0:T(8,128)(2,1)} %reshape.57.refs_0_), channel_id=1, source_target_pairs={{0,1},{1,0},{2,3},{3,2},{4,5},{5,4},{6,7},{7,6},{8,9},{9,8},{10,11... | collective-permute-start | bytes 2752520 | tf_op jit(solution)/shard_map/ppermute | solution.py:56
  114.4 9.4 %all-to-all-done.1 = f32[64,1,2]{2,1,0:T(1,128)S(1)} async-done(((f32[64,1,2]{2,1,0:T(1,128)}), f32[64,1,2]{2,1,0:T(1,128)S(1)}, u32[]{:S(2)}, u32[]{:S(2)}) %all-to-all-start.1) | async-done | bytes 544 | tf_op jit(solution)/shard_map/all_to_all | solution.py:225
  123.8 2.2 %broadcast_select_fusion = bf16[128,3584]{1,0:T(8,128)(2,1)} fusion(bf16[128,3584]{1,0:T(8,128)(2,1)S(1)} %collective-permute-done.9.refs_2_, bf16[128,3584]{1,0:T(8,128)(2,1)} %collective-permute-done.10.refs_3_, pred[]{:T(512)S(6)} %eq.71), kind=kLoop, calls=%fused_computation.4 | loop fusion | flops 458752 | bytes 2752513 | tf_op jit(solution)/shard_map/jit(_where)/select_n | solution.py:51
  126.1 3.4 %collective-permute-start.13 = (bf16[128,3584]{1,0:T(8,128)(2,1)}, bf16[128,3584]{1,0:T(8,128)(2,1)}, u32[]{:S(2)}, u32[]{:S(2)}) collective-permute-start(bf16[128,3584]{1,0:T(8,128)(2,1)} %broadcast_select_fusion), channel_id=1, source_target_pairs={{0,2},{1,7},{2,4},{3,1},{4,6},{5,3},{6,0},{7,5},{8,10},{9,15},{10,... | collective-permute-start | bytes 2752520 | tf_op jit(solution)/shard_map/ppermute | solution.py:51
  129.6 2.4 %collective-permute-start.11 = (bf16[128,3584]{1,0:T(8,128)(2,1)S(1)}, bf16[128,3584]{1,0:T(8,128)(2,1)}, u32[]{:S(2)}, u32[]{:S(2)}) collective-permute-start(bf16[128,3584]{1,0:T(8,128)(2,1)S(1)} %collective-permute-done.9.refs_2_), channel_id=1, source_target_pairs={{0,1},{1,0},{2,3},{3,2},{4,5},{5,4},{6,7},{7,6},{8,9},{9,8},{10,11... | collective-permute-start | bytes 2752520 | tf_op jit(solution)/shard_map/ppermute | solution.py:56
  132.0 2.0 %collective-permute-start.12 = (bf16[128,3584]{1,0:T(8,128)(2,1)}, bf16[128,3584]{1,0:T(8,128)(2,1)}, u32[]{:S(2)}, u32[]{:S(2)}) collective-permute-start(bf16[128,3584]{1,0:T(8,128)(2,1)} %collective-permute-done.10.refs_3_), channel_id=1, source_target_pairs={{0,1},{1,0},{2,3},{3,2},{4,5},{5,4},{6,7},{7,6},{8,9},{9,8},{10,11... | collective-permute-start | bytes 2752520 | tf_op jit(solution)/shard_map/ppermute | solution.py:56
  134.0 0.1 broadcast_in_dim.70
  134.3 0.6 broadcast_select_fusion.3
  134.9 3.4 %grads_first.1 = (f32[128,3584]{1,0:T(8,128)S(1)}, bf16[512,128]{1,0:T(8,128)(2,1)S(1)}) custom-call(s32[8]{0:T(128)S(1)} %stack.82.blocks_ref, bf16[128,3584]{1,0:T(8,128)(2,1)} %reshape.57.refs_0_, bf16[128,3584]{1,0:T(8,128)(2,1)} %collective-permute-done.8.refs_1_, bf16[128,3584]{1,0:T(8,128)(2,1)S(1)} %collective-permute-done.9.refs_2_, ...), custom_call_target="tpu_custom_call" | custom-call | flops 939524096 | bytes 9175040 | tf_op jit(solution)/shard_map/grads_first/pallas_call | solution.py:186
  138.4 2.4 %collective-permute-done.13.refs_2_ = bf16[128,3584]{1,0:T(8,128)(2,1)} collective-permute-done((bf16[128,3584]{1,0:T(8,128)(2,1)}, bf16[128,3584]{1,0:T(8,128)(2,1)}, u32[]{:S(2)}, u32[]{:S(2)}) %collective-permute-start.13) | collective-permute-done | bytes 917536 | tf_op jit(solution)/shard_map/ppermute | solution.py:51
  140.8 5.9 %collective-permute-start.14 = (bf16[128,3584]{1,0:T(8,128)(2,1)}, bf16[128,3584]{1,0:T(8,128)(2,1)S(1)}, u32[]{:S(2)}, u32[]{:S(2)}) collective-permute-start(bf16[128,3584]{1,0:T(8,128)(2,1)} %collective-permute-done.13.refs_2_), channel_id=1, source_target_pairs={{0,1},{1,0},{2,3},{3,2},{4,5},{5,4},{6,7},{7,6},{8,9},{9,8},{10,11... | collective-permute-start | bytes 2752520 | tf_op jit(solution)/shard_map/ppermute | solution.py:56
  146.7 2.3 %collective-permute-done.14.refs_3_ = bf16[128,3584]{1,0:T(8,128)(2,1)S(1)} collective-permute-done((bf16[128,3584]{1,0:T(8,128)(2,1)}, bf16[128,3584]{1,0:T(8,128)(2,1)S(1)}, u32[]{:S(2)}, u32[]{:S(2)}) %collective-permute-start.14) | collective-permute-done | bytes 917536 | tf_op jit(solution)/shard_map/ppermute | solution.py:56
  148.9 5.4 %grads_last.1 = (bf16[1024,128]{1,0:T(8,128)(2,1)}, bf16[128,3584]{1,0:T(8,128)(2,1)}, bf16[128,3584]{1,0:T(8,128)(2,1)}) custom-call(s32[8]{0:T(128)S(1)} %stack.82.blocks_ref, bf16[128,3584]{1,0:T(8,128)(2,1)} %collective-permute-done.11.refs_0_, bf16[128,3584]{1,0:T(8,128)(2,1)} %collective-permute-done.12.refs_1_, ...), custom_call_target="tpu_custom_call" | custom-call | flops 939524096 | bytes 9175040 | tf_op jit(solution)/shard_map/grads_last/pallas_call | solution.py:186
  (32 shorter events, 0.6 us)
Async XLA Ops:
  0.6 2.6 %copy-start = (bf16[128,3584]{1,0:T(8,128)(2,1)S(1)}, bf16[128,3584]{1,0:T(8,128)(2,1)}, u32[]{:S(2)}) copy-start(bf16[128,3584]{1,0:T(8,128)(2,1)} %param.6) | copy-start | bytes 2752516
  0.6 4.3 %copy-start.1 = (bf16[1,128,3584]{2,1,0:T(8,128)(2,1)S(1)}, bf16[1,128,3584]{2,1,0:T(8,128)(2,1)}, u32[]{:S(2)}) copy-start(bf16[1,128,3584]{2,1,0:T(8,128)(2,1)} %param.10) | copy-start | bytes 2752516
  3.2 27.7 %copy-start.3 = (bf16[1,1024,128]{2,1,0:T(8,128)(2,1)S(1)}, bf16[1,1024,128]{2,1,0:T(8,128)(2,1)}, u32[]{:S(2)}) copy-start(bf16[1,1024,128]{2,1,0:T(8,128)(2,1)} %param.9) | copy-start | bytes 786436
  4.9 26.2 %collective-permute-start = (bf16[128,3584]{1,0:T(8,128)(2,1)S(1)}, bf16[128,3584]{1,0:T(8,128)(2,1)S(1)}, u32[]{:S(2)}, u32[]{:S(2)}) collective-permute-start(bf16[128,3584]{1,0:T(8,128)(2,1)S(1)} %bitcast.55), channel_id=1, source_target_pairs={{0,2},{1,3},{2,4},{3,5},{4,6},{5,7},{6,0},{7,1},{8,10},{9,11},{10,... | collective-permute-start | bytes 2752520 | tf_op jit(solution)/shard_map/ppermute | solution.py:45
  8.9 22.3 %collective-permute-start.1 = (bf16[128,3584]{1,0:T(8,128)(2,1)S(1)}, bf16[128,3584]{1,0:T(8,128)(2,1)}, u32[]{:S(2)}, u32[]{:S(2)}) collective-permute-start(bf16[128,3584]{1,0:T(8,128)(2,1)S(1)} %bitcast.56), channel_id=1, source_target_pairs={{0,6},{1,7},{2,0},{3,1},{4,2},{5,3},{6,4},{7,5},{8,14},{9,15},{10,... | collective-permute-start | bytes 2752520 | tf_op jit(solution)/shard_map/ppermute | solution.py:45
  12.1 63.8 %all-to-all-start = ((bf16[64,2,3584]{2,1,0:T(2,128)(2,1)}), bf16[64,2,3584]{2,1,0:T(2,128)(2,1)}, u32[]{:S(2)}, u32[]{:S(2)}) async-start(bf16[64,2,3584]{2,1,0:T(2,128)(2,1)} %reshape.56), calls=%async_computation | async-start | bytes 1835008 | tf_op jit(solution)/shard_map/all_to_all | solution.py:212
  33.7 5.4 %collective-permute-start.2 = (bf16[2,2,128,128]{3,2,1,0:T(8,128)(2,1)S(1)}, bf16[2,2,128,128]{3,2,1,0:T(8,128)(2,1)S(1)}, u32[]{:S(2)}, u32[]{:S(2)}) collective-permute-start(bf16[2,2,128,128]{3,2,1,0:T(8,128)(2,1)S(1)} %get-tuple-element.59), channel_id=1, source_target_pairs={{0,1},{1,0},{2,3},{3,2},{4,5},{5,4},{6,7},{7,6},{8,9},{9,8},{10,11... | collective-permute-start | bytes 393224 | tf_op jit(solution)/shard_map/ppermute | solution.py:109
  42.0 37.1 %collective-permute-start.3 = (bf16[384,3584]{1,0:T(8,128)(2,1)}, bf16[384,3584]{1,0:T(8,128)(2,1)}, u32[]{:S(2)}, u32[]{:S(2)}) collective-permute-start(bf16[384,3584]{1,0:T(8,128)(2,1)} %pad_maximum_fusion), channel_id=1, source_target_pairs={{0,1},{1,0},{2,3},{3,2},{4,5},{5,4},{6,7},{7,6},{8,9},{9,8},{10,11... | collective-permute-start | bytes 8257544 | tf_op jit(solution)/shard_map/ppermute | solution.py:56
  46.5 17.6 %collective-permute-start.5 = (bf16[128,3584]{1,0:T(8,128)(2,1)}, bf16[128,3584]{1,0:T(8,128)(2,1)}, u32[]{:S(2)}, u32[]{:S(2)}) collective-permute-start(bf16[128,3584]{1,0:T(8,128)(2,1)} %broadcast_select_fusion.1), channel_id=1, source_target_pairs={{0,2},{1,7},{2,4},{3,1},{4,6},{5,3},{6,0},{7,5},{8,10},{9,15},{10,... | collective-permute-start | bytes 2752520 | tf_op jit(solution)/shard_map/ppermute | solution.py:51
  50.9 13.1 %collective-permute-start.4 = (bf16[2,2,128,128]{3,2,0,1:T(8,128)(2,1)S(1)}, bf16[2,2,128,128]{3,2,0,1:T(8,128)(2,1)S(1)}, u32[]{:S(2)}, u32[]{:S(2)}) collective-permute-start(bf16[2,2,128,128]{3,2,0,1:T(8,128)(2,1)S(1)} %fusion.4), channel_id=1, source_target_pairs={{0,2},{1,3},{2,0},{3,1},{4,6},{5,7},{6,4},{7,5},{8,10},{9,11},{10,... | collective-permute-start | bytes 393224 | tf_op jit(solution)/shard_map/ppermute | solution.py:109
  64.0 15.1 %collective-permute-start.6 = (bf16[128,3584]{1,0:T(8,128)(2,1)}, bf16[128,3584]{1,0:T(8,128)(2,1)}, u32[]{:S(2)}, u32[]{:S(2)}) collective-permute-start(bf16[128,3584]{1,0:T(8,128)(2,1)} %collective-permute-done.5.refs_4_), channel_id=1, source_target_pairs={{0,1},{1,0},{2,3},{3,2},{4,5},{5,4},{6,7},{7,6},{8,9},{9,8},{10,11... | collective-permute-start | bytes 2752520 | tf_op jit(solution)/shard_map/ppermute | solution.py:56
  66.7 8.3 %collective-permute-start.7 = (bf16[2,2,128,128]{3,2,0,1:T(8,128)(2,1)}, bf16[2,2,128,128]{3,2,0,1:T(8,128)(2,1)}, u32[]{:S(2)}, u32[]{:S(2)}) collective-permute-start(bf16[2,2,128,128]{3,2,0,1:T(8,128)(2,1)} %fusion.1), channel_id=1, source_target_pairs={{0,4},{1,5},{2,6},{3,7},{4,0},{5,1},{6,2},{7,3},{8,12},{9,13},{10,... | collective-permute-start | bytes 393224 | tf_op jit(solution)/shard_map/ppermute | solution.py:109
  83.0 40.8 %collective-permute-start.9 = (bf16[128,3584]{1,0:T(8,128)(2,1)}, bf16[128,3584]{1,0:T(8,128)(2,1)S(1)}, u32[]{:S(2)}, u32[]{:S(2)}) collective-permute-start(bf16[128,3584]{1,0:T(8,128)(2,1)} %reshape.57.refs_0_), channel_id=1, source_target_pairs={{0,2},{1,3},{2,4},{3,5},{4,6},{5,7},{6,0},{7,1},{8,10},{9,11},{10,... | collective-permute-start | bytes 2752520 | tf_op jit(solution)/shard_map/ppermute | solution.py:45
  86.4 37.4 %collective-permute-start.10 = (bf16[128,3584]{1,0:T(8,128)(2,1)}, bf16[128,3584]{1,0:T(8,128)(2,1)}, u32[]{:S(2)}, u32[]{:S(2)}) collective-permute-start(bf16[128,3584]{1,0:T(8,128)(2,1)} %reshape.57.refs_0_), channel_id=1, source_target_pairs={{0,6},{1,7},{2,0},{3,1},{4,2},{5,3},{6,4},{7,5},{8,14},{9,15},{10,... | collective-permute-start | bytes 2752520 | tf_op jit(solution)/shard_map/ppermute | solution.py:45
  91.9 31.9 %all-to-all-start.1 = ((f32[64,1,2]{2,1,0:T(1,128)}), f32[64,1,2]{2,1,0:T(1,128)S(1)}, u32[]{:S(2)}, u32[]{:S(2)}) async-start(f32[64,1,2]{2,1,0:T(1,128)} %bitcast.19), calls=%async_computation.1 | async-start | bytes 65536 | tf_op jit(solution)/shard_map/all_to_all | solution.py:225
  110.6 24.4 %collective-permute-start.8 = (bf16[128,3584]{1,0:T(8,128)(2,1)}, bf16[128,3584]{1,0:T(8,128)(2,1)}, u32[]{:S(2)}, u32[]{:S(2)}) collective-permute-start(bf16[128,3584]{1,0:T(8,128)(2,1)} %reshape.57.refs_0_), channel_id=1, source_target_pairs={{0,1},{1,0},{2,3},{3,2},{4,5},{5,4},{6,7},{7,6},{8,9},{9,8},{10,11... | collective-permute-start | bytes 2752520 | tf_op jit(solution)/shard_map/ppermute | solution.py:56
  126.1 14.7 %collective-permute-start.13 = (bf16[128,3584]{1,0:T(8,128)(2,1)}, bf16[128,3584]{1,0:T(8,128)(2,1)}, u32[]{:S(2)}, u32[]{:S(2)}) collective-permute-start(bf16[128,3584]{1,0:T(8,128)(2,1)} %broadcast_select_fusion), channel_id=1, source_target_pairs={{0,2},{1,7},{2,4},{3,1},{4,6},{5,3},{6,0},{7,5},{8,10},{9,15},{10,... | collective-permute-start | bytes 2752520 | tf_op jit(solution)/shard_map/ppermute | solution.py:51
  129.6 17.0 %collective-permute-start.11 = (bf16[128,3584]{1,0:T(8,128)(2,1)S(1)}, bf16[128,3584]{1,0:T(8,128)(2,1)}, u32[]{:S(2)}, u32[]{:S(2)}) collective-permute-start(bf16[128,3584]{1,0:T(8,128)(2,1)S(1)} %collective-permute-done.9.refs_2_), channel_id=1, source_target_pairs={{0,1},{1,0},{2,3},{3,2},{4,5},{5,4},{6,7},{7,6},{8,9},{9,8},{10,11... | collective-permute-start | bytes 2752520 | tf_op jit(solution)/shard_map/ppermute | solution.py:56
  132.0 14.7 %collective-permute-start.12 = (bf16[128,3584]{1,0:T(8,128)(2,1)}, bf16[128,3584]{1,0:T(8,128)(2,1)}, u32[]{:S(2)}, u32[]{:S(2)}) collective-permute-start(bf16[128,3584]{1,0:T(8,128)(2,1)} %collective-permute-done.10.refs_3_), channel_id=1, source_target_pairs={{0,1},{1,0},{2,3},{3,2},{4,5},{5,4},{6,7},{7,6},{8,9},{9,8},{10,11... | collective-permute-start | bytes 2752520 | tf_op jit(solution)/shard_map/ppermute | solution.py:56
  134.2 14.8 %copy-start.2 = (bf16[1,128,3584]{2,1,0:T(8,128)(2,1)S(1)}, bf16[1,128,3584]{2,1,0:T(8,128)(2,1)}, u32[]{:S(2)}) copy-start(bf16[1,128,3584]{2,1,0:T(8,128)(2,1)} %param.11) | copy-start | bytes 2752516
  140.8 8.2 %collective-permute-start.14 = (bf16[128,3584]{1,0:T(8,128)(2,1)}, bf16[128,3584]{1,0:T(8,128)(2,1)S(1)}, u32[]{:S(2)}, u32[]{:S(2)}) collective-permute-start(bf16[128,3584]{1,0:T(8,128)(2,1)} %collective-permute-done.13.refs_2_), channel_id=1, source_target_pairs={{0,1},{1,0},{2,3},{3,2},{4,5},{5,4},{6,7},{7,6},{8,9},{9,8},{10,11... | collective-permute-start | bytes 2752520 | tf_op jit(solution)/shard_map/ppermute | solution.py:56

commit v6 on v4

--- a/solution.py
+++ b/solution.py
@@ -143,7 +143,8 @@
         grad = grad + part_ref[:, at]
         second_new = beta_second * second_ref[:, at].astype(jnp.float32) + (1.0 - beta_second) * grad * grad
         weight_f = weight_now.astype(jnp.float32)
-        update = grad / (jnp.sqrt(second_new * (1.0 / correct_second)) + epsilon) + decay_rate * weight_f
+        corrected = second_new * (1.0 / correct_second)
+        update = grad / (corrected * lax.rsqrt(corrected) + epsilon) + decay_rate * weight_f
         weight_out[:, at] = (weight_f - learn_rate * update).astype(jnp.bfloat16)
         second_out[:, at] = second_new.astype(jnp.bfloat16)
 

time: 147 us -> 147 us (level)
  no operation moved by 1% of the time
where the time goes in v6:
time: 147 us; the launch traced here: 146 us
  starting transfers between devices  80.3 us (55%)
  waiting for transfers between devices  31.3 us (21%)
  Pallas kernels  12.3 us (8%)
  other arithmetic  12.2 us (8%)
  local copies, waits for them, and re-layouts  8.39 us (6%)
    ppermute x6, starting transfers between devices, hand_over(): return lax.ppermute(piece, 'local', [(i, i ^ 1) for i in range(members)])  19.7 us
    all_to_all x1, starting transfers between devices, on_device(): lax.all_to_all(leaving, 'node', split_axis=0, concat_axis=0, tiled=True)  18.9 us
    all_to_all x1, starting transfers between devices, on_device(): lax.all_to_all(own_score.reshape(node_count, CAP), 'node', split_axis=0,...  12.9 us
    all_to_all x1, waiting for transfers between devices, on_device(): lax.all_to_all(own_score.reshape(node_count, CAP), 'node', split_axis=0,...  10.4 us
    ppermute x3, waiting for transfers between devices, own_slots(): got = lax.ppermute(give, 'local', [(i, i ^ bit) for i in range(members)])  9.23 us
    ppermute x3, starting transfers between devices, own_slots(): got = lax.ppermute(give, 'local', [(i, i ^ bit) for i in range(members)])  8.6 us
    pallas_call x2, Pallas kernels, grads(): pl.pallas_call(functools.partial(grad_kernel, count, start, final), in_sp...  8.46 us
    ppermute x2, starting transfers between devices, gather_ways(): lax.ppermute(block, 'local', down)  7.76 us
  transfers between devices with their start and end apart: 17, of which 7 were waited for; matrix products, arithmetic and copies ran while one was open for 11% of the time, Pallas kernels for 2%

profile of v6, /device:TPU:1, one launch (start us, length us, event | category | flops | bytes accessed | tf_op | source)
XLA Modules:
  0.0 146.1 jit_solution(2877802289873640138)
XLA Ops:
  0.7 0.8 fusion.13
  1.5 0.7 fusion.10
  2.2 0.7 select_reduce_fusion.2
  2.9 0.2 convert_reduce_fusion
  3.1 0.1 select_reduce_fusion.1
  3.2 0.4 fusion
  3.6 1.3 reshape.56
  4.9 3.9 %collective-permute-start = (bf16[128,3584]{1,0:T(8,128)(2,1)S(1)}, bf16[128,3584]{1,0:T(8,128)(2,1)S(1)}, u32[]{:S(2)}, u32[]{:S(2)}) collective-permute-start(bf16[128,3584]{1,0:T(8,128)(2,1)S(1)} %bitcast.35), channel_id=1, source_target_pairs={{0,2},{1,3},{2,4},{3,5},{4,6},{5,7},{6,0},{7,1},{8,10},{9,11},{10,... | collective-permute-start | bytes 2752520 | tf_op jit(solution)/shard_map/ppermute | solution.py:45
  8.9 3.2 %collective-permute-start.1 = (bf16[128,3584]{1,0:T(8,128)(2,1)S(1)}, bf16[128,3584]{1,0:T(8,128)(2,1)}, u32[]{:S(2)}, u32[]{:S(2)}) collective-permute-start(bf16[128,3584]{1,0:T(8,128)(2,1)S(1)} %bitcast.36), channel_id=1, source_target_pairs={{0,6},{1,7},{2,0},{3,1},{4,2},{5,3},{6,4},{7,5},{8,14},{9,15},{10,... | collective-permute-start | bytes 2752520 | tf_op jit(solution)/shard_map/ppermute | solution.py:45
  12.1 18.9 %all-to-all-start = ((bf16[64,2,3584]{2,1,0:T(2,128)(2,1)}), bf16[64,2,3584]{2,1,0:T(2,128)(2,1)}, u32[]{:S(2)}, u32[]{:S(2)}) async-start(bf16[64,2,3584]{2,1,0:T(2,128)(2,1)} %reshape.56), calls=%async_computation | async-start | bytes 1835008 | tf_op jit(solution)/shard_map/all_to_all | solution.py:207
  31.0 0.1 copy.47
  31.2 3.0 %pad_maximum_fusion = bf16[384,3584]{1,0:T(8,128)(2,1)} fusion(bf16[128,3584]{1,0:T(8,128)(2,1)} %collective-permute-done.1.refs_2_, bf16[128,3584]{1,0:T(8,128)(2,1)S(1)} %collective-permute-done.refs_1_, bf16[128,3584]{1,0:T(8,128)(2,1)S(1)} %bitcast.37), kind=kLoop, calls=%fused_computation.2 | loop fusion | flops 8257536 | bytes 5505024 | tf_op jit(solution)/shard_map/concatenate | solution.py:216
  34.1 4.4 %collective-permute-start.2 = (bf16[384,3584]{1,0:T(8,128)(2,1)}, bf16[384,3584]{1,0:T(8,128)(2,1)}, u32[]{:S(2)}, u32[]{:S(2)}) collective-permute-start(bf16[384,3584]{1,0:T(8,128)(2,1)} %pad_maximum_fusion), channel_id=1, source_target_pairs={{0,1},{1,0},{2,3},{3,2},{4,5},{5,4},{6,7},{7,6},{8,9},{9,8},{10,11... | collective-permute-start | bytes 8257544 | tf_op jit(solution)/shard_map/ppermute | solution.py:56
  38.5 2.2 %broadcast_select_fusion.1 = bf16[128,3584]{1,0:T(8,128)(2,1)} fusion(bf16[128,3584]{1,0:T(8,128)(2,1)S(1)} %collective-permute-done.refs_1_, bf16[128,3584]{1,0:T(8,128)(2,1)} %collective-permute-done.1.refs_2_, pred[]{:T(512)S(6)} %eq.71), kind=kLoop, calls=%fused_computation.5 | loop fusion | flops 458752 | bytes 2752513 | tf_op jit(solution)/shard_map/jit(_where)/select_n | solution.py:51
  40.7 4.4 %collective-permute-start.3 = (bf16[128,3584]{1,0:T(8,128)(2,1)}, bf16[128,3584]{1,0:T(8,128)(2,1)}, u32[]{:S(2)}, u32[]{:S(2)}) collective-permute-start(bf16[128,3584]{1,0:T(8,128)(2,1)} %broadcast_select_fusion.1), channel_id=1, source_target_pairs={{0,2},{1,7},{2,4},{3,1},{4,6},{5,3},{6,0},{7,5},{8,10},{9,15},{10,... | collective-permute-start | bytes 2752520 | tf_op jit(solution)/shard_map/ppermute | solution.py:51
  45.1 0.2 reshape.58
  45.3 1.1 fusion.15
  46.3 1.1 copy.60
  47.4 0.2 copy.61
  47.6 1.9 %collective-permute-start.4 = (bf16[2,2,128,128]{3,2,1,0:T(8,128)(2,1)S(1)}, bf16[2,2,128,128]{3,2,1,0:T(8,128)(2,1)S(1)}, u32[]{:S(2)}, u32[]{:S(2)}) collective-permute-start(bf16[2,2,128,128]{3,2,1,0:T(8,128)(2,1)S(1)} %get-tuple-element.55), channel_id=1, source_target_pairs={{0,1},{1,0},{2,3},{3,2},{4,5},{5,4},{6,7},{7,6},{8,9},{9,8},{10,11... | collective-permute-start | bytes 393224 | tf_op jit(solution)/shard_map/ppermute | solution.py:109
  49.6 1.3 collective-permute-done.4
  50.9 1.9 %collective-permute-start.5 = (bf16[2,2,128,128]{3,2,0,1:T(8,128)(2,1)S(1)}, bf16[2,2,128,128]{3,2,0,1:T(8,128)(2,1)S(1)}, u32[]{:S(2)}, u32[]{:S(2)}) collective-permute-start(bf16[2,2,128,128]{3,2,0,1:T(8,128)(2,1)S(1)} %get-tuple-element.53), channel_id=1, source_target_pairs={{0,2},{1,3},{2,0},{3,1},{4,6},{5,7},{6,4},{7,5},{8,10},{9,11},{10,... | collective-permute-start | bytes 393224 | tf_op jit(solution)/shard_map/ppermute | solution.py:109
  52.9 5.0 %collective-permute-done.5 = bf16[2,2,128,128]{3,2,0,1:T(8,128)(2,1)S(1)} collective-permute-done((bf16[2,2,128,128]{3,2,0,1:T(8,128)(2,1)S(1)}, bf16[2,2,128,128]{3,2,0,1:T(8,128)(2,1)S(1)}, u32[]{:S(2)}, u32[]{:S(2)}) %collective-permute-start.5) | collective-permute-done | bytes 131104 | tf_op jit(solution)/shard_map/ppermute | solution.py:109
  57.9 4.8 %collective-permute-start.6 = (bf16[2,2,128,128]{3,2,0,1:T(8,128)(2,1)S(1)}, bf16[2,2,128,128]{3,2,0,1:T(8,128)(2,1)S(1)}, u32[]{:S(2)}, u32[]{:S(2)}) collective-permute-start(bf16[2,2,128,128]{3,2,0,1:T(8,128)(2,1)S(1)} %get-tuple-element.51), channel_id=1, source_target_pairs={{0,4},{1,5},{2,6},{3,7},{4,0},{5,1},{6,2},{7,3},{8,12},{9,13},{10,... | collective-permute-start | bytes 393224 | tf_op jit(solution)/shard_map/ppermute | solution.py:109
  62.6 3.0 %collective-permute-done.6 = bf16[2,2,128,128]{3,2,0,1:T(8,128)(2,1)S(1)} collective-permute-done((bf16[2,2,128,128]{3,2,0,1:T(8,128)(2,1)S(1)}, bf16[2,2,128,128]{3,2,0,1:T(8,128)(2,1)S(1)}, u32[]{:S(2)}, u32[]{:S(2)}) %collective-permute-start.6) | collective-permute-done | bytes 131104 | tf_op jit(solution)/shard_map/ppermute | solution.py:109
  65.7 3.5 %collective-permute-start.7 = (bf16[128,3584]{1,0:T(8,128)(2,1)}, bf16[128,3584]{1,0:T(8,128)(2,1)}, u32[]{:S(2)}, u32[]{:S(2)}) collective-permute-start(bf16[128,3584]{1,0:T(8,128)(2,1)} %collective-permute-done.3.refs_4_), channel_id=1, source_target_pairs={{0,1},{1,0},{2,3},{3,2},{4,5},{5,4},{6,7},{7,6},{8,9},{9,8},{10,11... | collective-permute-start | bytes 2752520 | tf_op jit(solution)/shard_map/ppermute | solution.py:56
  69.3 5.8 %all-to-all-done = bf16[64,2,3584]{2,1,0:T(2,128)(2,1)} async-done(((bf16[64,2,3584]{2,1,0:T(2,128)(2,1)}), bf16[64,2,3584]{2,1,0:T(2,128)(2,1)}, u32[]{:S(2)}, u32[]{:S(2)}) %all-to-all-start) | async-done | bytes 917536 | tf_op jit(solution)/shard_map/all_to_all | solution.py:207
  75.1 3.2 %reshape.57.refs_0_ = bf16[128,3584]{1,0:T(8,128)(2,1)} reshape(bf16[64,2,3584]{2,1,0:T(2,128)(2,1)} %all-to-all-done) | data formatting | bytes 1835008 | tf_op jit(solution)/shard_map/reshape | solution.py:207
  78.3 3.8 %back_projection.1 = f32[128,3584]{1,0:T(8,128)S(1)} custom-call(s32[8]{0:T(128)S(1)} %stack.67.partners_ref, bf16[128,3584]{1,0:T(8,128)(2,1)S(1)} %bitcast.38, bf16[128,3584]{1,0:T(8,128)(2,1)S(1)} %collective-permute-done.refs_1_, bf16[128,3584]{1,0:T(8,128)(2,1)} %collective-permute-done.1.refs_2_, bf16[384,3584]{1,0:T(8,128)(2,1)} %collective-permute-done.2.refs_3_, ...), custom_call_target="tpu_custom_call" | custom-call | flops 939524096 | bytes 9175040 | tf_op jit(solution)/shard_map/back_projection/pallas_call | solution.py:86
  82.1 1.9 %collective-permute-start.9 = (bf16[128,3584]{1,0:T(8,128)(2,1)}, bf16[128,3584]{1,0:T(8,128)(2,1)S(1)}, u32[]{:S(2)}, u32[]{:S(2)}) collective-permute-start(bf16[128,3584]{1,0:T(8,128)(2,1)} %reshape.57.refs_0_), channel_id=1, source_target_pairs={{0,2},{1,3},{2,4},{3,5},{4,6},{5,7},{6,0},{7,1},{8,10},{9,11},{10,... | collective-permute-start | bytes 2752520 | tf_op jit(solution)/shard_map/ppermute | solution.py:45
  84.0 4.6 %collective-permute-start.10 = (bf16[128,3584]{1,0:T(8,128)(2,1)}, bf16[128,3584]{1,0:T(8,128)(2,1)}, u32[]{:S(2)}, u32[]{:S(2)}) collective-permute-start(bf16[128,3584]{1,0:T(8,128)(2,1)} %reshape.57.refs_0_), channel_id=1, source_target_pairs={{0,6},{1,7},{2,0},{3,1},{4,2},{5,3},{6,4},{7,5},{8,14},{9,15},{10,... | collective-permute-start | bytes 2752520 | tf_op jit(solution)/shard_map/ppermute | solution.py:45
  88.6 1.5 %multiply_reduce_fusion = f32[128]{0:T(128)S(1)} fusion(f32[128,3584]{1,0:T(8,128)S(1)} %back_projection.1, bf16[128,3584]{1,0:T(8,128)(2,1)} %reshape.57.refs_0_), kind=kLoop, calls=%fused_computation.3 | loop fusion | flops 1376128 | bytes 2753024 | tf_op jit(solution)/shard_map/reduce_sum | solution.py:221
  90.1 0.8 all_to_all.12
  90.9 12.9 %all-to-all-start.1 = ((f32[64,1,2]{2,1,0:T(1,128)}), f32[64,1,2]{2,1,0:T(1,128)S(1)}, u32[]{:S(2)}, u32[]{:S(2)}) async-start(f32[64,1,2]{2,1,0:T(1,128)} %bitcast.13), calls=%async_computation.1 | async-start | bytes 65536 | tf_op jit(solution)/shard_map/all_to_all | solution.py:222
  103.7 2.8 %collective-permute-start.8 = (bf16[128,3584]{1,0:T(8,128)(2,1)}, bf16[128,3584]{1,0:T(8,128)(2,1)}, u32[]{:S(2)}, u32[]{:S(2)}) collective-permute-start(bf16[128,3584]{1,0:T(8,128)(2,1)} %reshape.57.refs_0_), channel_id=1, source_target_pairs={{0,1},{1,0},{2,3},{3,2},{4,5},{5,4},{6,7},{7,6},{8,9},{9,8},{10,11... | collective-permute-start | bytes 2752520 | tf_op jit(solution)/shard_map/ppermute | solution.py:56
  106.5 10.4 %all-to-all-done.1 = f32[64,1,2]{2,1,0:T(1,128)S(1)} async-done(((f32[64,1,2]{2,1,0:T(1,128)}), f32[64,1,2]{2,1,0:T(1,128)S(1)}, u32[]{:S(2)}, u32[]{:S(2)}) %all-to-all-start.1) | async-done | bytes 544 | tf_op jit(solution)/shard_map/all_to_all | solution.py:222
  117.0 2.2 %broadcast_select_fusion = bf16[128,3584]{1,0:T(8,128)(2,1)} fusion(bf16[128,3584]{1,0:T(8,128)(2,1)S(1)} %collective-permute-done.9.refs_2_, bf16[128,3584]{1,0:T(8,128)(2,1)} %collective-permute-done.10.refs_3_, pred[]{:T(512)S(6)} %eq.71), kind=kLoop, calls=%fused_computation.4 | loop fusion | flops 458752 | bytes 2752513 | tf_op jit(solution)/shard_map/jit(_where)/select_n | solution.py:51
  119.2 2.2 %collective-permute-start.13 = (bf16[128,3584]{1,0:T(8,128)(2,1)}, bf16[128,3584]{1,0:T(8,128)(2,1)}, u32[]{:S(2)}, u32[]{:S(2)}) collective-permute-start(bf16[128,3584]{1,0:T(8,128)(2,1)} %broadcast_select_fusion), channel_id=1, source_target_pairs={{0,2},{1,7},{2,4},{3,1},{4,6},{5,3},{6,0},{7,5},{8,10},{9,15},{10,... | collective-permute-start | bytes 2752520 | tf_op jit(solution)/shard_map/ppermute | solution.py:51
  121.7 2.4 %collective-permute-start.11 = (bf16[128,3584]{1,0:T(8,128)(2,1)S(1)}, bf16[128,3584]{1,0:T(8,128)(2,1)}, u32[]{:S(2)}, u32[]{:S(2)}) collective-permute-start(bf16[128,3584]{1,0:T(8,128)(2,1)S(1)} %collective-permute-done.9.refs_2_), channel_id=1, source_target_pairs={{0,1},{1,0},{2,3},{3,2},{4,5},{5,4},{6,7},{7,6},{8,9},{9,8},{10,11... | collective-permute-start | bytes 2752520 | tf_op jit(solution)/shard_map/ppermute | solution.py:56
  124.1 1.9 %collective-permute-start.12 = (bf16[128,3584]{1,0:T(8,128)(2,1)}, bf16[128,3584]{1,0:T(8,128)(2,1)}, u32[]{:S(2)}, u32[]{:S(2)}) collective-permute-start(bf16[128,3584]{1,0:T(8,128)(2,1)} %collective-permute-done.10.refs_3_), channel_id=1, source_target_pairs={{0,1},{1,0},{2,3},{3,2},{4,5},{5,4},{6,7},{7,6},{8,9},{9,8},{10,11... | collective-permute-start | bytes 2752520 | tf_op jit(solution)/shard_map/ppermute | solution.py:56
  126.1 0.1 broadcast_in_dim.70
  126.3 0.1 select_reduce_fusion
  126.4 0.6 broadcast_select_fusion.5
  127.0 3.4 %grads_first.1 = (f32[128,3584]{1,0:T(8,128)S(1)}, bf16[512,128]{1,0:T(8,128)(2,1)S(1)}) custom-call(s32[8]{0:T(128)S(1)} %stack.82.blocks_ref, bf16[128,3584]{1,0:T(8,128)(2,1)} %reshape.57.refs_0_, bf16[128,3584]{1,0:T(8,128)(2,1)} %collective-permute-done.8.refs_1_, bf16[128,3584]{1,0:T(8,128)(2,1)S(1)} %collective-permute-done.9.refs_2_, ...), custom_call_target="tpu_custom_call" | custom-call | flops 939524096 | bytes 9175040 | tf_op jit(solution)/shard_map/grads_first/pallas_call | solution.py:181
  130.4 3.6 %collective-permute-done.13.refs_2_ = bf16[128,3584]{1,0:T(8,128)(2,1)} collective-permute-done((bf16[128,3584]{1,0:T(8,128)(2,1)}, bf16[128,3584]{1,0:T(8,128)(2,1)}, u32[]{:S(2)}, u32[]{:S(2)}) %collective-permute-start.13) | collective-permute-done | bytes 917536 | tf_op jit(solution)/shard_map/ppermute | solution.py:51
  134.0 4.8 %collective-permute-start.14 = (bf16[128,3584]{1,0:T(8,128)(2,1)}, bf16[128,3584]{1,0:T(8,128)(2,1)S(1)}, u32[]{:S(2)}, u32[]{:S(2)}) collective-permute-start(bf16[128,3584]{1,0:T(8,128)(2,1)} %collective-permute-done.13.refs_2_), channel_id=1, source_target_pairs={{0,1},{1,0},{2,3},{3,2},{4,5},{5,4},{6,7},{7,6},{8,9},{9,8},{10,11... | collective-permute-start | bytes 2752520 | tf_op jit(solution)/shard_map/ppermute | solution.py:56
  138.8 2.3 %collective-permute-done.14.refs_3_ = bf16[128,3584]{1,0:T(8,128)(2,1)S(1)} collective-permute-done((bf16[128,3584]{1,0:T(8,128)(2,1)}, bf16[128,3584]{1,0:T(8,128)(2,1)S(1)}, u32[]{:S(2)}, u32[]{:S(2)}) %collective-permute-start.14) | collective-permute-done | bytes 917536 | tf_op jit(solution)/shard_map/ppermute | solution.py:56
  141.0 5.0 %grads_last.1 = (bf16[1024,128]{1,0:T(8,128)(2,1)}, bf16[128,3584]{1,0:T(8,128)(2,1)}, bf16[128,3584]{1,0:T(8,128)(2,1)}) custom-call(s32[8]{0:T(128)S(1)} %stack.82.blocks_ref, bf16[128,3584]{1,0:T(8,128)(2,1)} %collective-permute-done.11.refs_0_, bf16[128,3584]{1,0:T(8,128)(2,1)} %collective-permute-done.12.refs_1_, ...), custom_call_target="tpu_custom_call" | custom-call | flops 939524096 | bytes 9175040 | tf_op jit(solution)/shard_map/grads_last/pallas_call | solution.py:181
  (30 shorter events, 0.5 us)
Async XLA Ops:
  0.6 2.6 %copy-start = (bf16[128,3584]{1,0:T(8,128)(2,1)S(1)}, bf16[128,3584]{1,0:T(8,128)(2,1)}, u32[]{:S(2)}) copy-start(bf16[128,3584]{1,0:T(8,128)(2,1)} %param.6) | copy-start | bytes 2752516
  0.6 4.3 %copy-start.1 = (bf16[1,128,3584]{2,1,0:T(8,128)(2,1)S(1)}, bf16[1,128,3584]{2,1,0:T(8,128)(2,1)}, u32[]{:S(2)}) copy-start(bf16[1,128,3584]{2,1,0:T(8,128)(2,1)} %param.10) | copy-start | bytes 2752516
  3.2 27.7 %copy-start.3 = (bf16[1,1024,128]{2,1,0:T(8,128)(2,1)S(1)}, bf16[1,1024,128]{2,1,0:T(8,128)(2,1)}, u32[]{:S(2)}) copy-start(bf16[1,1024,128]{2,1,0:T(8,128)(2,1)} %param.9) | copy-start | bytes 786436
  4.9 26.2 %collective-permute-start = (bf16[128,3584]{1,0:T(8,128)(2,1)S(1)}, bf16[128,3584]{1,0:T(8,128)(2,1)S(1)}, u32[]{:S(2)}, u32[]{:S(2)}) collective-permute-start(bf16[128,3584]{1,0:T(8,128)(2,1)S(1)} %bitcast.35), channel_id=1, source_target_pairs={{0,2},{1,3},{2,4},{3,5},{4,6},{5,7},{6,0},{7,1},{8,10},{9,11},{10,... | collective-permute-start | bytes 2752520 | tf_op jit(solution)/shard_map/ppermute | solution.py:45
  8.9 22.3 %collective-permute-start.1 = (bf16[128,3584]{1,0:T(8,128)(2,1)S(1)}, bf16[128,3584]{1,0:T(8,128)(2,1)}, u32[]{:S(2)}, u32[]{:S(2)}) collective-permute-start(bf16[128,3584]{1,0:T(8,128)(2,1)S(1)} %bitcast.36), channel_id=1, source_target_pairs={{0,6},{1,7},{2,0},{3,1},{4,2},{5,3},{6,4},{7,5},{8,14},{9,15},{10,... | collective-permute-start | bytes 2752520 | tf_op jit(solution)/shard_map/ppermute | solution.py:45
  12.1 63.0 %all-to-all-start = ((bf16[64,2,3584]{2,1,0:T(2,128)(2,1)}), bf16[64,2,3584]{2,1,0:T(2,128)(2,1)}, u32[]{:S(2)}, u32[]{:S(2)}) async-start(bf16[64,2,3584]{2,1,0:T(2,128)(2,1)} %reshape.56), calls=%async_computation | async-start | bytes 1835008 | tf_op jit(solution)/shard_map/all_to_all | solution.py:207
  34.1 44.2 %collective-permute-start.2 = (bf16[384,3584]{1,0:T(8,128)(2,1)}, bf16[384,3584]{1,0:T(8,128)(2,1)}, u32[]{:S(2)}, u32[]{:S(2)}) collective-permute-start(bf16[384,3584]{1,0:T(8,128)(2,1)} %pad_maximum_fusion), channel_id=1, source_target_pairs={{0,1},{1,0},{2,3},{3,2},{4,5},{5,4},{6,7},{7,6},{8,9},{9,8},{10,11... | collective-permute-start | bytes 8257544 | tf_op jit(solution)/shard_map/ppermute | solution.py:56
  40.7 25.0 %collective-permute-start.3 = (bf16[128,3584]{1,0:T(8,128)(2,1)}, bf16[128,3584]{1,0:T(8,128)(2,1)}, u32[]{:S(2)}, u32[]{:S(2)}) collective-permute-start(bf16[128,3584]{1,0:T(8,128)(2,1)} %broadcast_select_fusion.1), channel_id=1, source_target_pairs={{0,2},{1,7},{2,4},{3,1},{4,6},{5,3},{6,0},{7,5},{8,10},{9,15},{10,... | collective-permute-start | bytes 2752520 | tf_op jit(solution)/shard_map/ppermute | solution.py:51
  47.6 3.2 %collective-permute-start.4 = (bf16[2,2,128,128]{3,2,1,0:T(8,128)(2,1)S(1)}, bf16[2,2,128,128]{3,2,1,0:T(8,128)(2,1)S(1)}, u32[]{:S(2)}, u32[]{:S(2)}) collective-permute-start(bf16[2,2,128,128]{3,2,1,0:T(8,128)(2,1)S(1)} %get-tuple-element.55), channel_id=1, source_target_pairs={{0,1},{1,0},{2,3},{3,2},{4,5},{5,4},{6,7},{7,6},{8,9},{9,8},{10,11... | collective-permute-start | bytes 393224 | tf_op jit(solution)/shard_map/ppermute | solution.py:109
  50.9 6.9 %collective-permute-start.5 = (bf16[2,2,128,128]{3,2,0,1:T(8,128)(2,1)S(1)}, bf16[2,2,128,128]{3,2,0,1:T(8,128)(2,1)S(1)}, u32[]{:S(2)}, u32[]{:S(2)}) collective-permute-start(bf16[2,2,128,128]{3,2,0,1:T(8,128)(2,1)S(1)} %get-tuple-element.53), channel_id=1, source_target_pairs={{0,2},{1,3},{2,0},{3,1},{4,6},{5,7},{6,4},{7,5},{8,10},{9,11},{10,... | collective-permute-start | bytes 393224 | tf_op jit(solution)/shard_map/ppermute | solution.py:109
  57.9 7.7 %collective-permute-start.6 = (bf16[2,2,128,128]{3,2,0,1:T(8,128)(2,1)S(1)}, bf16[2,2,128,128]{3,2,0,1:T(8,128)(2,1)S(1)}, u32[]{:S(2)}, u32[]{:S(2)}) collective-permute-start(bf16[2,2,128,128]{3,2,0,1:T(8,128)(2,1)S(1)} %get-tuple-element.51), channel_id=1, source_target_pairs={{0,4},{1,5},{2,6},{3,7},{4,0},{5,1},{6,2},{7,3},{8,12},{9,13},{10,... | collective-permute-start | bytes 393224 | tf_op jit(solution)/shard_map/ppermute | solution.py:109
  65.7 12.6 %collective-permute-start.7 = (bf16[128,3584]{1,0:T(8,128)(2,1)}, bf16[128,3584]{1,0:T(8,128)(2,1)}, u32[]{:S(2)}, u32[]{:S(2)}) collective-permute-start(bf16[128,3584]{1,0:T(8,128)(2,1)} %collective-permute-done.3.refs_4_), channel_id=1, source_target_pairs={{0,1},{1,0},{2,3},{3,2},{4,5},{5,4},{6,7},{7,6},{8,9},{9,8},{10,11... | collective-permute-start | bytes 2752520 | tf_op jit(solution)/shard_map/ppermute | solution.py:56
  82.1 34.9 %collective-permute-start.9 = (bf16[128,3584]{1,0:T(8,128)(2,1)}, bf16[128,3584]{1,0:T(8,128)(2,1)S(1)}, u32[]{:S(2)}, u32[]{:S(2)}) collective-permute-start(bf16[128,3584]{1,0:T(8,128)(2,1)} %reshape.57.refs_0_), channel_id=1, source_target_pairs={{0,2},{1,3},{2,4},{3,5},{4,6},{5,7},{6,0},{7,1},{8,10},{9,11},{10,... | collective-permute-start | bytes 2752520 | tf_op jit(solution)/shard_map/ppermute | solution.py:45
  84.0 33.0 %collective-permute-start.10 = (bf16[128,3584]{1,0:T(8,128)(2,1)}, bf16[128,3584]{1,0:T(8,128)(2,1)}, u32[]{:S(2)}, u32[]{:S(2)}) collective-permute-start(bf16[128,3584]{1,0:T(8,128)(2,1)} %reshape.57.refs_0_), channel_id=1, source_target_pairs={{0,6},{1,7},{2,0},{3,1},{4,2},{5,3},{6,4},{7,5},{8,14},{9,15},{10,... | collective-permute-start | bytes 2752520 | tf_op jit(solution)/shard_map/ppermute | solution.py:45
  90.9 26.1 %all-to-all-start.1 = ((f32[64,1,2]{2,1,0:T(1,128)}), f32[64,1,2]{2,1,0:T(1,128)S(1)}, u32[]{:S(2)}, u32[]{:S(2)}) async-start(f32[64,1,2]{2,1,0:T(1,128)} %bitcast.13), calls=%async_computation.1 | async-start | bytes 65536 | tf_op jit(solution)/shard_map/all_to_all | solution.py:222
  103.7 23.2 %collective-permute-start.8 = (bf16[128,3584]{1,0:T(8,128)(2,1)}, bf16[128,3584]{1,0:T(8,128)(2,1)}, u32[]{:S(2)}, u32[]{:S(2)}) collective-permute-start(bf16[128,3584]{1,0:T(8,128)(2,1)} %reshape.57.refs_0_), channel_id=1, source_target_pairs={{0,1},{1,0},{2,3},{3,2},{4,5},{5,4},{6,7},{7,6},{8,9},{9,8},{10,11... | collective-permute-start | bytes 2752520 | tf_op jit(solution)/shard_map/ppermute | solution.py:56
  119.2 14.7 %collective-permute-start.13 = (bf16[128,3584]{1,0:T(8,128)(2,1)}, bf16[128,3584]{1,0:T(8,128)(2,1)}, u32[]{:S(2)}, u32[]{:S(2)}) collective-permute-start(bf16[128,3584]{1,0:T(8,128)(2,1)} %broadcast_select_fusion), channel_id=1, source_target_pairs={{0,2},{1,7},{2,4},{3,1},{4,6},{5,3},{6,0},{7,5},{8,10},{9,15},{10,... | collective-permute-start | bytes 2752520 | tf_op jit(solution)/shard_map/ppermute | solution.py:51
  121.7 17.1 %collective-permute-start.11 = (bf16[128,3584]{1,0:T(8,128)(2,1)S(1)}, bf16[128,3584]{1,0:T(8,128)(2,1)}, u32[]{:S(2)}, u32[]{:S(2)}) collective-permute-start(bf16[128,3584]{1,0:T(8,128)(2,1)S(1)} %collective-permute-done.9.refs_2_), channel_id=1, source_target_pairs={{0,1},{1,0},{2,3},{3,2},{4,5},{5,4},{6,7},{7,6},{8,9},{9,8},{10,11... | collective-permute-start | bytes 2752520 | tf_op jit(solution)/shard_map/ppermute | solution.py:56
  124.1 14.7 %collective-permute-start.12 = (bf16[128,3584]{1,0:T(8,128)(2,1)}, bf16[128,3584]{1,0:T(8,128)(2,1)}, u32[]{:S(2)}, u32[]{:S(2)}) collective-permute-start(bf16[128,3584]{1,0:T(8,128)(2,1)} %collective-permute-done.10.refs_3_), channel_id=1, source_target_pairs={{0,1},{1,0},{2,3},{3,2},{4,5},{5,4},{6,7},{7,6},{8,9},{9,8},{10,11... | collective-permute-start | bytes 2752520 | tf_op jit(solution)/shard_map/ppermute | solution.py:56
  126.2 14.8 %copy-start.2 = (bf16[1,128,3584]{2,1,0:T(8,128)(2,1)S(1)}, bf16[1,128,3584]{2,1,0:T(8,128)(2,1)}, u32[]{:S(2)}) copy-start(bf16[1,128,3584]{2,1,0:T(8,128)(2,1)} %param.11) | copy-start | bytes 2752516
  134.0 7.1 %collective-permute-start.14 = (bf16[128,3584]{1,0:T(8,128)(2,1)}, bf16[128,3584]{1,0:T(8,128)(2,1)S(1)}, u32[]{:S(2)}, u32[]{:S(2)}) collective-permute-start(bf16[128,3584]{1,0:T(8,128)(2,1)} %collective-permute-done.13.refs_2_), channel_id=1, source_target_pairs={{0,1},{1,0},{2,3},{3,2},{4,5},{5,4},{6,7},{7,6},{8,9},{9,8},{10,11... | collective-permute-start | bytes 2752520 | tf_op jit(solution)/shard_map/ppermute | solution.py:56
